TPU v7x, 512 devices: a whole 4x8x8 slice. The times are simulated.
512 devices in a mesh: rows: 64 (over x, y, core), vec: 8 (over z).
Axes of the slice: x: 4, y: 8, z: 8, core: 2. Of those that a mesh axis runs over, the one named last changes fastest.
Arguments:
- vectors: float32 [64, 131072], P('vec', 'rows'), may hold values from -6 to 6
- damage: float32 [131072], P('rows')
- diag_blocks: bfloat16 [1024, 128, 128], P('rows')
- upper_blocks: bfloat16 [8192, 128, 128], P('rows'), may hold values from -0.5 to 0.5
- block_rows: int32 [8192], P('rows'), may hold values from 0 to 1023, as said below
- block_cols: int32 [8192], P('rows'), may hold values from 1 to 1023, as said below
- live_slots: int32 [64], P('rows'), may hold values from 64 to 128, as said below
Outputs:
- product: float32 [64, 131072], P('vec', 'rows')
- projected: float32 [64, 64], P('vec')
Inputs may be any that keep to these rules, and one draw needn't show every extreme that they name: `block_rows`: the slots of device d name block rows d * 16 to (d + 1) * 16 - 1; a slot whose column lies on another device names one of the last 6 of these. block_cols[s] is greater than block_rows[s], and block_cols[s] // 16 lies between d and d + 3 for a slot of device d; some slots reach d + 3. A column on device e other than d is one of the first 6 block rows of e. A pair may appear in several slots; their blocks add. `live_slots`: some device has all its slots stored.
All inputs are finite; a program needn't handle non-finite values.
Results may differ from a plain program's by a relative error of at most 0.0029.
Values may be sent and summed in bfloat16 or wider, within the bound.
No kernel may reach another device: no remote copies, remote signals or barrier semaphores. Data moves between devices by JAX's collectives and lax.ppermute only.
A program may use at most 64 MiB of HBM per device.

v0:
```python
import jax
import jax.numpy as jnp
from jax import lax
from jax.sharding import PartitionSpec as P

REACH = 4
RIM = 6


resid_eta = 0.001


def passed_along(array, axis, by):
    devices = lax.axis_size(axis)
    pairs = [(i, i + by) for i in range(devices) if 0 <= i + by < devices]
    return lax.ppermute(array, axis, pairs)


def on_device(vectors, damage, diag_blocks, upper_blocks, block_rows, block_cols, live_slots):
    vec_here, width = vectors.shape
    rb_here = diag_blocks.shape[0]
    block_size = diag_blocks.shape[1]
    slot_count = upper_blocks.shape[0]
    mine = lax.axis_index("rows")
    soft = jnp.sqrt((1.0 - damage) ** 2 + resid_eta)
    scaled = (vectors * soft[None, :]).astype(jnp.bfloat16).reshape(vec_here, rb_here, block_size)
    stored = (jnp.arange(slot_count) < live_slots[0]).astype(jnp.float32)
    local_rows = block_rows - mine * rb_here
    row_pick = (local_rows[:, None] == jnp.arange(rb_here)[None, :]).astype(jnp.float32) * stored[
        :, None
    ]
    own_rows = jnp.einsum(
        "vrb,sr->vsb", scaled, row_pick.astype(jnp.bfloat16), preferred_element_type=jnp.float32
    ).astype(jnp.bfloat16)
    accum = jnp.einsum("vrj,rij->vri", scaled, diag_blocks, preferred_element_type=jnp.float32)
    backward = jnp.einsum(
        "vsi,sij->vsj", own_rows, upper_blocks, preferred_element_type=jnp.float32
    )
    pieces = [scaled]
    for step in range(1, REACH):
        pieces.append(passed_along(scaled[:, :RIM], "rows", -step))
    window = jnp.concatenate(pieces, axis=1)
    relative = block_cols - mine * rb_here
    dev_step = relative // rb_here
    within = relative - dev_step * rb_here
    col_index = jnp.where(dev_step == 0, within, rb_here + (dev_step - 1) * RIM + within)
    span = window.shape[1]
    col_pick = (col_index[:, None] == jnp.arange(span)[None, :]).astype(jnp.float32) * stored[
        :, None
    ]
    far_cols = jnp.einsum(
        "vcb,sc->vsb", window, col_pick.astype(jnp.bfloat16), preferred_element_type=jnp.float32
    ).astype(jnp.bfloat16)
    forward = jnp.einsum("vsj,sij->vsi", far_cols, upper_blocks, preferred_element_type=jnp.float32)
    gathered = jnp.einsum("vsi,sr->vri", forward, row_pick, precision=lax.Precision.HIGHEST)
    spread = jnp.einsum("vsj,sc->vcj", backward, col_pick, precision=lax.Precision.HIGHEST)
    gathered, spread = (gathered, spread)
    accum = accum + gathered + spread[:, :rb_here]
    for step in range(1, REACH):
        low = rb_here + (step - 1) * RIM
        arrived = passed_along(spread[:, low : low + RIM], "rows", step)
        accum = accum.at[:, :RIM].add(arrived)
    product = soft[None, :] * accum.reshape(vec_here, width)
    partial_gram = jnp.dot(
        vectors,
        lax.all_gather(product.astype(jnp.bfloat16), "vec", axis=0, tiled=True)
        .astype(jnp.float32)
        .T,
        precision=lax.Precision.HIGHEST,
        preferred_element_type=jnp.float32,
    )
    total_dof = width * lax.axis_size("rows")
    projected = lax.psum(partial_gram, "rows") / total_dof
    return (product, projected)


def solution(mesh):
    return jax.shard_map(
        on_device,
        mesh=mesh,
        in_specs=(
            P("vec", "rows"),
            P("rows"),
            P("rows", None, None),
            P("rows", None, None),
            P("rows"),
            P("rows"),
            P("rows"),
        ),
        out_specs=(P("vec", "rows"), P("vec", None)),
        check_vma=False,
    )
```

profile of v0, /device:TPU:1, one launch (start us, length us, event | category | flops | bytes accessed | tf_op | source)
XLA Modules:
  0.0 186.2 jit_solution(1229719728883084545)
XLA Ops:
  0.6 0.0 copy-start
  0.6 0.8 add_sqrt_fusion
  1.4 0.9 fusion.16
  2.3 1.3 collective-permute-start.2
  3.6 1.3 collective-permute-start.1
  4.9 8.8 %collective-permute-start = (bf16[8,6,128]{2,0,1:T(8,128)(2,1)S(1)}, bf16[8,6,128]{2,0,1:T(8,128)(2,1)S(1)}, u32[]{:S(2)}, u32[]{:S(2)}) collective-permute-start(bf16[8,6,128]{2,0,1:T(8,128)(2,1)S(1)} %slice.91), channel_id=1, source_target_pairs={{8,0},{16,8},{24,16},{32,24},{40,32},{48,40},{56,48},{64,56},{72,6... | collective-permute-start | bytes 36872 | tf_op jit(solution)/shard_map/ppermute | solution.py:16
  14.3 0.0 copy-start.1
  14.3 0.8 broadcast_subtract_fusion
  15.2 0.8 compare_select_fusion
  16.0 0.3 fusion.17
  16.3 3.4 %fusion.12 = f32[128,8,128]{2,1,0:T(8,128)S(1)} fusion(bf16[128,128,128]{2,1,0:T(8,128)(2,1)} %param.16, bf16[128,8,128]{2,0,1:T(8,128)(2,1)S(1)} %fusion.17), kind=kOutput, calls=%fused_computation.15 | convolution fusion | flops 33554432 | bytes 4980736 | tf_op jit(solution)/shard_map/vsi,sij->vsj/dot_general | solution.py:36
  19.7 0.5 fusion.2
  20.1 0.0 copy-start.2
  20.2 6.0 %collective-permute-start.5 = (f32[8,6,128]{2,0,1:T(8,128)S(1)}, f32[8,6,128]{2,0,1:T(8,128)S(1)}, u32[]{:S(2)}, u32[]{:S(2)}) collective-permute-start(f32[8,6,128]{2,0,1:T(8,128)S(1)} %get-tuple-element.40), channel_id=1, source_target_pairs={{0,24},{8,32},{16,40},{24,48},{32,56},{40,64},{48,72},{56,80},{64,... | collective-permute-start | bytes 73736 | tf_op jit(solution)/shard_map/ppermute | solution.py:16
  26.2 3.4 %collective-permute-start.4 = (f32[8,6,128]{2,0,1:T(8,128)S(1)}, f32[8,6,128]{2,0,1:T(8,128)S(1)}, u32[]{:S(2)}, u32[]{:S(2)}) collective-permute-start(f32[8,6,128]{2,0,1:T(8,128)S(1)} %get-tuple-element.41), channel_id=1, source_target_pairs={{0,16},{8,24},{16,32},{24,40},{32,48},{40,56},{48,64},{56,72},{64,... | collective-permute-start | bytes 73736 | tf_op jit(solution)/shard_map/ppermute | solution.py:16
  29.5 0.0 collective-permute-done.2
  29.5 1.9 %collective-permute-start.3 = (f32[8,6,128]{2,0,1:T(8,128)S(1)}, f32[8,6,128]{2,0,1:T(8,128)S(1)}, u32[]{:S(2)}, u32[]{:S(2)}) collective-permute-start(f32[8,6,128]{2,0,1:T(8,128)S(1)} %get-tuple-element.42), channel_id=1, source_target_pairs={{0,8},{8,16},{16,24},{24,32},{32,40},{40,48},{48,56},{56,64},{64,7... | collective-permute-start | bytes 73736 | tf_op jit(solution)/shard_map/ppermute | solution.py:16
  31.5 0.0 collective-permute-done.1
  31.5 0.0 collective-permute-done
  31.5 0.3 fusion.14
  31.8 0.0 copy-done.1
  31.8 2.3 %fusion.9 = f32[128,8,128]{2,1,0:T(8,128)S(1)} fusion(bf16[128,128,128]{2,1,0:T(8,128)(2,1)S(1)} %copy-done.1, bf16[128,8,128]{2,0,1:T(8,128)(2,1)S(1)} %fusion.14), kind=kOutput, calls=%fused_computation.13 | convolution fusion | flops 33554432 | bytes 4980736 | tf_op jit(solution)/shard_map/vsj,sij->vsi/dot_general | solution.py:54
  34.0 0.4 fusion.4
  34.5 0.4 fusion.1
  34.9 0.0 collective-permute-done.3
  34.9 0.0 collective-permute-done.4
  34.9 0.0 collective-permute-done.5
  34.9 0.6 fusion.39
  35.6 20.4 %all_gather.3 = bf16[64,2048]{1,0:T(8,128)(2,1)S(1)} all-gather(bf16[8,2048]{1,0:T(8,128)(2,1)S(1)} %get-tuple-element.38), channel_id=1, replica_groups=mesh['rows'=64,'vec'=8] {'vec'}, dimensions={0}, use_global_device_ids=true | all-gather | bytes 294912 | tf_op jit(solution)/shard_map/all_gather | solution.py:66
  56.0 0.3 convolution_bitcast_fusion
  56.3 129.3 %psum.7 = f32[8,64]{1,0:T(8,128)S(1)} all-reduce(f32[8,64]{1,0:T(8,128)S(1)} %convolution_bitcast_fusion), channel_id=1, replica_groups=mesh['rows'=64,'vec'=8] {'rows'}, use_global_device_ids=true, to_apply=%region_0.1 | all-reduce | flops 512 | bytes 4096 | tf_op jit(solution)/shard_map/psum | solution.py:73
  185.6 0.6 broadcast_multiply_fusion
  (11 shorter events, 0.1 us)
Async XLA Ops:
  0.6 33.8 %copy-start = (bf16[16,128,128]{2,1,0:T(8,128)(2,1)S(1)}, bf16[16,128,128]{2,1,0:T(8,128)(2,1)}, u32[]{:S(2)}) copy-start(bf16[16,128,128]{2,1,0:T(8,128)(2,1)} %param.15) | copy-start | bytes 1572868
  2.3 27.2 %collective-permute-start.2 = (bf16[8,6,128]{2,0,1:T(8,128)(2,1)S(1)}, bf16[8,6,128]{2,0,1:T(8,128)(2,1)S(1)}, u32[]{:S(2)}, u32[]{:S(2)}) collective-permute-start(bf16[8,6,128]{2,0,1:T(8,128)(2,1)S(1)} %slice.91), channel_id=1, source_target_pairs={{24,0},{32,8},{40,16},{48,24},{56,32},{64,40},{72,48},{80,56},{88,... | collective-permute-start | bytes 36872 | tf_op jit(solution)/shard_map/ppermute | solution.py:16
  3.6 27.9 %collective-permute-start.1 = (bf16[8,6,128]{2,0,1:T(8,128)(2,1)S(1)}, bf16[8,6,128]{2,0,1:T(8,128)(2,1)S(1)}, u32[]{:S(2)}, u32[]{:S(2)}) collective-permute-start(bf16[8,6,128]{2,0,1:T(8,128)(2,1)S(1)} %slice.91), channel_id=1, source_target_pairs={{16,0},{24,8},{32,16},{40,24},{48,32},{56,40},{64,48},{72,56},{80,... | collective-permute-start | bytes 36872 | tf_op jit(solution)/shard_map/ppermute | solution.py:16
  4.9 26.6 %collective-permute-start = (bf16[8,6,128]{2,0,1:T(8,128)(2,1)S(1)}, bf16[8,6,128]{2,0,1:T(8,128)(2,1)S(1)}, u32[]{:S(2)}, u32[]{:S(2)}) collective-permute-start(bf16[8,6,128]{2,0,1:T(8,128)(2,1)S(1)} %slice.91), channel_id=1, source_target_pairs={{8,0},{16,8},{24,16},{32,24},{40,32},{48,40},{56,48},{64,56},{72,6... | collective-permute-start | bytes 36872 | tf_op jit(solution)/shard_map/ppermute | solution.py:16
  14.3 17.4 %copy-start.1 = (bf16[128,128,128]{2,1,0:T(8,128)(2,1)S(1)}, bf16[128,128,128]{2,1,0:T(8,128)(2,1)}, u32[]{:S(2)}) copy-start(bf16[128,128,128]{2,1,0:T(8,128)(2,1)} %param.16) | copy-start | bytes 12582916
  20.1 35.9 %copy-start.2 = (f32[8,2048]{1,0:T(8,128)S(1)}, f32[8,2048]{1,0:T(8,128)}, u32[]{:S(2)}) copy-start(f32[8,2048]{1,0:T(8,128)} %param.13) | copy-start | bytes 196612
  20.2 14.7 %collective-permute-start.5 = (f32[8,6,128]{2,0,1:T(8,128)S(1)}, f32[8,6,128]{2,0,1:T(8,128)S(1)}, u32[]{:S(2)}, u32[]{:S(2)}) collective-permute-start(f32[8,6,128]{2,0,1:T(8,128)S(1)} %get-tuple-element.40), channel_id=1, source_target_pairs={{0,24},{8,32},{16,40},{24,48},{32,56},{40,64},{48,72},{56,80},{64,... | collective-permute-start | bytes 73736 | tf_op jit(solution)/shard_map/ppermute | solution.py:16
  26.2 8.7 %collective-permute-start.4 = (f32[8,6,128]{2,0,1:T(8,128)S(1)}, f32[8,6,128]{2,0,1:T(8,128)S(1)}, u32[]{:S(2)}, u32[]{:S(2)}) collective-permute-start(f32[8,6,128]{2,0,1:T(8,128)S(1)} %get-tuple-element.41), channel_id=1, source_target_pairs={{0,16},{8,24},{16,32},{24,40},{32,48},{40,56},{48,64},{56,72},{64,... | collective-permute-start | bytes 73736 | tf_op jit(solution)/shard_map/ppermute | solution.py:16
  29.5 5.3 %collective-permute-start.3 = (f32[8,6,128]{2,0,1:T(8,128)S(1)}, f32[8,6,128]{2,0,1:T(8,128)S(1)}, u32[]{:S(2)}, u32[]{:S(2)}) collective-permute-start(f32[8,6,128]{2,0,1:T(8,128)S(1)} %get-tuple-element.42), channel_id=1, source_target_pairs={{0,8},{8,16},{16,24},{24,32},{32,40},{40,48},{48,56},{56,64},{64,7... | collective-permute-start | bytes 73736 | tf_op jit(solution)/shard_map/ppermute | solution.py:16
where the time goes:
time: 187 us; the launch traced here: 186 us
  blocking collectives  150 us (80%)
  starting transfers between devices  22.6 us (12%)
  matrix products  7.72 us (4%)
  other arithmetic  4.55 us (2%)
    psum x1, blocking collectives, on_device(): projected = lax.psum(partial_gram, 'rows') / total_dof  129 us
    ppermute x6, starting transfers between devices, passed_along(): return lax.ppermute(array, axis, pairs)  22.6 us
    all_gather x1, blocking collectives, on_device(): lax.all_gather(product.astype(jnp.bfloat16), 'vec', axis=0, tiled=True)  20.4 us
  transfers between devices with their start and end apart: 6, of which 0 were waited for; matrix products, arithmetic and copies ran while one was open for 5% of the time, Pallas kernels for 0%

commit v1 on v0

--- a/solution.py
+++ b/solution.py
@@ -16,6 +16,11 @@
     return lax.ppermute(array, axis, pairs)
 
 
+def everyones(array, axis):
+    copies = jnp.broadcast_to(array[None], (lax.axis_size(axis),) + array.shape)
+    return lax.all_to_all(copies, axis, 0, 0)
+
+
 def on_device(vectors, damage, diag_blocks, upper_blocks, block_rows, block_cols, live_slots):
     vec_here, width = vectors.shape
     rb_here = diag_blocks.shape[0]
@@ -23,7 +28,8 @@
     slot_count = upper_blocks.shape[0]
     mine = lax.axis_index("rows")
     soft = jnp.sqrt((1.0 - damage) ** 2 + resid_eta)
-    scaled = (vectors * soft[None, :]).astype(jnp.bfloat16).reshape(vec_here, rb_here, block_size)
+    flat = (vectors * soft[None, :]).astype(jnp.bfloat16)
+    scaled = flat.reshape(vec_here, rb_here, block_size)
     stored = (jnp.arange(slot_count) < live_slots[0]).astype(jnp.float32)
     local_rows = block_rows - mine * rb_here
     row_pick = (local_rows[:, None] == jnp.arange(rb_here)[None, :]).astype(jnp.float32) * stored[
@@ -54,23 +60,26 @@
     forward = jnp.einsum("vsj,sij->vsi", far_cols, upper_blocks, preferred_element_type=jnp.float32)
     gathered = jnp.einsum("vsi,sr->vri", forward, row_pick, precision=lax.Precision.HIGHEST)
     spread = jnp.einsum("vsj,sc->vcj", backward, col_pick, precision=lax.Precision.HIGHEST)
-    gathered, spread = (gathered, spread)
     accum = accum + gathered + spread[:, :rb_here]
     for step in range(1, REACH):
         low = rb_here + (step - 1) * RIM
         arrived = passed_along(spread[:, low : low + RIM], "rows", step)
         accum = accum.at[:, :RIM].add(arrived)
-    product = soft[None, :] * accum.reshape(vec_here, width)
+    raw = accum.reshape(vec_here, width)
+    product = soft[None, :] * raw
+    every = everyones(flat, "vec").reshape(-1, width)
     partial_gram = jnp.dot(
-        vectors,
-        lax.all_gather(product.astype(jnp.bfloat16), "vec", axis=0, tiled=True)
-        .astype(jnp.float32)
-        .T,
+        raw,
+        every.astype(jnp.float32).T,
         precision=lax.Precision.HIGHEST,
         preferred_element_type=jnp.float32,
     )
+    half = vec_here // 2
+    packed = jnp.concatenate([partial_gram[:half], partial_gram[half:]], axis=1)
     total_dof = width * lax.axis_size("rows")
-    projected = lax.psum(partial_gram, "rows") / total_dof
+    packed = jnp.sum(everyones(packed, "rows"), axis=0) / total_dof
+    columns = partial_gram.shape[1]
+    projected = jnp.concatenate([packed[:, :columns], packed[:, columns:]], axis=0)
     return (product, projected)
 
 

time: 187 us -> 69.2 us (0.37)
  blocking collectives: 150 us -> 0 us
  starting transfers between devices: 22.6 us -> 39.4 us
  waiting for transfers between devices: 0.02 us -> 12.5 us
  matrix products: 7.72 us -> 9.92 us
    psum x1 -> x0, blocking collectives: 129 us -> none  [on_device(): projected = lax.psum(partial_gram, 'rows') / total_dof]
    all_gather x1 -> x0, blocking collectives: 20.4 us -> none  [on_device(): lax.all_gather(product.astype(jnp.bfloat16), 'vec', axis=0, tiled=True)]
    all_to_all x0 -> x2, starting transfers between devices: none -> 16.6 us  [everyones(): return lax.all_to_all(copies, axis, 0, 0)]
    all_to_all x0 -> x2, waiting for transfers between devices: none -> 12.5 us  [everyones(): return lax.all_to_all(copies, axis, 0, 0)]
    dot_general x1, matrix products: 2.25 us -> 4.43 us  [on_device(): jnp.einsum('vsj,sij->vsi', far_cols, upper_blocks, preferred_element_type...]
  transfers between devices with their start and end apart: 6 -> 8, of which waited for: 0 -> 2; matrix products, arithmetic and copies ran while one was open for 5% -> 17% of each run, Pallas kernels for 0% -> 0%
where the time goes in v1:
time: 69.2 us; the launch traced here: 68.6 us
  starting transfers between devices  39.4 us (57%)
  waiting for transfers between devices  12.5 us (18%)
  matrix products  9.92 us (14%)
  other arithmetic  3.77 us (5%)
  local copies, waits for them, and re-layouts  1.55 us (2%)
  between operations  1.53 us (2%)
    ppermute x6, starting transfers between devices, passed_along(): return lax.ppermute(array, axis, pairs)  22.8 us
    all_to_all x2, starting transfers between devices, everyones(): return lax.all_to_all(copies, axis, 0, 0)  16.6 us
    all_to_all x2, waiting for transfers between devices, everyones(): return lax.all_to_all(copies, axis, 0, 0)  12.5 us
    dot_general x1, matrix products, on_device(): jnp.einsum('vsj,sij->vsi', far_cols, upper_blocks, preferred_element_type...  4.43 us
    dot_general x1, matrix products, on_device(): jnp.einsum('vsi,sij->vsj', own_rows, upper_blocks, preferred_element_type...  3.38 us
    broadcast_in_dim x2, local copies, waits for them, and re-layouts, everyones(): copies = jnp.broadcast_to(array[None], (lax.axis_size(axis),) + array.shape)  1.4 us
  transfers between devices with their start and end apart: 8, of which 2 were waited for; matrix products, arithmetic and copies ran while one was open for 17% of the time, Pallas kernels for 0%

profile of v1, /device:TPU:1, one launch (start us, length us, event | category | flops | bytes accessed | tf_op | source)
XLA Modules:
  0.0 68.6 jit_solution(9560042727449284684)
XLA Ops:
  0.6 0.0 copy-start
  0.6 0.0 copy-start.1
  0.7 0.8 %add_sqrt_fusion = f32[2048]{0:T(1024)S(1)} fusion(f32[2048]{0:T(1024)} %param.14), kind=kLoop, calls=%fused_computation.46 | loop fusion | flops 6144 | bytes 16384 | tf_op jit(solution)/shard_map/sqrt | solution.py:30
  1.4 0.9 %fusion.48 = bf16[1,8,16,128]{3,1,2,0:T(8,128)(2,1)S(1)} fusion(f32[8,2048]{1,0:T(8,128)} %param.13, f32[2048]{0:T(1024)S(1)} %add_sqrt_fusion), kind=kLoop, calls=%fused_computation.73 | loop fusion | flops 32768 | bytes 106496
  2.3 8.8 %collective-permute-start = (bf16[8,6,128]{2,1,0:T(8,128)(2,1)S(1)}, bf16[8,6,128]{2,1,0:T(8,128)(2,1)S(1)}, u32[]{:S(2)}, u32[]{:S(2)}) collective-permute-start(bf16[8,6,128]{2,1,0:T(8,128)(2,1)S(1)} %slice.107), channel_id=1, source_target_pairs={{8,0},{16,8},{24,16},{32,24},{40,32},{48,40},{56,48},{64,56},{72,6... | collective-permute-start | bytes 36872 | tf_op jit(solution)/shard_map/ppermute | solution.py:16
  11.1 1.3 %collective-permute-start.1 = (bf16[8,6,128]{2,1,0:T(8,128)(2,1)S(1)}, bf16[8,6,128]{2,1,0:T(8,128)(2,1)S(1)}, u32[]{:S(2)}, u32[]{:S(2)}) collective-permute-start(bf16[8,6,128]{2,1,0:T(8,128)(2,1)S(1)} %slice.107), channel_id=1, source_target_pairs={{16,0},{24,8},{32,16},{40,24},{48,32},{56,40},{64,48},{72,56},{80,... | collective-permute-start | bytes 36872 | tf_op jit(solution)/shard_map/ppermute | solution.py:16
  12.4 1.3 %collective-permute-start.2 = (bf16[8,6,128]{2,1,0:T(8,128)(2,1)S(1)}, bf16[8,6,128]{2,1,0:T(8,128)(2,1)S(1)}, u32[]{:S(2)}, u32[]{:S(2)}) collective-permute-start(bf16[8,6,128]{2,1,0:T(8,128)(2,1)S(1)} %slice.107), channel_id=1, source_target_pairs={{24,0},{32,8},{40,16},{48,24},{56,32},{64,40},{72,48},{80,56},{88,... | collective-permute-start | bytes 36872 | tf_op jit(solution)/shard_map/ppermute | solution.py:16
  14.4 0.7 %compare_select_fusion = (s32[128]{0:T(128)S(1)}, s32[128]{0:T(128)S(1)}) fusion(s32[128]{0:T(128)} %param.18, s32[]{:T(128)S(6)} %mul.45, s32[128]{0:T(128)} %param.17), kind=kLoop, calls=%fused_computation.56 | loop fusion | flops 3200 | bytes 2052 | tf_op jit(solution)/shard_map/jit(_where)/select_n | solution.py:52
  15.1 0.3 fusion.1
  15.3 3.4 %convolution_bitcast_fusion = f32[8,128,128]{2,0,1:T(8,128)S(1)} fusion(bf16[128,128,128]{2,1,0:T(8,128)(2,1)} %param.16, bf16[8,128,128]{2,1,0:T(8,128)(2,1)S(1)} %fusion.1), kind=kOutput, calls=%fused_computation | convolution fusion | flops 33554432 | bytes 4980736 | tf_op jit(solution)/shard_map/vsi,sij->vsj/dot_general | solution.py:42
  18.7 0.5 fusion.4
  19.2 3.5 %collective-permute-start.3 = (f32[8,6,128]{2,0,1:T(8,128)S(1)}, f32[8,6,128]{2,0,1:T(8,128)S(1)}, u32[]{:S(2)}, u32[]{:S(2)}) collective-permute-start(f32[8,6,128]{2,0,1:T(8,128)S(1)} %get-tuple-element.40), channel_id=1, source_target_pairs={{0,8},{8,16},{16,24},{24,32},{32,40},{40,48},{48,56},{56,64},{64,7... | collective-permute-start | bytes 73736 | tf_op jit(solution)/shard_map/ppermute | solution.py:16
  22.8 3.8 %collective-permute-start.4 = (f32[8,6,128]{2,0,1:T(8,128)S(1)}, f32[8,6,128]{2,0,1:T(8,128)S(1)}, u32[]{:S(2)}, u32[]{:S(2)}) collective-permute-start(f32[8,6,128]{2,0,1:T(8,128)S(1)} %get-tuple-element.39), channel_id=1, source_target_pairs={{0,16},{8,24},{16,32},{24,40},{32,48},{40,56},{48,64},{56,72},{64,... | collective-permute-start | bytes 73736 | tf_op jit(solution)/shard_map/ppermute | solution.py:16
  26.6 0.7 %broadcast_in_dim.4 = bf16[8,8,2048]{2,1,0:T(8,128)(2,1)} broadcast(bf16[8,2048]{1,0:T(8,128)(2,1)S(1)} %multiply_convert_fusion), dimensions={1,2} | broadcast | bytes 294912 | tf_op jit(solution)/shard_map/broadcast_in_dim | solution.py:20
  27.4 5.3 %all-to-all-start = ((bf16[8,8,2048]{2,1,0:T(8,128)(2,1)}), bf16[8,8,2048]{2,1,0:T(8,128)(2,1)S(1)}, u32[]{:S(2)}, u32[]{:S(2)}) async-start(bf16[8,8,2048]{2,1,0:T(8,128)(2,1)} %broadcast_in_dim.4), calls=%async_computation | async-start | bytes 524288 | tf_op jit(solution)/shard_map/all_to_all | solution.py:21
  32.7 0.0 collective-permute-done
  32.7 4.0 %collective-permute-start.5 = (f32[8,6,128]{2,0,1:T(8,128)S(1)}, f32[8,6,128]{2,0,1:T(8,128)S(1)}, u32[]{:S(2)}, u32[]{:S(2)}) collective-permute-start(f32[8,6,128]{2,0,1:T(8,128)S(1)} %get-tuple-element.38), channel_id=1, source_target_pairs={{0,24},{8,32},{16,40},{24,48},{32,56},{40,64},{48,72},{56,80},{64,... | collective-permute-start | bytes 73736 | tf_op jit(solution)/shard_map/ppermute | solution.py:16
  36.7 0.3 fusion
  37.0 4.4 %convolution_bitcast_fusion.1 = f32[8,128,128]{2,0,1:T(8,128)S(1)} fusion(bf16[128,128,128]{2,1,0:T(8,128)(2,1)} %param.16, bf16[8,128,128]{2,1,0:T(8,128)(2,1)S(1)} %fusion), kind=kOutput, calls=%fused_computation.1 | convolution fusion | flops 33554432 | bytes 4980736 | tf_op jit(solution)/shard_map/vsj,sij->vsi/dot_general | solution.py:60
  41.4 0.4 fusion.6
  41.9 0.4 fusion.3
  42.3 0.0 collective-permute-done.3
  42.3 2.7 %all-to-all-done = bf16[8,8,2048]{2,1,0:T(8,128)(2,1)S(1)} async-done(((bf16[8,8,2048]{2,1,0:T(8,128)(2,1)}), bf16[8,8,2048]{2,1,0:T(8,128)(2,1)S(1)}, u32[]{:S(2)}, u32[]{:S(2)}) %all-to-all-start) | async-done | bytes 262176 | tf_op jit(solution)/shard_map/all_to_all | solution.py:21
  45.1 0.3 fusion.8
  45.4 0.1 pad_maximum_fusion.1
  45.5 0.7 broadcast_in_dim.5
  46.2 11.3 %all-to-all-start.1 = ((f32[64,4,128]{2,1,0:T(4,128)}), f32[64,4,128]{2,1,0:T(4,128)S(1)}, u32[]{:S(2)}, u32[]{:S(2)}) async-start(f32[64,4,128]{2,1,0:T(4,128)} %broadcast_in_dim.5), calls=%async_computation.1 | async-start | bytes 262144 | tf_op jit(solution)/shard_map/all_to_all | solution.py:21
  57.5 0.6 bitcast_multiply_fusion
  58.1 9.7 %all-to-all-done.1 = f32[64,4,128]{2,1,0:T(4,128)S(1)} async-done(((f32[64,4,128]{2,1,0:T(4,128)}), f32[64,4,128]{2,1,0:T(4,128)S(1)}, u32[]{:S(2)}, u32[]{:S(2)}) %all-to-all-start.1) | async-done | bytes 131104 | tf_op jit(solution)/shard_map/all_to_all | solution.py:21
  67.9 0.1 reduce_sum.9
  67.9 0.1 fusion.44
  68.0 0.6 pad_maximum_fusion
  (18 shorter events, 0.1 us)
Async XLA Ops:
  0.6 41.2 %copy-start = (bf16[16,128,128]{2,1,0:T(8,128)(2,1)S(1)}, bf16[16,128,128]{2,1,0:T(8,128)(2,1)}, u32[]{:S(2)}) copy-start(bf16[16,128,128]{2,1,0:T(8,128)(2,1)} %param.15) | copy-start | bytes 1572868
  0.6 26.0 %copy-start.1 = (f32[8,2048]{1,0:T(8,128)S(1)}, f32[8,2048]{1,0:T(8,128)}, u32[]{:S(2)}) copy-start(f32[8,2048]{1,0:T(8,128)} %param.13) | copy-start | bytes 196612
  2.3 30.3 %collective-permute-start = (bf16[8,6,128]{2,1,0:T(8,128)(2,1)S(1)}, bf16[8,6,128]{2,1,0:T(8,128)(2,1)S(1)}, u32[]{:S(2)}, u32[]{:S(2)}) collective-permute-start(bf16[8,6,128]{2,1,0:T(8,128)(2,1)S(1)} %slice.107), channel_id=1, source_target_pairs={{8,0},{16,8},{24,16},{32,24},{40,32},{48,40},{56,48},{64,56},{72,6... | collective-permute-start | bytes 36872 | tf_op jit(solution)/shard_map/ppermute | solution.py:16
  11.1 25.6 %collective-permute-start.1 = (bf16[8,6,128]{2,1,0:T(8,128)(2,1)S(1)}, bf16[8,6,128]{2,1,0:T(8,128)(2,1)S(1)}, u32[]{:S(2)}, u32[]{:S(2)}) collective-permute-start(bf16[8,6,128]{2,1,0:T(8,128)(2,1)S(1)} %slice.107), channel_id=1, source_target_pairs={{16,0},{24,8},{32,16},{40,24},{48,32},{56,40},{64,48},{72,56},{80,... | collective-permute-start | bytes 36872 | tf_op jit(solution)/shard_map/ppermute | solution.py:16
  12.4 24.3 %collective-permute-start.2 = (bf16[8,6,128]{2,1,0:T(8,128)(2,1)S(1)}, bf16[8,6,128]{2,1,0:T(8,128)(2,1)S(1)}, u32[]{:S(2)}, u32[]{:S(2)}) collective-permute-start(bf16[8,6,128]{2,1,0:T(8,128)(2,1)S(1)} %slice.107), channel_id=1, source_target_pairs={{24,0},{32,8},{40,16},{48,24},{56,32},{64,40},{72,48},{80,56},{88,... | collective-permute-start | bytes 36872 | tf_op jit(solution)/shard_map/ppermute | solution.py:16
  19.2 23.0 %collective-permute-start.3 = (f32[8,6,128]{2,0,1:T(8,128)S(1)}, f32[8,6,128]{2,0,1:T(8,128)S(1)}, u32[]{:S(2)}, u32[]{:S(2)}) collective-permute-start(f32[8,6,128]{2,0,1:T(8,128)S(1)} %get-tuple-element.40), channel_id=1, source_target_pairs={{0,8},{8,16},{16,24},{24,32},{32,40},{40,48},{48,56},{56,64},{64,7... | collective-permute-start | bytes 73736 | tf_op jit(solution)/shard_map/ppermute | solution.py:16
  22.8 19.5 %collective-permute-start.4 = (f32[8,6,128]{2,0,1:T(8,128)S(1)}, f32[8,6,128]{2,0,1:T(8,128)S(1)}, u32[]{:S(2)}, u32[]{:S(2)}) collective-permute-start(f32[8,6,128]{2,0,1:T(8,128)S(1)} %get-tuple-element.39), channel_id=1, source_target_pairs={{0,16},{8,24},{16,32},{24,40},{32,48},{40,56},{48,64},{56,72},{64,... | collective-permute-start | bytes 73736 | tf_op jit(solution)/shard_map/ppermute | solution.py:16
  27.4 17.7 %all-to-all-start = ((bf16[8,8,2048]{2,1,0:T(8,128)(2,1)}), bf16[8,8,2048]{2,1,0:T(8,128)(2,1)S(1)}, u32[]{:S(2)}, u32[]{:S(2)}) async-start(bf16[8,8,2048]{2,1,0:T(8,128)(2,1)} %broadcast_in_dim.4), calls=%async_computation | async-start | bytes 524288 | tf_op jit(solution)/shard_map/all_to_all | solution.py:21
  32.7 9.7 %collective-permute-start.5 = (f32[8,6,128]{2,0,1:T(8,128)S(1)}, f32[8,6,128]{2,0,1:T(8,128)S(1)}, u32[]{:S(2)}, u32[]{:S(2)}) collective-permute-start(f32[8,6,128]{2,0,1:T(8,128)S(1)} %get-tuple-element.38), channel_id=1, source_target_pairs={{0,24},{8,32},{16,40},{24,48},{32,56},{40,64},{48,72},{56,80},{64,... | collective-permute-start | bytes 73736 | tf_op jit(solution)/shard_map/ppermute | solution.py:16
  46.2 21.7 %all-to-all-start.1 = ((f32[64,4,128]{2,1,0:T(4,128)}), f32[64,4,128]{2,1,0:T(4,128)S(1)}, u32[]{:S(2)}, u32[]{:S(2)}) async-start(f32[64,4,128]{2,1,0:T(4,128)} %broadcast_in_dim.5), calls=%async_computation.1 | async-start | bytes 262144 | tf_op jit(solution)/shard_map/all_to_all | solution.py:21

commit v2 on v0

v2 whole, which is shorter than its diff:
```python
import functools

import jax
import jax.numpy as jnp
from jax import lax
from jax.experimental import pallas as pl
from jax.experimental.pallas import tpu as pltpu
from jax.sharding import PartitionSpec as P

REACH = 4
RIM = 6
UNROLL = 64
VMEM_BYTES = 8 << 20
WIDE_VMEM_BYTES = 46 << 20
CHUNKS = 8


resid_eta = 0.001

VM = pl.BlockSpec(memory_space=pltpu.VMEM)
FAR = pl.BlockSpec(memory_space=pl.ANY)
SM = pl.BlockSpec(memory_space=pltpu.SMEM)
TRANSPOSED = (((1,), (1,)), ((), ()))


def passed_along(array, axis, by):
    devices = lax.axis_size(axis)
    pairs = [(i, i + by) for i in range(devices) if 0 <= i + by < devices]
    return lax.ppermute(array, axis, pairs)


def call(kernel, name, in_specs, outs, scratch, flops, moved, vmem=VMEM_BYTES):
    return pl.pallas_call(
        kernel,
        name=name,
        in_specs=in_specs,
        out_specs=[VM] * len(outs),
        out_shape=[jax.ShapeDtypeStruct(shape, dtype) for shape, dtype in outs],
        scratch_shapes=scratch,
        compiler_params=pltpu.CompilerParams(vmem_limit_bytes=vmem),
        cost_estimate=pl.CostEstimate(flops=flops, bytes_accessed=moved, transcendentals=0),
    )


def softness(damage):
    return jnp.sqrt((1.0 - damage) ** 2 + resid_eta)


def scale_kernel(vectors, damage, copies, blocks, rim):
    soft = softness(damage[...])
    size = blocks.shape[2]
    for b in range(blocks.shape[0]):
        cut = slice(b * size, (b + 1) * size)
        scaled = (vectors[:, cut] * soft[b : b + 1, :]).astype(jnp.bfloat16)
        blocks[b] = scaled
        if b < RIM:
            rim[b] = scaled
        for i in range(copies.shape[0]):
            copies[i, :, cut] = scaled


def spread_halves(upper_half, lower_half, parts, last):
    for at, ref in parts:
        for i in range(ref.shape[0]):
            x = ref[i].astype(jnp.float32)
            z = jnp.zeros_like(x)
            upper_half[at + i] = jnp.concatenate([x, z], 0).astype(jnp.bfloat16)
            lower_half[at + i] = jnp.concatenate([z, x], 0).astype(jnp.bfloat16)
    upper_half[last] = jnp.zeros(upper_half.shape[1:], jnp.bfloat16)
    lower_half[last] = jnp.zeros(lower_half.shape[1:], jnp.bfloat16)


def each_pair(start, slots, take, give, top, bottom, total, product, none_from, none_to, base, live):
    vecs = total.shape[1]

    unroll = min(slots, UNROLL)

    @pl.loop(0, slots // unroll)
    def _(group):
        first = start + group * unroll
        results = []
        for k in range(0, unroll, 2):
            s = first + k
            a = jnp.where(s < live, take[s] - base, none_from)
            b = jnp.where(s + 1 < live, take[s + 1] - base, none_from)
            x = jnp.concatenate([top[a], bottom[b]], axis=1)
            y = product(x, s)
            results += [y[:vecs], y[vecs:]]
        for k in range(unroll):
            s = first + k
            to = jnp.where(s < live, give[s] - base, none_to)
            total[to] += results[k]


def backward_kernel(
    rows, cols, place, blocks, upper_far, own, one, two, three, upper, total, top, bottom, sems
):
    here = own.shape[0]
    per = upper.shape[0] // CHUNKS

    def chunk(c):
        cut = pl.ds(c * per, per)
        return pltpu.make_async_copy(upper_far.at[cut], upper.at[cut], sems.at[c])

    for c in range(CHUNKS):
        chunk(c).start()
    total[...] = jnp.zeros_like(total)
    spread_halves(top, bottom, [(0, blocks)], here)

    def product(x, s):
        size = upper.shape[1]
        pair = upper[pl.ds(s, 2)].reshape(2 * size, size)
        return jnp.dot(x, pair, preferred_element_type=jnp.float32)

    for c in range(CHUNKS):
        chunk(c).wait()
        each_pair(
            c * per, per, rows, cols, top, bottom, total, product, here, REACH * here, place[0],
            place[1],
        )
    own[...] = total[:here]
    for step, out in ((1, one), (2, two), (3, three)):
        out[...] = total[step * here : step * here + RIM]


def forward_kernel(
    rows, cols, place, blocks, far1, far2, far3, own, back1, back2, back3, diag, every, damage,
    upper, product_out, copies, total, top, bottom
):
    here = own.shape[0]
    size = diag.shape[1]
    vecs = blocks.shape[1]
    parts = [(0, blocks), (here, far1), (2 * here, far2), (3 * here, far3)]
    spread_halves(top, bottom, parts, REACH * here)
    total[:here] = own[...]
    total[:RIM] += back1[...] + back2[...] + back3[...]

    def product(x, s):
        pair = jnp.concatenate([upper[s], upper[s + 1]], axis=1)
        return lax.dot_general(x, pair, TRANSPOSED, preferred_element_type=jnp.float32)

    each_pair(
        0, upper.shape[0], cols, rows, top, bottom, total, product, REACH * here, here, place[0],
        place[1],
    )
    soft = softness(damage[...])
    gram = jnp.zeros((2 * vecs, every.shape[0]), jnp.float32)
    for b in range(here):
        raw = total[b] + lax.dot_general(
            blocks[b], diag[b], TRANSPOSED, preferred_element_type=jnp.float32
        )
        cut = slice(b * size, (b + 1) * size)
        product_out[:, cut] = raw * soft[b : b + 1, :]
        high = raw.astype(jnp.bfloat16)
        low = (raw - high.astype(jnp.float32)).astype(jnp.bfloat16)
        gram += lax.dot_general(
            jnp.concatenate([high, low], 0), every[:, cut], TRANSPOSED,
            preferred_element_type=jnp.float32,
        )
    gram = gram[:vecs] + gram[vecs:]
    half = vecs // 2
    packed = jnp.concatenate([gram[:half], gram[half:]], axis=1)
    copies[...] = jnp.broadcast_to(packed[None], copies.shape)


def sum_kernel(scale, parts, out):
    packed = jnp.sum(parts[...], axis=0) * scale
    columns = out.shape[1]
    half = packed.shape[0]
    out[:half] = packed[:, :columns]
    out[half:] = packed[:, columns:]


def on_device(vectors, damage, diag_blocks, upper_blocks, block_rows, block_cols, live_slots):
    f32, bf16 = jnp.float32, jnp.bfloat16
    vecs, width = vectors.shape
    here, size = diag_blocks.shape[:2]
    slots = upper_blocks.shape[0]
    owners, groups = lax.axis_size("rows"), lax.axis_size("vec")
    base = lax.axis_index("rows").astype(jnp.int32) * here
    place = jnp.stack([base, live_slots[0]])
    damage = damage.reshape(here, size)
    rim = (RIM, vecs, size)

    copies, blocks, edge = call(
        scale_kernel, "scale", [VM, VM],
        [((groups, vecs, width), bf16), ((here, vecs, size), bf16), (rim, bf16)],
        [], vecs * width, 6 * vecs * width,
    )(vectors, damage)
    every = lax.all_to_all(copies, "vec", 0, 0)
    far = [passed_along(edge, "rows", -step) for step in range(1, REACH)]

    flops = 4 * slots * vecs * size * size
    moved = 2 * slots * size * size
    own, *spread, upper_near = call(
        backward_kernel, "backward", [SM, SM, SM, VM, FAR],
        [((here, vecs, size), f32)] + [(rim, f32)] * 3 + [(upper_blocks.shape, bf16)],
        [
            pltpu.VMEM((REACH * here + 1, vecs, size), f32),
            pltpu.VMEM((here + 1, 2 * vecs, size), bf16),
            pltpu.VMEM((here + 1, 2 * vecs, size), bf16),
            pltpu.SemaphoreType.DMA((CHUNKS,)),
        ],
        flops, moved, WIDE_VMEM_BYTES,
    )(block_rows, block_cols, place, blocks, upper_blocks)
    back = [passed_along(spread[step - 1], "rows", step) for step in range(1, REACH)]

    product, partials = call(
        forward_kernel, "forward", [SM] * 3 + [VM] * 12,
        [((vecs, width), f32), ((owners, vecs // 2, 2 * groups * vecs), f32)],
        [
            pltpu.VMEM((here + 1, vecs, size), f32),
            pltpu.VMEM((REACH * here + 1, 2 * vecs, size), bf16),
            pltpu.VMEM((REACH * here + 1, 2 * vecs, size), bf16),
        ],
        flops, moved,
    )(
        block_rows, block_cols, place, blocks, *far, own, *back, diag_blocks,
        every.reshape(groups * vecs, width), damage, upper_near,
    )
    partials = lax.all_to_all(partials, "rows", 0, 0)
    (projected,) = call(
        functools.partial(sum_kernel, 1.0 / (width * owners)), "sum", [VM],
        [((vecs, groups * vecs), f32)], [], 0, partials.size * 4,
    )(partials)
    return (product, projected)


def solution(mesh):
    return jax.shard_map(
        on_device,
        mesh=mesh,
        in_specs=(
            P("vec", "rows"),
            P("rows"),
            P("rows", None, None),
            P("rows", None, None),
            P("rows"),
            P("rows"),
            P("rows"),
        ),
        out_specs=(P("vec", "rows"), P("vec", None)),
        check_vma=False,
    )
```

time: 187 us -> 69.3 us (0.37)
  blocking collectives: 150 us -> 21 us
  Pallas kernels: 0 us -> 8.14 us
  matrix products: 7.72 us -> 0 us
  local copies, waits for them, and re-layouts: 0.07 us -> 7.03 us
  starting transfers between devices: 22.6 us -> 27.1 us
  other arithmetic: 4.55 us -> 0.08 us
  waiting for transfers between devices: 0.02 us -> 4.11 us
    psum x1 -> x0, blocking collectives: 129 us -> none  [on_device(): projected = lax.psum(partial_gram, 'rows') / total_dof]
    all_to_all x0 -> x1, blocking collectives: none -> 21 us  [on_device(): partials = lax.all_to_all(partials, 'rows', 0, 0)]
    all_gather x1 -> x0, blocking collectives: 20.4 us -> none  [on_device(): lax.all_gather(product.astype(jnp.bfloat16), 'vec', axis=0, tiled=True)]
    all_to_all x0 -> x1, starting transfers between devices: none -> 10.9 us  [on_device(): every = lax.all_to_all(copies, 'vec', 0, 0)]
    pallas_call x0 -> x4, Pallas kernels: none -> 8.14 us  [the longest x1 3.31 us: on_device(): call(backward_kernel, 'backward', [SM, SM, SM, VM, FAR], [((here, vecs, s...]
    dot_general x8 -> x0, matrix products: 7.72 us -> none  [the longest x1 3.38 us: on_device(): jnp.einsum('vsi,sij->vsj', own_rows, upper_blocks, preferred_element_type...]
    unnamed x7 -> x20, local copies, waits for them, and re-layouts: 0.03 us -> 7.03 us
    ppermute x6, starting transfers between devices: 22.6 us -> 16.2 us  [passed_along(): return lax.ppermute(array, axis, pairs)]
  transfers between devices with their start and end apart: 6 -> 7, of which waited for: 0 -> 2; matrix products, arithmetic and copies ran while one was open for 5% -> 0% of each run, Pallas kernels for 0% -> 5%
where the time goes in v2:
time: 69.3 us; the launch traced here: 68.8 us
  starting transfers between devices  27.1 us (39%)
  blocking collectives  21 us (30%)
  Pallas kernels  8.14 us (12%)
  local copies, waits for them, and re-layouts  7.03 us (10%)
  waiting for transfers between devices  4.11 us (6%)
  between operations  1.43 us (2%)
    all_to_all x1, blocking collectives, on_device(): partials = lax.all_to_all(partials, 'rows', 0, 0)  21 us
    ppermute x6, starting transfers between devices, passed_along(): return lax.ppermute(array, axis, pairs)  16.2 us
    all_to_all x1, starting transfers between devices, on_device(): every = lax.all_to_all(copies, 'vec', 0, 0)  10.9 us
    unnamed x20, local copies, waits for them, and re-layouts  7.03 us
    ppermute x6, waiting for transfers between devices, passed_along(): return lax.ppermute(array, axis, pairs)  4.11 us
    pallas_call x1, Pallas kernels, on_device(): call(backward_kernel, 'backward', [SM, SM, SM, VM, FAR], [((here, vecs, s...  3.31 us
    pallas_call x1, Pallas kernels, on_device(): call(forward_kernel, 'forward', [SM] * 3 + [VM] * 12, [((vecs, width), f3...  3.3 us
  transfers between devices with their start and end apart: 7, of which 2 were waited for; matrix products, arithmetic and copies ran while one was open for 0% of the time, Pallas kernels for 5%

profile of v2, /device:TPU:1, one launch (start us, length us, event | category | flops | bytes accessed | tf_op | source)
XLA Modules:
  0.0 68.8 jit_solution(2650161008827892629)
XLA Ops:
  0.6 0.0 copy-start.2
  0.6 0.0 copy-start.3
  0.6 0.9 %copy-done.3 = f32[8,2048]{1,0:T(8,128)S(1)} copy-done((f32[8,2048]{1,0:T(8,128)S(1)}, f32[8,2048]{1,0:T(8,128)}, u32[]{:S(2)}) %copy-start.3) | copy-done | bytes 65560
  1.5 0.7 %copy-done.4 = f32[2048]{0:T(1024)S(1)} copy-done((f32[2048]{0:T(1024)S(1)}, f32[2048]{0:T(1024)}, u32[]{:S(2)}) %copy-start.4) | copy-done | bytes 8216
  2.2 0.8 %scale.1 = (bf16[8,8,2048]{2,1,0:T(8,128)(2,1)}, bf16[16,8,128]{2,1,0:T(8,128)(2,1)S(1)}, bf16[6,8,128]{2,1,0:T(8,128)(2,1)S(1)}) custom-call(f32[8,2048]{1,0:T(8,128)S(1)} %copy-done.3, f32[16,128]{1,0:T(8,128)S(1)} %bitcast.4), custom_call_target="tpu_custom_call" | custom-call | flops 16384 | bytes 98304 | tf_op jit(solution)/shard_map/scale/pallas_call | solution.py:185
  3.0 10.9 %all-to-all-start = ((bf16[8,8,2048]{2,1,0:T(8,128)(2,1)}), bf16[8,8,2048]{2,1,0:T(8,128)(2,1)S(1)}, u32[]{:S(2)}, u32[]{:S(2)}) async-start(bf16[8,8,2048]{2,1,0:T(8,128)(2,1)} %get-tuple-element.18), calls=%async_computation | async-start | bytes 524288 | tf_op jit(solution)/shard_map/all_to_all | solution.py:190
  13.9 1.3 %collective-permute-start.2 = (bf16[6,8,128]{2,1,0:T(8,128)(2,1)S(1)}, bf16[6,8,128]{2,1,0:T(8,128)(2,1)S(1)}, u32[]{:S(2)}, u32[]{:S(2)}) collective-permute-start(bf16[6,8,128]{2,1,0:T(8,128)(2,1)S(1)} %get-tuple-element.13), channel_id=1, source_target_pairs={{24,0},{32,8},{40,16},{48,24},{56,32},{64,40},{72,48},{80,56},{88,... | collective-permute-start | bytes 36872 | tf_op jit(solution)/shard_map/ppermute | solution.py:29
  15.8 0.1 pad_add_fusion.place
  15.9 0.7 copy-done.6
  16.6 0.7 copy-done.8
  17.2 3.3 %backward.1 = (f32[16,8,128]{2,1,0:T(8,128)S(1)}, f32[6,8,128]{2,1,0:T(8,128)S(1)}, f32[6,8,128]{2,1,0:T(8,128)S(1)}, f32[6,8,128]{2,1,0:T(8,128)S(1)}, bf16[128,128,128]{2,1,0:T(8,128)(2,1)S(1)}) custom-call(s32[128]{0:T(128)S(1)} %copy-done.6, s32[128]{0:T(128)S(1)} %copy-done.8, s32[2]{0:T(128)S(1)} %pad_add_fusion.place, ...), custom_call_target="tpu_custom_call" | custom-call | flops 67108864 | bytes 4194304 | tf_op jit(solution)/shard_map/backward/pallas_call | solution.py:195
  20.5 0.0 copy-start
  20.6 1.9 %copy-done = bf16[128,128,128]{2,1,0:T(8,128)(2,1)} copy-done((bf16[128,128,128]{2,1,0:T(8,128)(2,1)}, bf16[128,128,128]{2,1,0:T(8,128)(2,1)S(1)}, u32[]{:S(2)}) %copy-start) | copy-done | bytes 4194328
  22.5 4.1 %collective-permute-start.3 = (f32[6,8,128]{2,1,0:T(8,128)S(1)}, f32[6,8,128]{2,1,0:T(8,128)S(1)}, u32[]{:S(2)}, u32[]{:S(2)}) collective-permute-start(f32[6,8,128]{2,1,0:T(8,128)S(1)} %get-tuple-element.15), channel_id=1, source_target_pairs={{0,8},{8,16},{16,24},{24,32},{32,40},{40,48},{48,56},{56,64},{64,7... | collective-permute-start | bytes 73736 | tf_op jit(solution)/shard_map/ppermute | solution.py:29
  26.6 3.8 %collective-permute-start.4 = (f32[6,8,128]{2,1,0:T(8,128)S(1)}, f32[6,8,128]{2,1,0:T(8,128)S(1)}, u32[]{:S(2)}, u32[]{:S(2)}) collective-permute-start(f32[6,8,128]{2,1,0:T(8,128)S(1)} %get-tuple-element.16), channel_id=1, source_target_pairs={{0,16},{8,24},{16,32},{24,40},{32,48},{40,56},{48,64},{56,72},{64,... | collective-permute-start | bytes 73736 | tf_op jit(solution)/shard_map/ppermute | solution.py:29
  30.5 3.8 %collective-permute-start.5 = (f32[6,8,128]{2,1,0:T(8,128)S(1)}, f32[6,8,128]{2,1,0:T(8,128)S(1)}, u32[]{:S(2)}, u32[]{:S(2)}) collective-permute-start(f32[6,8,128]{2,1,0:T(8,128)S(1)} %get-tuple-element.17), channel_id=1, source_target_pairs={{0,24},{8,32},{16,40},{24,48},{32,56},{40,64},{48,72},{56,80},{64,... | collective-permute-start | bytes 73736 | tf_op jit(solution)/shard_map/ppermute | solution.py:29
  34.2 1.3 %collective-permute-start.1 = (bf16[6,8,128]{2,1,0:T(8,128)(2,1)S(1)}, bf16[6,8,128]{2,1,0:T(8,128)(2,1)S(1)}, u32[]{:S(2)}, u32[]{:S(2)}) collective-permute-start(bf16[6,8,128]{2,1,0:T(8,128)(2,1)S(1)} %get-tuple-element.13), channel_id=1, source_target_pairs={{16,0},{24,8},{32,16},{40,24},{48,32},{56,40},{64,48},{72,56},{80,... | collective-permute-start | bytes 36872 | tf_op jit(solution)/shard_map/ppermute | solution.py:29
  35.5 0.0 collective-permute-done.2.far3
  35.6 1.9 %collective-permute-start = (bf16[6,8,128]{2,1,0:T(8,128)(2,1)S(1)}, bf16[6,8,128]{2,1,0:T(8,128)(2,1)S(1)}, u32[]{:S(2)}, u32[]{:S(2)}) collective-permute-start(bf16[6,8,128]{2,1,0:T(8,128)(2,1)S(1)} %get-tuple-element.13), channel_id=1, source_target_pairs={{8,0},{16,8},{24,16},{32,24},{40,32},{48,40},{56,48},{64,56},{72,6... | collective-permute-start | bytes 36872 | tf_op jit(solution)/shard_map/ppermute | solution.py:29
  37.5 2.5 %collective-permute-done.1.far2 = bf16[6,8,128]{2,1,0:T(8,128)(2,1)S(1)} collective-permute-done((bf16[6,8,128]{2,1,0:T(8,128)(2,1)S(1)}, bf16[6,8,128]{2,1,0:T(8,128)(2,1)S(1)}, u32[]{:S(2)}, u32[]{:S(2)}) %collective-permute-start.1) | collective-permute-done | bytes 12320 | tf_op jit(solution)/shard_map/ppermute | solution.py:29
  40.0 1.6 %collective-permute-done.far1 = bf16[6,8,128]{2,1,0:T(8,128)(2,1)S(1)} collective-permute-done((bf16[6,8,128]{2,1,0:T(8,128)(2,1)S(1)}, bf16[6,8,128]{2,1,0:T(8,128)(2,1)S(1)}, u32[]{:S(2)}, u32[]{:S(2)}) %collective-permute-start) | collective-permute-done | bytes 12320 | tf_op jit(solution)/shard_map/ppermute | solution.py:29
  41.6 0.0 collective-permute-done.3.back1
  41.6 0.0 collective-permute-done.4.back2
  41.6 0.0 collective-permute-done.5.back3
  41.6 0.0 all-to-all-done
  41.6 0.0 copy-done.2
  41.6 0.0 copy-done.5
  41.6 0.0 copy-done.7
  41.7 2.2 %copy-done.1 = bf16[128,128,128]{2,1,0:T(8,128)(2,1)S(1)} copy-done((bf16[128,128,128]{2,1,0:T(8,128)(2,1)S(1)}, bf16[128,128,128]{2,1,0:T(8,128)(2,1)}, u32[]{:S(2)}) %copy-start.1) | copy-done | bytes 4194328
  43.8 3.3 %forward.1 = (f32[8,2048]{1,0:T(8,128)}, f32[64,4,128]{2,1,0:T(4,128)S(1)}) custom-call(s32[128]{0:T(128)S(1)} %copy-done.7, s32[128]{0:T(128)S(1)} %copy-done.9, s32[2]{0:T(128)S(1)} %pad_add_fusion.place, bf16[16,8,128]{2,1,0:T(8,128)(2,1)S(1)} %get-tuple-element.12.blocks, bf16[6,8,128]{2,1,0:T(8,128)(2,1)S(1)} %collective-permute-done.far1, ...), custom_call_target="tpu_custom_call" | custom-call | flops 67108864 | bytes 4194304 | tf_op jit(solution)/shard_map/forward/pallas_call | solution.py:208
  47.1 21.0 %all_to_all.10.parts = f32[64,4,128]{2,1,0:T(4,128)S(1)} all-to-all(f32[64,4,128]{2,1,0:T(4,128)S(1)} %get-tuple-element.21), channel_id=1, replica_groups=mesh['rows'=64,'vec'=8] {'rows'}, dimensions={0} | all-to-all | bytes 262144 | tf_op jit(solution)/shard_map/all_to_all | solution.py:221
  68.1 0.7 %sum.1 = f32[8,64]{1,0:T(8,128)} custom-call(f32[64,4,128]{2,1,0:T(4,128)S(1)} %all_to_all.10.parts), custom_call_target="tpu_custom_call" | custom-call | bytes 131072 | tf_op jit(solution)/shard_map/sum/pallas_call | solution.py:222
  (8 shorter events, 0.0 us)
Async XLA Ops:
  0.6 41.0 %copy-start.2 = (bf16[16,128,128]{2,1,0:T(8,128)(2,1)S(1)}, bf16[16,128,128]{2,1,0:T(8,128)(2,1)}, u32[]{:S(2)}) copy-start(bf16[16,128,128]{2,1,0:T(8,128)(2,1)} %diag.1) | copy-start | bytes 1572868
  0.6 0.9 %copy-start.3 = (f32[8,2048]{1,0:T(8,128)S(1)}, f32[8,2048]{1,0:T(8,128)}, u32[]{:S(2)}) copy-start(f32[8,2048]{1,0:T(8,128)} %vectors.1) | copy-start | bytes 196612
  1.5 0.7 %copy-start.4 = (f32[2048]{0:T(1024)S(1)}, f32[2048]{0:T(1024)}, u32[]{:S(2)}) copy-start(f32[2048]{0:T(1024)} %param.8) | copy-start | bytes 24580
  2.2 39.4 %copy-start.5 = (f32[2048]{0:T(1024)S(1)}, f32[2048]{0:T(1024)}, u32[]{:S(2)}) copy-start(f32[2048]{0:T(1024)} %param.8) | copy-start | bytes 24580
  2.2 39.4 %copy-start.7 = (s32[128]{0:T(128)S(1)}, s32[128]{0:T(128)}, u32[]{:S(2)}) copy-start(s32[128]{0:T(128)} %rows.3) | copy-start | bytes 1540
  2.2 39.4 %copy-start.9 = (s32[128]{0:T(128)S(1)}, s32[128]{0:T(128)}, u32[]{:S(2)}) copy-start(s32[128]{0:T(128)} %cols.3) | copy-start | bytes 1540
  3.0 38.6 %all-to-all-start = ((bf16[8,8,2048]{2,1,0:T(8,128)(2,1)}), bf16[8,8,2048]{2,1,0:T(8,128)(2,1)S(1)}, u32[]{:S(2)}, u32[]{:S(2)}) async-start(bf16[8,8,2048]{2,1,0:T(8,128)(2,1)} %get-tuple-element.18), calls=%async_computation | async-start | bytes 524288 | tf_op jit(solution)/shard_map/all_to_all | solution.py:190
  13.9 21.7 %collective-permute-start.2 = (bf16[6,8,128]{2,1,0:T(8,128)(2,1)S(1)}, bf16[6,8,128]{2,1,0:T(8,128)(2,1)S(1)}, u32[]{:S(2)}, u32[]{:S(2)}) collective-permute-start(bf16[6,8,128]{2,1,0:T(8,128)(2,1)S(1)} %get-tuple-element.13), channel_id=1, source_target_pairs={{24,0},{32,8},{40,16},{48,24},{56,32},{64,40},{72,48},{80,56},{88,... | collective-permute-start | bytes 36872 | tf_op jit(solution)/shard_map/ppermute | solution.py:29
  15.9 0.7 copy-start.6
  16.6 0.7 copy-start.8
  20.5 1.9 %copy-start = (bf16[128,128,128]{2,1,0:T(8,128)(2,1)}, bf16[128,128,128]{2,1,0:T(8,128)(2,1)S(1)}, u32[]{:S(2)}) copy-start(bf16[128,128,128]{2,1,0:T(8,128)(2,1)S(1)} %get-tuple-element.19.upper) | copy-start | bytes 12582916
  22.5 19.1 %collective-permute-start.3 = (f32[6,8,128]{2,1,0:T(8,128)S(1)}, f32[6,8,128]{2,1,0:T(8,128)S(1)}, u32[]{:S(2)}, u32[]{:S(2)}) collective-permute-start(f32[6,8,128]{2,1,0:T(8,128)S(1)} %get-tuple-element.15), channel_id=1, source_target_pairs={{0,8},{8,16},{16,24},{24,32},{32,40},{40,48},{48,56},{56,64},{64,7... | collective-permute-start | bytes 73736 | tf_op jit(solution)/shard_map/ppermute | solution.py:29
  26.6 15.0 %collective-permute-start.4 = (f32[6,8,128]{2,1,0:T(8,128)S(1)}, f32[6,8,128]{2,1,0:T(8,128)S(1)}, u32[]{:S(2)}, u32[]{:S(2)}) collective-permute-start(f32[6,8,128]{2,1,0:T(8,128)S(1)} %get-tuple-element.16), channel_id=1, source_target_pairs={{0,16},{8,24},{16,32},{24,40},{32,48},{40,56},{48,64},{56,72},{64,... | collective-permute-start | bytes 73736 | tf_op jit(solution)/shard_map/ppermute | solution.py:29
  30.5 11.1 %collective-permute-start.5 = (f32[6,8,128]{2,1,0:T(8,128)S(1)}, f32[6,8,128]{2,1,0:T(8,128)S(1)}, u32[]{:S(2)}, u32[]{:S(2)}) collective-permute-start(f32[6,8,128]{2,1,0:T(8,128)S(1)} %get-tuple-element.17), channel_id=1, source_target_pairs={{0,24},{8,32},{16,40},{24,48},{32,56},{40,64},{48,72},{56,80},{64,... | collective-permute-start | bytes 73736 | tf_op jit(solution)/shard_map/ppermute | solution.py:29
  34.2 5.8 %collective-permute-start.1 = (bf16[6,8,128]{2,1,0:T(8,128)(2,1)S(1)}, bf16[6,8,128]{2,1,0:T(8,128)(2,1)S(1)}, u32[]{:S(2)}, u32[]{:S(2)}) collective-permute-start(bf16[6,8,128]{2,1,0:T(8,128)(2,1)S(1)} %get-tuple-element.13), channel_id=1, source_target_pairs={{16,0},{24,8},{32,16},{40,24},{48,32},{56,40},{64,48},{72,56},{80,... | collective-permute-start | bytes 36872 | tf_op jit(solution)/shard_map/ppermute | solution.py:29
  35.6 6.0 %collective-permute-start = (bf16[6,8,128]{2,1,0:T(8,128)(2,1)S(1)}, bf16[6,8,128]{2,1,0:T(8,128)(2,1)S(1)}, u32[]{:S(2)}, u32[]{:S(2)}) collective-permute-start(bf16[6,8,128]{2,1,0:T(8,128)(2,1)S(1)} %get-tuple-element.13), channel_id=1, source_target_pairs={{8,0},{16,8},{24,16},{32,24},{40,32},{48,40},{56,48},{64,56},{72,6... | collective-permute-start | bytes 36872 | tf_op jit(solution)/shard_map/ppermute | solution.py:29
  41.6 2.2 %copy-start.1 = (bf16[128,128,128]{2,1,0:T(8,128)(2,1)S(1)}, bf16[128,128,128]{2,1,0:T(8,128)(2,1)}, u32[]{:S(2)}) copy-start(bf16[128,128,128]{2,1,0:T(8,128)(2,1)} %copy-done) | copy-start | bytes 12582916

commit v3 on v2

v3 whole, which is shorter than its diff:
```python
import functools

import jax
import jax.numpy as jnp
from jax import lax
from jax.experimental import pallas as pl
from jax.experimental.pallas import tpu as pltpu
from jax.sharding import PartitionSpec as P

REACH = 4
RIM = 6
PIECES = (16, 32, 32, 48)
SMALL_VMEM = 8 << 20
BLOCKS_STAY = 50 << 20
FIRST_VMEM = 53 << 20


resid_eta = 0.001

VM = pl.BlockSpec(memory_space=pltpu.VMEM)
SM = pl.BlockSpec(memory_space=pltpu.SMEM)
FAR = pl.BlockSpec(memory_space=pl.ANY)
ROW, COL, CORE = 0, 1, 2
TRANSPOSED = (((1,), (1,)), ((), ()))


def call(kernel, name, in_specs, outs, scratch, vmem, flops, moved):
    return pl.pallas_call(
        kernel,
        name=name,
        in_specs=in_specs,
        out_specs=[VM] * len(outs),
        out_shape=[jax.ShapeDtypeStruct(shape, dtype) for shape, dtype in outs],
        scratch_shapes=scratch,
        compiler_params=pltpu.CompilerParams(vmem_limit_bytes=vmem),
        cost_estimate=pl.CostEstimate(flops=flops, bytes_accessed=moved, transcendentals=0),
    )


def softness(damage):
    return jnp.sqrt((1.0 - damage) ** 2 + resid_eta)


def put_halves(top, bottom, at, x):
    z = jnp.zeros_like(x)
    top[at] = jnp.concatenate([x, z], 0).astype(jnp.bfloat16)
    bottom[at] = jnp.concatenate([z, x], 0).astype(jnp.bfloat16)


def streamed(upper_far, upper, sems):
    copies, first = [], 0
    for i, count in enumerate(PIECES):
        cut = pl.ds(first, count)
        copies.append(pltpu.make_async_copy(upper_far.at[cut], upper.at[cut], sems.at[i]))
        first += count
    assert first == upper.shape[0]
    return copies


def each_pair(first, count, where, take, give, top, bottom, total, product):
    vecs = total.shape[1]
    results = []
    for s in range(first, first + count, 2):
        x = jnp.concatenate([top[where[take, s]], bottom[where[take, s + 1]]], axis=1)
        y = product(x, s)
        results += [y[:vecs], y[vecs:]]
    for k in range(count):
        total[where[give, first + k]] += results[k]


def backward_kernel(
    where, vectors, damage, upper_far, everyones, blocks, rim, own, one, chips, swap,
    upper, total, top, bottom, sems
):
    here = own.shape[0]
    size = upper.shape[1]
    copies = streamed(upper_far, upper, sems)
    for copy in copies:
        copy.start()
    total[...] = jnp.zeros_like(total)
    soft = softness(damage[...])
    for b in range(here):
        cut = slice(b * size, (b + 1) * size)
        scaled = (vectors[:, cut] * soft[b : b + 1, :]).astype(jnp.bfloat16)
        blocks[b] = scaled
        if b < RIM:
            rim[b] = scaled
        for i in range(everyones.shape[0]):
            everyones[i, :, cut] = scaled
        put_halves(top, bottom, b, scaled.astype(jnp.float32))
    put_halves(top, bottom, here, jnp.zeros(total.shape[1:], jnp.float32))

    def product(x, s):
        pair = upper[pl.ds(s, 2)].reshape(2 * size, size)
        return jnp.dot(x, pair, preferred_element_type=jnp.float32)

    first = 0
    for copy, count in zip(copies, PIECES):
        copy.wait()
        each_pair(first, count, where, ROW, COL, top, bottom, total, product)
        first += count
    own[...] = total[:here]
    one[...] = total[here : here + RIM]
    second_core = where[CORE, 0]
    other = jnp.where(second_core == 1, here, 3 * here)
    chips[0] = total[2 * here : 2 * here + RIM]
    chips[1] = total[pl.ds(other, RIM)]
    swap[...] = jnp.where(
        second_core == 1, total[3 * here : 3 * here + RIM], blocks[:RIM].astype(jnp.float32)
    )


def relay_kernel(where, rim, far, one, chips, out):
    out[0] = rim[...].astype(jnp.float32)
    out[1] = far[...].astype(jnp.float32)
    out[2] = chips[1] + jnp.where(where[CORE, 0] == 1, 0.0, one[...])


def forward_kernel(
    where, blocks, far, chips, swap, mate, own, diag, every, damage, upper_far,
    product_out, copies_out, upper, total, top, bottom, sems
):
    here = own.shape[0]
    size = diag.shape[1]
    vecs = blocks.shape[1]
    copies = streamed(upper_far, upper, sems)
    for copy in copies:
        copy.start()
    second_core = where[CORE, 0] == 1
    for b in range(here):
        put_halves(top, bottom, b, blocks[b].astype(jnp.float32))
    for b in range(RIM):
        put_halves(top, bottom, here + b, jnp.where(second_core, mate[1, b], mate[0, b]))
        put_halves(top, bottom, 2 * here + b, far[b].astype(jnp.float32))
        put_halves(top, bottom, 3 * here + b, jnp.where(second_core, swap[b], mate[1, b]))
    put_halves(top, bottom, REACH * here, jnp.zeros((vecs, size), jnp.float32))
    for b in range(here):
        total[b] = own[b] + lax.dot_general(
            blocks[b], diag[b], TRANSPOSED, preferred_element_type=jnp.float32
        )
    total[:RIM] += chips[0] + mate[2] + jnp.where(second_core, 0.0, swap[...])

    def product(x, s):
        pair = jnp.concatenate([upper[s], upper[s + 1]], axis=1)
        return lax.dot_general(x, pair, TRANSPOSED, preferred_element_type=jnp.float32)

    first = 0
    for copy, count in zip(copies, PIECES):
        copy.wait()
        each_pair(first, count, where, COL, ROW, top, bottom, total, product)
        first += count
    soft = softness(damage[...])
    gram = jnp.zeros((2 * vecs, every.shape[0]), jnp.float32)
    for b in range(here):
        raw = total[b]
        cut = slice(b * size, (b + 1) * size)
        product_out[:, cut] = raw * soft[b : b + 1, :]
        high = raw.astype(jnp.bfloat16)
        low = (raw - high.astype(jnp.float32)).astype(jnp.bfloat16)
        gram += lax.dot_general(
            jnp.concatenate([high, low], 0), every[:, cut], TRANSPOSED,
            preferred_element_type=jnp.float32,
        )
    gram = gram[:vecs] + gram[vecs:]
    half = vecs // 2
    packed = jnp.concatenate([gram[:half], gram[half:]], axis=1)
    copies_out[...] = jnp.broadcast_to(packed[None], copies_out.shape)


def sum_kernel(scale, parts, out):
    packed = jnp.sum(parts[...], axis=0) * scale
    columns = out.shape[1]
    half = packed.shape[0]
    out[:half] = packed[:, :columns]
    out[half:] = packed[:, columns:]


def backward(groups, where, vectors, damage, upper):
    f32, bf16 = jnp.float32, jnp.bfloat16
    vecs = vectors.shape[0]
    here, size = damage.shape
    slots = upper.shape[0]
    rim = (RIM, vecs, size)
    return call(
        backward_kernel, "backward", [SM, VM, VM, FAR],
        [
            ((groups, vecs, here * size), bf16), ((here, vecs, size), bf16), (rim, bf16),
            ((here, vecs, size), f32), (rim, f32), ((2,) + rim, f32), (rim, f32),
        ],
        [
            pltpu.VMEM(upper.shape, bf16),
            pltpu.VMEM((REACH * here + 1, vecs, size), f32),
            pltpu.VMEM((here + 1, 2 * vecs, size), bf16),
            pltpu.VMEM((here + 1, 2 * vecs, size), bf16),
            pltpu.SemaphoreType.DMA((len(PIECES),)),
        ],
        FIRST_VMEM, 2 * slots * vecs * size * size, 2 * slots * size * size,
    )(where, vectors, damage, upper)


def forward(owners, where, blocks, far, chips, swap, mate, own, diag, every, damage, upper):
    f32, bf16 = jnp.float32, jnp.bfloat16
    here, vecs, size = blocks.shape
    slots = upper.shape[0]
    return call(
        forward_kernel, "forward", [SM] + [VM] * 9 + [FAR],
        [((vecs, here * size), f32), ((owners, vecs // 2, 2 * every.shape[0]), f32)],
        [
            pltpu.VMEM(upper.shape, bf16),
            pltpu.VMEM((here + 1, vecs, size), f32),
            pltpu.VMEM((REACH * here + 1, 2 * vecs, size), bf16),
            pltpu.VMEM((REACH * here + 1, 2 * vecs, size), bf16),
            pltpu.SemaphoreType.DMA((len(PIECES),)),
        ],
        BLOCKS_STAY, 2 * slots * vecs * size * size, 2 * slots * size * size,
    )(where, blocks, far, chips, swap, mate, own, diag, every, damage, upper)


def on_device(vectors, damage, diag_blocks, upper_blocks, block_rows, block_cols, live_slots):
    f32, bf16 = jnp.float32, jnp.bfloat16
    vecs, width = vectors.shape
    here, size = diag_blocks.shape[:2]
    owners, groups = lax.axis_size("rows"), lax.axis_size("vec")
    mine = lax.axis_index("rows").astype(jnp.int32)
    stored = jnp.arange(upper_blocks.shape[0]) < live_slots[0]
    rows = jnp.where(stored, block_rows - mine * here, here)
    cols = jnp.where(stored, block_cols - mine * here, REACH * here)
    where = jnp.stack([rows, cols, jnp.full_like(rows, mine & 1)])
    damage = damage.reshape(here, size)
    rim = (RIM, vecs, size)

    copies, blocks, edge, own, one, chips, swap = backward(
        groups, where, vectors, damage, upper_blocks
    )
    every = lax.all_to_all(copies, "vec", 0, 0).reshape(groups * vecs, width)

    down = [(d, d - 2) for d in range(2, owners)]
    up = [(d, d + 2) for d in range(owners - 2)]
    across = [(d, d + 3) for d in range(1, owners - 3, 2)]
    across += [(b, a) for a, b in across]
    mates = [(d, d ^ 1) for d in range(owners)]

    far = lax.ppermute(edge, "rows", down)
    chips = lax.ppermute(chips, "rows", up)
    swap = lax.ppermute(swap, "rows", across)
    (mate,) = call(
        relay_kernel, "relay", [SM] + [VM] * 4, [((3,) + rim, f32)], [], SMALL_VMEM, 0, 8 * size,
    )(where, edge, far, one, chips)
    mate = lax.ppermute(mate, "rows", mates)

    product, partials = forward(
        owners, where, blocks, far, chips, swap, mate, own, diag_blocks,
        every, damage, upper_blocks,
    )
    partials = lax.all_to_all(partials, "rows", 0, 0)
    (projected,) = call(
        functools.partial(sum_kernel, 1.0 / (width * owners)), "sum", [VM],
        [((vecs, groups * vecs), f32)], [], SMALL_VMEM, 0, partials.size * 4,
    )(partials)
    return (product, projected)


def solution(mesh):
    return jax.shard_map(
        on_device,
        mesh=mesh,
        in_specs=(
            P("vec", "rows"),
            P("rows"),
            P("rows", None, None),
            P("rows", None, None),
            P("rows"),
            P("rows"),
            P("rows"),
        ),
        out_specs=(P("vec", "rows"), P("vec", None)),
        check_vma=False,
    )
```

time: 69.3 us -> 64.4 us (0.929)
  local copies, waits for them, and re-layouts: 7.03 us -> 1.62 us
  starting transfers between devices: 27.1 us -> 24.3 us
  Pallas kernels: 8.14 us -> 9.43 us
  waiting for transfers between devices: 4.11 us -> 4.94 us
    unnamed x20 -> x8, local copies, waits for them, and re-layouts: 7.03 us -> 1.54 us
    ppermute x6 -> x4, starting transfers between devices: 16.2 us -> 13.4 us  [the longest x1 4.94 us: on_device(): swap = lax.ppermute(swap, 'rows', across)]
    pallas_call x3, Pallas kernels: 7.41 us -> 8.71 us  [the longest x1 4.33 us: forward(): call(forward_kernel, 'forward', [SM] + [VM] * 9 + [FAR], [((vecs, here *...]
    ppermute x6 -> x4, waiting for transfers between devices: 4.11 us -> 4.94 us  [the longest x1 3.43 us: on_device(): far = lax.ppermute(edge, 'rows', down)]
  transfers between devices with their start and end apart: 7 -> 5, of which waited for: 2 -> 2; matrix products, arithmetic and copies ran while one was open for 0% -> 0% of each run, Pallas kernels for 5% -> 1%
where the time goes in v3:
time: 64.4 us; the launch traced here: 63.9 us
  starting transfers between devices  24.3 us (38%)
  blocking collectives  21.5 us (33%)
  Pallas kernels  9.43 us (15%)
  waiting for transfers between devices  4.94 us (8%)
  local copies, waits for them, and re-layouts  1.62 us (3%)
  between operations  1.42 us (2%)
  other arithmetic  0.75 us (1%)
    all_to_all x1, blocking collectives, on_device(): partials = lax.all_to_all(partials, 'rows', 0, 0)  21.5 us
    all_to_all x1, starting transfers between devices, on_device(): every = lax.all_to_all(copies, 'vec', 0, 0).reshape(groups * vecs, width)  10.9 us
    ppermute x1, starting transfers between devices, on_device(): swap = lax.ppermute(swap, 'rows', across)  4.94 us
    pallas_call x1, Pallas kernels, forward(): call(forward_kernel, 'forward', [SM] + [VM] * 9 + [FAR], [((vecs, here *...  4.33 us
    ppermute x1, starting transfers between devices, on_device(): mate = lax.ppermute(mate, 'rows', mates)  3.98 us
    pallas_call x1, Pallas kernels, backward(): call(backward_kernel, 'backward', [SM, VM, VM, FAR], [((groups, vecs, her...  3.81 us
    ppermute x1, waiting for transfers between devices, on_device(): far = lax.ppermute(edge, 'rows', down)  3.43 us
    ppermute x1, starting transfers between devices, on_device(): chips = lax.ppermute(chips, 'rows', up)  3.2 us
  transfers between devices with their start and end apart: 5, of which 2 were waited for; matrix products, arithmetic and copies ran while one was open for 0% of the time, Pallas kernels for 1%

profile of v3, /device:TPU:1, one launch (start us, length us, event | category | flops | bytes accessed | tf_op | source)
XLA Modules:
  0.0 63.9 jit_solution(3887213197210054282)
XLA Ops:
  0.6 0.0 copy-start
  1.3 0.1 pad.2.clone
  1.4 0.7 %fusion = (s32[1,128]{1,0:T(1,128)S(1)}, s32[1,128]{1,0:T(1,128)S(1)}) fusion(s32[128]{0:T(128)} %param.11, s32[]{:T(128)S(6)} %mul.4, s32[]{:T(128)} %bitcast.8, s32[128]{0:T(128)} %param.12), kind=kLoop, calls=%fused_computation.3 | loop fusion | flops 640 | bytes 2056 | tf_op jit(solution)/shard_map/stack | solution.py:228
  2.1 0.1 add_add_fusion.where
  2.2 0.0 copy-start.1
  2.2 0.8 %copy-done.1 = f32[8,2048]{1,0:T(8,128)S(1)} copy-done((f32[8,2048]{1,0:T(8,128)S(1)}, f32[8,2048]{1,0:T(8,128)}, u32[]{:S(2)}) %copy-start.1) | copy-done | bytes 65560
  3.0 0.0 copy-start.2
  3.0 0.7 %copy-done.2 = f32[2048]{0:T(1024)S(1)} copy-done((f32[2048]{0:T(1024)S(1)}, f32[2048]{0:T(1024)}, u32[]{:S(2)}) %copy-start.2) | copy-done | bytes 8216
  3.7 0.0 copy-start.3
  3.7 3.8 %backward.1 = (bf16[8,8,2048]{2,1,0:T(8,128)(2,1)}, bf16[16,8,128]{2,1,0:T(8,128)(2,1)S(1)}, bf16[6,8,128]{2,1,0:T(8,128)(2,1)S(1)}, f32[16,8,128]{2,1,0:T(8,128...) custom-call(s32[3,128]{1,0:T(4,128)S(1)} %add_add_fusion.where, ...), custom_call_target="tpu_custom_call" | custom-call | flops 33554432 | bytes 4194304 | tf_op jit(solution)/shard_map/backward/pallas_call | solution.py:184
  7.5 10.9 %all-to-all-start = ((bf16[8,8,2048]{2,1,0:T(8,128)(2,1)}), bf16[8,8,2048]{2,1,0:T(8,128)(2,1)S(1)}, u32[]{:S(2)}, u32[]{:S(2)}) async-start(bf16[8,8,2048]{2,1,0:T(8,128)(2,1)} %get-tuple-element.17), calls=%async_computation | async-start | bytes 524288 | tf_op jit(solution)/shard_map/all_to_all | solution.py:235
  18.4 3.2 %collective-permute-start.1 = (f32[2,6,8,128]{3,2,1,0:T(8,128)S(1)}, f32[2,6,8,128]{3,2,1,0:T(8,128)S(1)}, u32[]{:S(2)}, u32[]{:S(2)}) collective-permute-start(f32[2,6,8,128]{3,2,1,0:T(8,128)S(1)} %get-tuple-element.13), channel_id=1, source_target_pairs={{0,16},{8,24},{16,32},{24,40},{32,48},{40,56},{48,64},{56,72},{64,... | collective-permute-start | bytes 147464 | tf_op jit(solution)/shard_map/ppermute | solution.py:244
  21.6 1.3 %collective-permute-start = (bf16[6,8,128]{2,1,0:T(8,128)(2,1)S(1)}, bf16[6,8,128]{2,1,0:T(8,128)(2,1)S(1)}, u32[]{:S(2)}, u32[]{:S(2)}) collective-permute-start(bf16[6,8,128]{2,1,0:T(8,128)(2,1)S(1)} %get-tuple-element.12.rim), channel_id=1, source_target_pairs={{16,0},{24,8},{32,16},{40,24},{48,32},{56,40},{64,48},{72,56},{80,... | collective-permute-start | bytes 36872 | tf_op jit(solution)/shard_map/ppermute | solution.py:243
  22.9 3.4 %collective-permute-done.far = bf16[6,8,128]{2,1,0:T(8,128)(2,1)S(1)} collective-permute-done((bf16[6,8,128]{2,1,0:T(8,128)(2,1)S(1)}, bf16[6,8,128]{2,1,0:T(8,128)(2,1)S(1)}, u32[]{:S(2)}, u32[]{:S(2)}) %collective-permute-start) | collective-permute-done | bytes 12320 | tf_op jit(solution)/shard_map/ppermute | solution.py:243
  26.3 0.0 collective-permute-done.1.chips
  26.4 0.6 relay.1
  26.9 4.0 %collective-permute-start.3 = (f32[3,6,8,128]{3,2,1,0:T(8,128)S(1)}, f32[3,6,8,128]{3,2,1,0:T(8,128)S(1)}, u32[]{:S(2)}, u32[]{:S(2)}) collective-permute-start(f32[3,6,8,128]{3,2,1,0:T(8,128)S(1)} %relay.1), channel_id=1, source_target_pairs={{0,8},{8,0},{16,24},{24,16},{32,40},{40,32},{48,56},{56,48},{64,72... | collective-permute-start | bytes 221192 | tf_op jit(solution)/shard_map/ppermute | solution.py:249
  30.9 4.9 %collective-permute-start.2 = (f32[6,8,128]{2,1,0:T(8,128)S(1)}, f32[6,8,128]{2,1,0:T(8,128)S(1)}, u32[]{:S(2)}, u32[]{:S(2)}) collective-permute-start(f32[6,8,128]{2,1,0:T(8,128)S(1)} %get-tuple-element.14), channel_id=1, source_target_pairs={{8,32},{24,48},{40,64},{56,80},{72,96},{88,112},{104,128},{120,144... | collective-permute-start | bytes 73736 | tf_op jit(solution)/shard_map/ppermute | solution.py:245
  35.9 1.5 %collective-permute-done.2.swap = f32[6,8,128]{2,1,0:T(8,128)S(1)} collective-permute-done((f32[6,8,128]{2,1,0:T(8,128)S(1)}, f32[6,8,128]{2,1,0:T(8,128)S(1)}, u32[]{:S(2)}, u32[]{:S(2)}) %collective-permute-start.2) | collective-permute-done | bytes 24608 | tf_op jit(solution)/shard_map/ppermute | solution.py:245
  37.4 0.0 collective-permute-done.3.mate
  37.4 0.0 all-to-all-done
  37.4 0.0 copy-done
  37.4 0.0 copy-done.3
  37.4 4.3 %forward.1 = (f32[8,2048]{1,0:T(8,128)}, f32[64,4,128]{2,1,0:T(4,128)S(1)}) custom-call(s32[3,128]{1,0:T(4,128)S(1)} %add_add_fusion.where, bf16[16,8,128]{2,1,0:T(8,128)(2,1)S(1)} %get-tuple-element.11.blocks, bf16[6,8,128]{2,1,0:T(8,128)(2,1)S(1)} %collective-permute-done.far, f32[2,6,8,128]{3,2,1,0:T(8,128)S(1)} %collective-permute-done.1.chips, ...), custom_call_target="tpu_custom_call" | custom-call | flops 33554432 | bytes 4194304 | tf_op jit(solution)/shard_map/forward/pallas_call | solution.py:205
  41.7 21.5 %all_to_all.10.parts = f32[64,4,128]{2,1,0:T(4,128)S(1)} all-to-all(f32[64,4,128]{2,1,0:T(4,128)S(1)} %get-tuple-element.19), channel_id=1, replica_groups=mesh['rows'=64,'vec'=8] {'rows'}, dimensions={0} | all-to-all | bytes 262144 | tf_op jit(solution)/shard_map/all_to_all | solution.py:255
  63.2 0.7 %sum.1 = f32[8,64]{1,0:T(8,128)} custom-call(f32[64,4,128]{2,1,0:T(4,128)S(1)} %all_to_all.10.parts), custom_call_target="tpu_custom_call" | custom-call | bytes 131072 | tf_op jit(solution)/shard_map/sum/pallas_call | solution.py:256
Async XLA Ops:
  0.6 36.7 %copy-start = (bf16[16,128,128]{2,1,0:T(8,128)(2,1)S(1)}, bf16[16,128,128]{2,1,0:T(8,128)(2,1)}, u32[]{:S(2)}) copy-start(bf16[16,128,128]{2,1,0:T(8,128)(2,1)} %diag.1) | copy-start | bytes 1572868
  2.2 0.8 %copy-start.1 = (f32[8,2048]{1,0:T(8,128)S(1)}, f32[8,2048]{1,0:T(8,128)}, u32[]{:S(2)}) copy-start(f32[8,2048]{1,0:T(8,128)} %vectors.1) | copy-start | bytes 196612
  3.0 0.7 %copy-start.2 = (f32[2048]{0:T(1024)S(1)}, f32[2048]{0:T(1024)}, u32[]{:S(2)}) copy-start(f32[2048]{0:T(1024)} %param.8) | copy-start | bytes 24580
  3.7 33.7 %copy-start.3 = (f32[2048]{0:T(1024)S(1)}, f32[2048]{0:T(1024)}, u32[]{:S(2)}) copy-start(f32[2048]{0:T(1024)} %param.8) | copy-start | bytes 24580
  7.5 29.8 %all-to-all-start = ((bf16[8,8,2048]{2,1,0:T(8,128)(2,1)}), bf16[8,8,2048]{2,1,0:T(8,128)(2,1)S(1)}, u32[]{:S(2)}, u32[]{:S(2)}) async-start(bf16[8,8,2048]{2,1,0:T(8,128)(2,1)} %get-tuple-element.17), calls=%async_computation | async-start | bytes 524288 | tf_op jit(solution)/shard_map/all_to_all | solution.py:235
  18.4 8.0 %collective-permute-start.1 = (f32[2,6,8,128]{3,2,1,0:T(8,128)S(1)}, f32[2,6,8,128]{3,2,1,0:T(8,128)S(1)}, u32[]{:S(2)}, u32[]{:S(2)}) collective-permute-start(f32[2,6,8,128]{3,2,1,0:T(8,128)S(1)} %get-tuple-element.13), channel_id=1, source_target_pairs={{0,16},{8,24},{16,32},{24,40},{32,48},{40,56},{48,64},{56,72},{64,... | collective-permute-start | bytes 147464 | tf_op jit(solution)/shard_map/ppermute | solution.py:244
  21.6 4.7 %collective-permute-start = (bf16[6,8,128]{2,1,0:T(8,128)(2,1)S(1)}, bf16[6,8,128]{2,1,0:T(8,128)(2,1)S(1)}, u32[]{:S(2)}, u32[]{:S(2)}) collective-permute-start(bf16[6,8,128]{2,1,0:T(8,128)(2,1)S(1)} %get-tuple-element.12.rim), channel_id=1, source_target_pairs={{16,0},{24,8},{32,16},{40,24},{48,32},{56,40},{64,48},{72,56},{80,... | collective-permute-start | bytes 36872 | tf_op jit(solution)/shard_map/ppermute | solution.py:243
  26.9 10.4 %collective-permute-start.3 = (f32[3,6,8,128]{3,2,1,0:T(8,128)S(1)}, f32[3,6,8,128]{3,2,1,0:T(8,128)S(1)}, u32[]{:S(2)}, u32[]{:S(2)}) collective-permute-start(f32[3,6,8,128]{3,2,1,0:T(8,128)S(1)} %relay.1), channel_id=1, source_target_pairs={{0,8},{8,0},{16,24},{24,16},{32,40},{40,32},{48,56},{56,48},{64,72... | collective-permute-start | bytes 221192 | tf_op jit(solution)/shard_map/ppermute | solution.py:249
  30.9 6.4 %collective-permute-start.2 = (f32[6,8,128]{2,1,0:T(8,128)S(1)}, f32[6,8,128]{2,1,0:T(8,128)S(1)}, u32[]{:S(2)}, u32[]{:S(2)}) collective-permute-start(f32[6,8,128]{2,1,0:T(8,128)S(1)} %get-tuple-element.14), channel_id=1, source_target_pairs={{8,32},{24,48},{40,64},{56,80},{72,96},{88,112},{104,128},{120,144... | collective-permute-start | bytes 73736 | tf_op jit(solution)/shard_map/ppermute | solution.py:245

commit v4 on v3

--- a/solution.py
+++ b/solution.py
@@ -11,8 +11,7 @@
 RIM = 6
 PIECES = (16, 32, 32, 48)
 SMALL_VMEM = 8 << 20
-BLOCKS_STAY = 50 << 20
-FIRST_VMEM = 53 << 20
+BLOCKS_STAY = 16 << 20
 
 
 resid_eta = 0.001
@@ -20,8 +19,11 @@
 VM = pl.BlockSpec(memory_space=pltpu.VMEM)
 SM = pl.BlockSpec(memory_space=pltpu.SMEM)
 FAR = pl.BlockSpec(memory_space=pl.ANY)
-ROW, COL, CORE = 0, 1, 2
 TRANSPOSED = (((1,), (1,)), ((), ()))
+
+
+def in_hbm(array):
+    return pltpu.with_memory_space_constraint(array, pltpu.HBM)
 
 
 def call(kernel, name, in_specs, outs, scratch, vmem, flops, moved):
@@ -57,27 +59,42 @@
     return copies
 
 
-def each_pair(first, count, where, take, give, top, bottom, total, product):
+def each_pair(first, count, live, take, give, top, bottom, total, product):
     vecs = total.shape[1]
+    none_from, none_to = top.shape[0] - 1, total.shape[0] - 1
+
+    def taken(s):
+        return jnp.where(s < live, take(s), none_from)
+
     results = []
     for s in range(first, first + count, 2):
-        x = jnp.concatenate([top[where[take, s]], bottom[where[take, s + 1]]], axis=1)
-        y = product(x, s)
+        y = product(jnp.concatenate([top[taken(s)], bottom[taken(s + 1)]], axis=1), s)
         results += [y[:vecs], y[vecs:]]
     for k in range(count):
-        total[where[give, first + k]] += results[k]
+        s = first + k
+        total[jnp.where(s < live, give(s), none_to)] += results[k]
 
 
 def backward_kernel(
-    where, vectors, damage, upper_far, everyones, blocks, rim, own, one, chips, swap,
-    upper, total, top, bottom, sems
+    rows_far, cols_far, live_far, vectors_far, damage_far, upper_far, everyones, blocks, rim, own,
+    one, chips, swap, rows, cols, live, vectors, damage, upper, total, top, bottom, sems, few_sems
 ):
     here = own.shape[0]
     size = upper.shape[1]
+    few = [
+        pltpu.make_async_copy(source, target, few_sems.at[i])
+        for i, (source, target) in enumerate(
+            ((vectors_far, vectors), (damage_far, damage), (rows_far, rows), (cols_far, cols),
+             (live_far, live))
+        )
+    ]
     copies = streamed(upper_far, upper, sems)
-    for copy in copies:
+    for copy in few + copies:
         copy.start()
+    mine = lax.axis_index("rows")
     total[...] = jnp.zeros_like(total)
+    for copy in few:
+        copy.wait()
     soft = softness(damage[...])
     for b in range(here):
         cut = slice(b * size, (b + 1) * size)
@@ -97,11 +114,14 @@
     first = 0
     for copy, count in zip(copies, PIECES):
         copy.wait()
-        each_pair(first, count, where, ROW, COL, top, bottom, total, product)
+        each_pair(
+            first, count, live[0], lambda s: rows[s] - mine * here, lambda s: cols[s] - mine * here,
+            top, bottom, total, product,
+        )
         first += count
     own[...] = total[:here]
     one[...] = total[here : here + RIM]
-    second_core = where[CORE, 0]
+    second_core = lax.rem(mine, 2)
     other = jnp.where(second_core == 1, here, 3 * here)
     chips[0] = total[2 * here : 2 * here + RIM]
     chips[1] = total[pl.ds(other, RIM)]
@@ -110,14 +130,16 @@
     )
 
 
-def relay_kernel(where, rim, far, one, chips, out):
+def relay_kernel(rim, far, one, chips, swap, out, back):
+    first_core = lax.rem(lax.axis_index("rows"), 2) == 0
     out[0] = rim[...].astype(jnp.float32)
     out[1] = far[...].astype(jnp.float32)
-    out[2] = chips[1] + jnp.where(where[CORE, 0] == 1, 0.0, one[...])
+    out[2] = chips[1] + jnp.where(first_core, one[...], 0.0)
+    back[...] = chips[0] + jnp.where(first_core, swap[...], 0.0)
 
 
 def forward_kernel(
-    where, blocks, far, chips, swap, mate, own, diag, every, damage, upper_far,
+    rows, cols, live, blocks, far, back, swap, mate, own, diag, every, damage, upper_far,
     product_out, copies_out, upper, total, top, bottom, sems
 ):
     here = own.shape[0]
@@ -126,7 +148,8 @@
     copies = streamed(upper_far, upper, sems)
     for copy in copies:
         copy.start()
-    second_core = where[CORE, 0] == 1
+    mine = lax.axis_index("rows")
+    second_core = lax.rem(mine, 2) == 1
     for b in range(here):
         put_halves(top, bottom, b, blocks[b].astype(jnp.float32))
     for b in range(RIM):
@@ -138,7 +161,7 @@
         total[b] = own[b] + lax.dot_general(
             blocks[b], diag[b], TRANSPOSED, preferred_element_type=jnp.float32
         )
-    total[:RIM] += chips[0] + mate[2] + jnp.where(second_core, 0.0, swap[...])
+    total[:RIM] += back[...] + mate[2]
 
     def product(x, s):
         pair = jnp.concatenate([upper[s], upper[s + 1]], axis=1)
@@ -147,7 +170,10 @@
     first = 0
     for copy, count in zip(copies, PIECES):
         copy.wait()
-        each_pair(first, count, where, COL, ROW, top, bottom, total, product)
+        each_pair(
+            first, count, live[0], lambda s: cols[s] - mine * here, lambda s: rows[s] - mine * here,
+            top, bottom, total, product,
+        )
         first += count
     soft = softness(damage[...])
     gram = jnp.zeros((2 * vecs, every.shape[0]), jnp.float32)
@@ -175,35 +201,43 @@
     out[half:] = packed[:, columns:]
 
 
-def backward(groups, where, vectors, damage, upper):
+def backward(groups, rows, cols, live, vectors, damage, upper):
     f32, bf16 = jnp.float32, jnp.bfloat16
     vecs = vectors.shape[0]
     here, size = damage.shape
     slots = upper.shape[0]
     rim = (RIM, vecs, size)
     return call(
-        backward_kernel, "backward", [SM, VM, VM, FAR],
+        backward_kernel, "backward", [FAR] * 6,
         [
             ((groups, vecs, here * size), bf16), ((here, vecs, size), bf16), (rim, bf16),
             ((here, vecs, size), f32), (rim, f32), ((2,) + rim, f32), (rim, f32),
         ],
         [
+            pltpu.SMEM(rows.shape, rows.dtype),
+            pltpu.SMEM(cols.shape, cols.dtype),
+            pltpu.SMEM(live.shape, live.dtype),
+            pltpu.VMEM(vectors.shape, f32),
+            pltpu.VMEM(damage.shape, f32),
             pltpu.VMEM(upper.shape, bf16),
             pltpu.VMEM((REACH * here + 1, vecs, size), f32),
             pltpu.VMEM((here + 1, 2 * vecs, size), bf16),
             pltpu.VMEM((here + 1, 2 * vecs, size), bf16),
             pltpu.SemaphoreType.DMA((len(PIECES),)),
+            pltpu.SemaphoreType.DMA((5,)),
         ],
-        FIRST_VMEM, 2 * slots * vecs * size * size, 2 * slots * size * size,
-    )(where, vectors, damage, upper)
-
-
-def forward(owners, where, blocks, far, chips, swap, mate, own, diag, every, damage, upper):
+        BLOCKS_STAY, 2 * slots * vecs * size * size, 2 * slots * size * size,
+    )(in_hbm(rows), in_hbm(cols), live, in_hbm(vectors), in_hbm(damage), in_hbm(upper))
+
+
+def forward(
+    owners, rows, cols, live, blocks, far, back, swap, mate, own, diag, every, damage, upper
+):
     f32, bf16 = jnp.float32, jnp.bfloat16
     here, vecs, size = blocks.shape
     slots = upper.shape[0]
     return call(
-        forward_kernel, "forward", [SM] + [VM] * 9 + [FAR],
+        forward_kernel, "forward", [SM] * 3 + [VM] * 9 + [FAR],
         [((vecs, here * size), f32), ((owners, vecs // 2, 2 * every.shape[0]), f32)],
         [
             pltpu.VMEM(upper.shape, bf16),
@@ -213,7 +247,7 @@
             pltpu.SemaphoreType.DMA((len(PIECES),)),
         ],
         BLOCKS_STAY, 2 * slots * vecs * size * size, 2 * slots * size * size,
-    )(where, blocks, far, chips, swap, mate, own, diag, every, damage, upper)
+    )(rows, cols, live, blocks, far, back, swap, mate, own, diag, every, damage, in_hbm(upper))
 
 
 def on_device(vectors, damage, diag_blocks, upper_blocks, block_rows, block_cols, live_slots):
@@ -221,16 +255,11 @@
     vecs, width = vectors.shape
     here, size = diag_blocks.shape[:2]
     owners, groups = lax.axis_size("rows"), lax.axis_size("vec")
-    mine = lax.axis_index("rows").astype(jnp.int32)
-    stored = jnp.arange(upper_blocks.shape[0]) < live_slots[0]
-    rows = jnp.where(stored, block_rows - mine * here, here)
-    cols = jnp.where(stored, block_cols - mine * here, REACH * here)
-    where = jnp.stack([rows, cols, jnp.full_like(rows, mine & 1)])
     damage = damage.reshape(here, size)
     rim = (RIM, vecs, size)
 
     copies, blocks, edge, own, one, chips, swap = backward(
-        groups, where, vectors, damage, upper_blocks
+        groups, block_rows, block_cols, live_slots, vectors, damage, upper_blocks
     )
     every = lax.all_to_all(copies, "vec", 0, 0).reshape(groups * vecs, width)
 
@@ -243,13 +272,14 @@
     far = lax.ppermute(edge, "rows", down)
     chips = lax.ppermute(chips, "rows", up)
     swap = lax.ppermute(swap, "rows", across)
-    (mate,) = call(
-        relay_kernel, "relay", [SM] + [VM] * 4, [((3,) + rim, f32)], [], SMALL_VMEM, 0, 8 * size,
-    )(where, edge, far, one, chips)
+    mate, back = call(
+        relay_kernel, "relay", [VM] * 5, [((3,) + rim, f32), (rim, f32)], [], SMALL_VMEM,
+        0, 8 * size,
+    )(edge, far, one, chips, swap)
     mate = lax.ppermute(mate, "rows", mates)
 
     product, partials = forward(
-        owners, where, blocks, far, chips, swap, mate, own, diag_blocks,
+        owners, block_rows, block_cols, live_slots, blocks, far, back, swap, mate, own, diag_blocks,
         every, damage, upper_blocks,
     )
     partials = lax.all_to_all(partials, "rows", 0, 0)

time: 64.4 us -> 57 us (0.89)
  blocking collectives: 21.5 us -> 18.7 us
  starting transfers between devices: 24.3 us -> 22.6 us
  local copies, waits for them, and re-layouts: 1.62 us -> 0.02 us
  Pallas kernels: 9.43 us -> 8.38 us
  other arithmetic: 0.75 us -> 0 us
    all_to_all x1, blocking collectives: 21.5 us -> 18.7 us  [on_device(): partials = lax.all_to_all(partials, 'rows', 0, 0)]
    ppermute x1, starting transfers between devices: 3.98 us -> 1.92 us  [on_device(): mate = lax.ppermute(mate, 'rows', mates)]
    unnamed x8, local copies, waits for them, and re-layouts: 1.54 us -> 0.02 us
    ppermute x1, waiting for transfers between devices: 1.5 us -> 0.01 us  [on_device(): swap = lax.ppermute(swap, 'rows', across)]
    ppermute x1, waiting for transfers between devices: 0.01 us -> 1.23 us  [on_device(): mate = lax.ppermute(mate, 'rows', mates)]
    pallas_call x3, Pallas kernels: 8.71 us -> 7.65 us  [the longest x1 4.31 us: forward(): call(forward_kernel, 'forward', [SM] * 3 + [VM] * 9 + [FAR], [((vecs, her...]
    ppermute x1, waiting for transfers between devices: 3.43 us -> 4.23 us  [on_device(): far = lax.ppermute(edge, 'rows', down)]
    another operation x2 -> x0, other arithmetic: 0.75 us -> none  [on_device(): where = jnp.stack([rows, cols, jnp.full_like(rows, mine & 1)])]
  transfers between devices with their start and end apart: 5 -> 5, of which waited for: 2 -> 2; matrix products, arithmetic and copies ran while one was open for 0% -> 0% of each run, Pallas kernels for 1% -> 0%
where the time goes in v4:
time: 57 us; the launch traced here: 56.6 us
  starting transfers between devices  22.6 us (40%)
  blocking collectives  18.7 us (33%)
  Pallas kernels  8.38 us (15%)
  waiting for transfers between devices  5.47 us (10%)
  between operations  1.45 us (3%)
    all_to_all x1, blocking collectives, on_device(): partials = lax.all_to_all(partials, 'rows', 0, 0)  18.7 us
    all_to_all x1, starting transfers between devices, on_device(): every = lax.all_to_all(copies, 'vec', 0, 0).reshape(groups * vecs, width)  10.9 us
    ppermute x1, starting transfers between devices, on_device(): swap = lax.ppermute(swap, 'rows', across)  5.31 us
    pallas_call x1, Pallas kernels, forward(): call(forward_kernel, 'forward', [SM] * 3 + [VM] * 9 + [FAR], [((vecs, her...  4.31 us
    ppermute x1, waiting for transfers between devices, on_device(): far = lax.ppermute(edge, 'rows', down)  4.23 us
    pallas_call x1, Pallas kernels, backward(): call(backward_kernel, 'backward', [FAR] * 6, [((groups, vecs, here * size...  3.33 us
    ppermute x1, starting transfers between devices, on_device(): chips = lax.ppermute(chips, 'rows', up)  3.22 us
    ppermute x1, starting transfers between devices, on_device(): mate = lax.ppermute(mate, 'rows', mates)  1.92 us
  transfers between devices with their start and end apart: 5, of which 2 were waited for; matrix products, arithmetic and copies ran while one was open for 0% of the time, Pallas kernels for 0%

profile of v4, /device:TPU:1, one launch (start us, length us, event | category | flops | bytes accessed | tf_op | source)
XLA Modules:
  0.0 56.6 jit_solution(9769075767329806872)
XLA Ops:
  0.6 0.0 copy-start.3
  0.6 0.0 copy-start.2
  0.7 0.0 copy-start.1
  0.7 0.0 copy-start
  1.4 3.3 %backward.1 = (bf16[8,8,2048]{2,1,0:T(8,128)(2,1)}, bf16[16,8,128]{2,1,0:T(8,128)(2,1)S(1)}, bf16[6,8,128]{2,1,0:T(8,128)(2,1)S(1)}, f32[16,8,128]{2,1,0:T(8,128...) custom-call(s32[128]{0:T(128)} %rows.1, s32[128]{0:T(128)} %cols.1, ...), custom_call_target="tpu_custom_call" | custom-call | flops 33554432 | bytes 4194304 | tf_op jit(solution)/shard_map/backward/pallas_call | solution.py:210
  4.7 10.9 %all-to-all-start = ((bf16[8,8,2048]{2,1,0:T(8,128)(2,1)}), bf16[8,8,2048]{2,1,0:T(8,128)(2,1)S(1)}, u32[]{:S(2)}, u32[]{:S(2)}) async-start(bf16[8,8,2048]{2,1,0:T(8,128)(2,1)} %get-tuple-element.21), calls=%async_computation | async-start | bytes 524288 | tf_op jit(solution)/shard_map/all_to_all | solution.py:264
  15.6 3.2 %collective-permute-start.1 = (f32[2,6,8,128]{3,2,1,0:T(8,128)S(1)}, f32[2,6,8,128]{3,2,1,0:T(8,128)S(1)}, u32[]{:S(2)}, u32[]{:S(2)}) collective-permute-start(f32[2,6,8,128]{3,2,1,0:T(8,128)S(1)} %get-tuple-element.16), channel_id=1, source_target_pairs={{0,16},{8,24},{16,32},{24,40},{32,48},{40,56},{48,64},{56,72},{64,... | collective-permute-start | bytes 147464 | tf_op jit(solution)/shard_map/ppermute | solution.py:273
  18.8 5.3 %collective-permute-start.2 = (f32[6,8,128]{2,1,0:T(8,128)S(1)}, f32[6,8,128]{2,1,0:T(8,128)S(1)}, u32[]{:S(2)}, u32[]{:S(2)}) collective-permute-start(f32[6,8,128]{2,1,0:T(8,128)S(1)} %get-tuple-element.17), channel_id=1, source_target_pairs={{8,32},{24,48},{40,64},{56,80},{72,96},{88,112},{104,128},{120,144... | collective-permute-start | bytes 73736 | tf_op jit(solution)/shard_map/ppermute | solution.py:274
  24.1 1.3 %collective-permute-start = (bf16[6,8,128]{2,1,0:T(8,128)(2,1)S(1)}, bf16[6,8,128]{2,1,0:T(8,128)(2,1)S(1)}, u32[]{:S(2)}, u32[]{:S(2)}) collective-permute-start(bf16[6,8,128]{2,1,0:T(8,128)(2,1)S(1)} %get-tuple-element.14.rim), channel_id=1, source_target_pairs={{16,0},{24,8},{32,16},{40,24},{48,32},{56,40},{64,48},{72,56},{80,... | collective-permute-start | bytes 36872 | tf_op jit(solution)/shard_map/ppermute | solution.py:272
  25.4 4.2 %collective-permute-done.far = bf16[6,8,128]{2,1,0:T(8,128)(2,1)S(1)} collective-permute-done((bf16[6,8,128]{2,1,0:T(8,128)(2,1)S(1)}, bf16[6,8,128]{2,1,0:T(8,128)(2,1)S(1)}, u32[]{:S(2)}, u32[]{:S(2)}) %collective-permute-start) | collective-permute-done | bytes 12320 | tf_op jit(solution)/shard_map/ppermute | solution.py:272
  29.7 0.0 collective-permute-done.2.swap
  29.7 0.0 collective-permute-done.1.chips
  29.7 1.9 %collective-permute-start.3 = (f32[3,6,8,128]{3,2,1,0:T(8,128)S(1)}, f32[3,6,8,128]{3,2,1,0:T(8,128)S(1)}, u32[]{:S(2)}, u32[]{:S(2)}) collective-permute-start(f32[3,6,8,128]{3,2,1,0:T(8,128)S(1)} %get-tuple-element.19), channel_id=1, source_target_pairs={{0,8},{8,0},{16,24},{24,16},{32,40},{40,32},{48,56},{56,48},{64,72... | collective-permute-start | bytes 221192 | tf_op jit(solution)/shard_map/ppermute | solution.py:279
  31.6 1.2 %collective-permute-done.3.mate = f32[3,6,8,128]{3,2,1,0:T(8,128)S(1)} collective-permute-done((f32[3,6,8,128]{3,2,1,0:T(8,128)S(1)}, f32[3,6,8,128]{3,2,1,0:T(8,128)S(1)}, u32[]{:S(2)}, u32[]{:S(2)}) %collective-permute-start.3) | collective-permute-done | bytes 73760 | tf_op jit(solution)/shard_map/ppermute | solution.py:279
  32.9 0.0 all-to-all-done
  32.9 0.0 copy-done.3
  32.9 0.0 copy-done.2
  32.9 0.0 copy-done.1
  32.9 0.0 copy-done
  32.9 4.3 %forward.1 = (f32[8,2048]{1,0:T(8,128)}, f32[64,4,128]{2,1,0:T(4,128)S(1)}) custom-call(s32[128]{0:T(128)S(1)} %copy-done.2, s32[128]{0:T(128)S(1)} %copy-done.3, s32[1]{0:T(128)S(6)} %copy.9.live_far.live, bf16[16,8,128]{2,1,0:T(8,128)(2,1)S(1)} %get-tuple-element.13.blocks, bf16[6,8,128]{2,1,0:T(8,128)(2,1)S(1)} %collective-permute-done.far, ...), custom_call_target="tpu_custom_call" | custom-call | flops 33554432 | bytes 4194304 | tf_op jit(solution)/shard_map/forward/pallas_call | solution.py:239
  37.2 18.7 %all_to_all.10.parts = f32[64,4,128]{2,1,0:T(4,128)S(1)} all-to-all(f32[64,4,128]{2,1,0:T(4,128)S(1)} %get-tuple-element.23), channel_id=1, replica_groups=mesh['rows'=64,'vec'=8] {'rows'}, dimensions={0} | all-to-all | bytes 262144 | tf_op jit(solution)/shard_map/all_to_all | solution.py:285
  55.9 0.7 %sum.1 = f32[8,64]{1,0:T(8,128)} custom-call(f32[64,4,128]{2,1,0:T(4,128)S(1)} %all_to_all.10.parts), custom_call_target="tpu_custom_call" | custom-call | bytes 131072 | tf_op jit(solution)/shard_map/sum/pallas_call | solution.py:286
  (1 shorter events, 0.0 us)
Async XLA Ops:
  0.6 32.2 %copy-start.3 = (s32[128]{0:T(128)S(1)}, s32[128]{0:T(128)}, u32[]{:S(2)}) copy-start(s32[128]{0:T(128)} %cols.1) | copy-start | bytes 1540
  0.6 32.2 %copy-start.2 = (s32[128]{0:T(128)S(1)}, s32[128]{0:T(128)}, u32[]{:S(2)}) copy-start(s32[128]{0:T(128)} %rows.1) | copy-start | bytes 1540
  0.7 32.2 %copy-start.1 = (f32[2048]{0:T(1024)S(1)}, f32[2048]{0:T(1024)}, u32[]{:S(2)}) copy-start(f32[2048]{0:T(1024)} %param.8) | copy-start | bytes 24580
  0.7 32.2 %copy-start = (bf16[16,128,128]{2,1,0:T(8,128)(2,1)S(1)}, bf16[16,128,128]{2,1,0:T(8,128)(2,1)}, u32[]{:S(2)}) copy-start(bf16[16,128,128]{2,1,0:T(8,128)(2,1)} %diag.1) | copy-start | bytes 1572868
  4.7 28.1 %all-to-all-start = ((bf16[8,8,2048]{2,1,0:T(8,128)(2,1)}), bf16[8,8,2048]{2,1,0:T(8,128)(2,1)S(1)}, u32[]{:S(2)}, u32[]{:S(2)}) async-start(bf16[8,8,2048]{2,1,0:T(8,128)(2,1)} %get-tuple-element.21), calls=%async_computation | async-start | bytes 524288 | tf_op jit(solution)/shard_map/all_to_all | solution.py:264
  15.6 14.1 %collective-permute-start.1 = (f32[2,6,8,128]{3,2,1,0:T(8,128)S(1)}, f32[2,6,8,128]{3,2,1,0:T(8,128)S(1)}, u32[]{:S(2)}, u32[]{:S(2)}) collective-permute-start(f32[2,6,8,128]{3,2,1,0:T(8,128)S(1)} %get-tuple-element.16), channel_id=1, source_target_pairs={{0,16},{8,24},{16,32},{24,40},{32,48},{40,56},{48,64},{56,72},{64,... | collective-permute-start | bytes 147464 | tf_op jit(solution)/shard_map/ppermute | solution.py:273
  18.8 10.8 %collective-permute-start.2 = (f32[6,8,128]{2,1,0:T(8,128)S(1)}, f32[6,8,128]{2,1,0:T(8,128)S(1)}, u32[]{:S(2)}, u32[]{:S(2)}) collective-permute-start(f32[6,8,128]{2,1,0:T(8,128)S(1)} %get-tuple-element.17), channel_id=1, source_target_pairs={{8,32},{24,48},{40,64},{56,80},{72,96},{88,112},{104,128},{120,144... | collective-permute-start | bytes 73736 | tf_op jit(solution)/shard_map/ppermute | solution.py:274
  24.1 5.5 %collective-permute-start = (bf16[6,8,128]{2,1,0:T(8,128)(2,1)S(1)}, bf16[6,8,128]{2,1,0:T(8,128)(2,1)S(1)}, u32[]{:S(2)}, u32[]{:S(2)}) collective-permute-start(bf16[6,8,128]{2,1,0:T(8,128)(2,1)S(1)} %get-tuple-element.14.rim), channel_id=1, source_target_pairs={{16,0},{24,8},{32,16},{40,24},{48,32},{56,40},{64,48},{72,56},{80,... | collective-permute-start | bytes 36872 | tf_op jit(solution)/shard_map/ppermute | solution.py:272
  29.7 3.2 %collective-permute-start.3 = (f32[3,6,8,128]{3,2,1,0:T(8,128)S(1)}, f32[3,6,8,128]{3,2,1,0:T(8,128)S(1)}, u32[]{:S(2)}, u32[]{:S(2)}) collective-permute-start(f32[3,6,8,128]{3,2,1,0:T(8,128)S(1)} %get-tuple-element.19), channel_id=1, source_target_pairs={{0,8},{8,0},{16,24},{24,16},{32,40},{40,32},{48,56},{56,48},{64,72... | collective-permute-start | bytes 221192 | tf_op jit(solution)/shard_map/ppermute | solution.py:279

commit v5 on v4

--- a/solution.py
+++ b/solution.py
@@ -9,9 +9,10 @@
 
 REACH = 4
 RIM = 6
-PIECES = (16, 32, 32, 48)
+PIECES = (16, 48, 32, 32)
+KEPT = 64
+LATE_PIECES = (64,)
 SMALL_VMEM = 8 << 20
-BLOCKS_STAY = 16 << 20
 
 
 resid_eta = 0.001
@@ -26,12 +27,12 @@
     return pltpu.with_memory_space_constraint(array, pltpu.HBM)
 
 
-def call(kernel, name, in_specs, outs, scratch, vmem, flops, moved):
+def call(kernel, name, in_specs, outs, scratch, vmem, flops, moved, first_far=False):
     return pl.pallas_call(
         kernel,
         name=name,
         in_specs=in_specs,
-        out_specs=[VM] * len(outs),
+        out_specs=[FAR if first_far and i == 0 else VM for i in range(len(outs))],
         out_shape=[jax.ShapeDtypeStruct(shape, dtype) for shape, dtype in outs],
         scratch_shapes=scratch,
         compiler_params=pltpu.CompilerParams(vmem_limit_bytes=vmem),
@@ -49,14 +50,25 @@
     bottom[at] = jnp.concatenate([z, x], 0).astype(jnp.bfloat16)
 
 
-def streamed(upper_far, upper, sems):
-    copies, first = [], 0
-    for i, count in enumerate(PIECES):
-        cut = pl.ds(first, count)
-        copies.append(pltpu.make_async_copy(upper_far.at[cut], upper.at[cut], sems.at[i]))
+def streamed(upper_far, parts, pieces, sems):
+    copies = []
+    for i, (first, count) in enumerate(pieces):
+        start, buffer = [part for part in parts if part[0] <= first][-1]
+        copies.append(
+            pltpu.make_async_copy(
+                upper_far.at[pl.ds(first, count)], buffer.at[pl.ds(first - start, count)], sems.at[i]
+            )
+        )
+    return copies
+
+
+def pieces_of(first, slots, sizes):
+    pieces = []
+    for count in sizes:
+        pieces.append((first, count))
         first += count
-    assert first == upper.shape[0]
-    return copies
+    assert first == slots
+    return pieces
 
 
 def each_pair(first, count, live, take, give, top, bottom, total, product):
@@ -76,11 +88,13 @@
 
 
 def backward_kernel(
-    rows_far, cols_far, live_far, vectors_far, damage_far, upper_far, everyones, blocks, rim, own,
-    one, chips, swap, rows, cols, live, vectors, damage, upper, total, top, bottom, sems, few_sems
+    rows_far, cols_far, live_far, vectors_far, damage_far, upper_far, everyones_far, blocks, rim,
+    own, one, chips, swap, near, rows, cols, live, vectors, damage, flat, rest, total, top, bottom,
+    sems, few_sems, out_sems
 ):
     here = own.shape[0]
-    size = upper.shape[1]
+    size = near.shape[1]
+    kept = near.shape[0]
     few = [
         pltpu.make_async_copy(source, target, few_sems.at[i])
         for i, (source, target) in enumerate(
@@ -88,7 +102,8 @@
              (live_far, live))
         )
     ]
-    copies = streamed(upper_far, upper, sems)
+    pieces = pieces_of(0, upper_far.shape[0], PIECES)
+    copies = streamed(upper_far, ((0, near), (kept, rest)), pieces, sems)
     for copy in few + copies:
         copy.start()
     mine = lax.axis_index("rows")
@@ -102,32 +117,38 @@
         blocks[b] = scaled
         if b < RIM:
             rim[b] = scaled
-        for i in range(everyones.shape[0]):
-            everyones[i, :, cut] = scaled
+        flat[:, cut] = scaled
         put_halves(top, bottom, b, scaled.astype(jnp.float32))
     put_halves(top, bottom, here, jnp.zeros(total.shape[1:], jnp.float32))
+    gifts = [
+        pltpu.make_async_copy(flat, everyones_far.at[i], out_sems.at[i])
+        for i in range(everyones_far.shape[0])
+    ]
+    for gift in gifts:
+        gift.start()
 
     def product(x, s):
-        pair = upper[pl.ds(s, 2)].reshape(2 * size, size)
-        return jnp.dot(x, pair, preferred_element_type=jnp.float32)
-
-    first = 0
-    for copy, count in zip(copies, PIECES):
+        blocks_of = near[pl.ds(s, 2)] if s < kept else rest[pl.ds(s - kept, 2)]
+        return jnp.dot(x, blocks_of.reshape(2 * size, size), preferred_element_type=jnp.float32)
+
+    for copy, (first, count) in zip(copies, pieces):
         copy.wait()
         each_pair(
             first, count, live[0], lambda s: rows[s] - mine * here, lambda s: cols[s] - mine * here,
             top, bottom, total, product,
         )
-        first += count
     own[...] = total[:here]
     one[...] = total[here : here + RIM]
     second_core = lax.rem(mine, 2)
     other = jnp.where(second_core == 1, here, 3 * here)
     chips[0] = total[2 * here : 2 * here + RIM]
     chips[1] = total[pl.ds(other, RIM)]
-    swap[...] = jnp.where(
+    swap[:RIM] = jnp.where(
         second_core == 1, total[3 * here : 3 * here + RIM], blocks[:RIM].astype(jnp.float32)
     )
+    swap[RIM:] = jnp.zeros((swap.shape[0] - RIM,) + swap.shape[1:], jnp.float32)
+    for gift in gifts:
+        gift.wait()
 
 
 def relay_kernel(rim, far, one, chips, swap, out, back):
@@ -135,19 +156,20 @@
     out[0] = rim[...].astype(jnp.float32)
     out[1] = far[...].astype(jnp.float32)
     out[2] = chips[1] + jnp.where(first_core, one[...], 0.0)
-    back[...] = chips[0] + jnp.where(first_core, swap[...], 0.0)
+    back[...] = chips[0] + jnp.where(first_core, swap[:RIM], 0.0)
 
 
 def forward_kernel(
-    rows, cols, live, blocks, far, back, swap, mate, own, diag, every, damage, upper_far,
-    product_out, copies_out, upper, total, top, bottom, sems
+    rows, cols, live, blocks, far, back, swap, mate, own, diag, near, upper_far, raw, rest, total,
+    top, bottom, sems
 ):
     here = own.shape[0]
-    size = diag.shape[1]
-    vecs = blocks.shape[1]
-    copies = streamed(upper_far, upper, sems)
+    kept = near.shape[0]
+    pieces = pieces_of(kept, upper_far.shape[0], LATE_PIECES)
+    copies = streamed(upper_far, ((kept, rest),), pieces, sems)
     for copy in copies:
         copy.start()
+    vecs, size = blocks.shape[1:]
     mine = lax.axis_index("rows")
     second_core = lax.rem(mine, 2) == 1
     for b in range(here):
@@ -164,33 +186,42 @@
     total[:RIM] += back[...] + mate[2]
 
     def product(x, s):
-        pair = jnp.concatenate([upper[s], upper[s + 1]], axis=1)
-        return lax.dot_general(x, pair, TRANSPOSED, preferred_element_type=jnp.float32)
-
-    first = 0
-    for copy, count in zip(copies, PIECES):
-        copy.wait()
+        pair = (near[s], near[s + 1]) if s < kept else (rest[s - kept], rest[s - kept + 1])
+        return lax.dot_general(
+            x, jnp.concatenate(pair, axis=1), TRANSPOSED, preferred_element_type=jnp.float32
+        )
+
+    for copy, (first, count) in zip([None] + copies, [(0, kept)] + pieces):
+        if copy is not None:
+            copy.wait()
         each_pair(
             first, count, live[0], lambda s: cols[s] - mine * here, lambda s: rows[s] - mine * here,
             top, bottom, total, product,
         )
-        first += count
+    raw[...] = total[:here]
+
+
+def finish_kernel(raws, damage, every, product_far, copies_out, product, sem):
+    here, vecs, size = raws.shape
     soft = softness(damage[...])
+    for b in range(here):
+        product[:, b * size : (b + 1) * size] = raws[b] * soft[b : b + 1, :]
+    leave = pltpu.make_async_copy(product, product_far, sem)
+    leave.start()
     gram = jnp.zeros((2 * vecs, every.shape[0]), jnp.float32)
     for b in range(here):
-        raw = total[b]
-        cut = slice(b * size, (b + 1) * size)
-        product_out[:, cut] = raw * soft[b : b + 1, :]
+        raw = raws[b]
         high = raw.astype(jnp.bfloat16)
         low = (raw - high.astype(jnp.float32)).astype(jnp.bfloat16)
         gram += lax.dot_general(
-            jnp.concatenate([high, low], 0), every[:, cut], TRANSPOSED,
+            jnp.concatenate([high, low], 0), every[:, b * size : (b + 1) * size], TRANSPOSED,
             preferred_element_type=jnp.float32,
         )
     gram = gram[:vecs] + gram[vecs:]
     half = vecs // 2
     packed = jnp.concatenate([gram[:half], gram[half:]], axis=1)
     copies_out[...] = jnp.broadcast_to(packed[None], copies_out.shape)
+    leave.wait()
 
 
 def sum_kernel(scale, parts, out):
@@ -207,11 +238,13 @@
     here, size = damage.shape
     slots = upper.shape[0]
     rim = (RIM, vecs, size)
+    swapped = (2 * RIM + 2, vecs, size)
     return call(
         backward_kernel, "backward", [FAR] * 6,
         [
             ((groups, vecs, here * size), bf16), ((here, vecs, size), bf16), (rim, bf16),
-            ((here, vecs, size), f32), (rim, f32), ((2,) + rim, f32), (rim, f32),
+            ((here, vecs, size), f32), (rim, f32), ((2,) + rim, f32),
+            (swapped, f32), ((KEPT, size, size), bf16),
         ],
         [
             pltpu.SMEM(rows.shape, rows.dtype),
@@ -219,35 +252,34 @@
             pltpu.SMEM(live.shape, live.dtype),
             pltpu.VMEM(vectors.shape, f32),
             pltpu.VMEM(damage.shape, f32),
-            pltpu.VMEM(upper.shape, bf16),
+            pltpu.VMEM((vecs, here * size), bf16),
+            pltpu.VMEM((slots - KEPT, size, size), bf16),
             pltpu.VMEM((REACH * here + 1, vecs, size), f32),
             pltpu.VMEM((here + 1, 2 * vecs, size), bf16),
             pltpu.VMEM((here + 1, 2 * vecs, size), bf16),
             pltpu.SemaphoreType.DMA((len(PIECES),)),
             pltpu.SemaphoreType.DMA((5,)),
+            pltpu.SemaphoreType.DMA((groups,)),
         ],
-        BLOCKS_STAY, 2 * slots * vecs * size * size, 2 * slots * size * size,
+        SMALL_VMEM, 2 * slots * vecs * size * size, 2 * slots * size * size, True,
     )(in_hbm(rows), in_hbm(cols), live, in_hbm(vectors), in_hbm(damage), in_hbm(upper))
 
 
-def forward(
-    owners, rows, cols, live, blocks, far, back, swap, mate, own, diag, every, damage, upper
-):
+def forward(rows, cols, live, blocks, far, back, swap, mate, own, diag, near, upper):
     f32, bf16 = jnp.float32, jnp.bfloat16
     here, vecs, size = blocks.shape
     slots = upper.shape[0]
     return call(
-        forward_kernel, "forward", [SM] * 3 + [VM] * 9 + [FAR],
-        [((vecs, here * size), f32), ((owners, vecs // 2, 2 * every.shape[0]), f32)],
+        forward_kernel, "forward", [SM] * 3 + [VM] * 8 + [FAR], [((here, vecs, size), f32)],
         [
-            pltpu.VMEM(upper.shape, bf16),
+            pltpu.VMEM((slots - KEPT, size, size), bf16),
             pltpu.VMEM((here + 1, vecs, size), f32),
             pltpu.VMEM((REACH * here + 1, 2 * vecs, size), bf16),
             pltpu.VMEM((REACH * here + 1, 2 * vecs, size), bf16),
-            pltpu.SemaphoreType.DMA((len(PIECES),)),
+            pltpu.SemaphoreType.DMA((len(LATE_PIECES),)),
         ],
-        BLOCKS_STAY, 2 * slots * vecs * size * size, 2 * slots * size * size,
-    )(rows, cols, live, blocks, far, back, swap, mate, own, diag, every, damage, in_hbm(upper))
+        SMALL_VMEM, 2 * slots * vecs * size * size, 2 * slots * size * size,
+    )(rows, cols, live, blocks, far, back, swap, mate, own, diag, near, in_hbm(upper))
 
 
 def on_device(vectors, damage, diag_blocks, upper_blocks, block_rows, block_cols, live_slots):
@@ -258,7 +290,7 @@
     damage = damage.reshape(here, size)
     rim = (RIM, vecs, size)
 
-    copies, blocks, edge, own, one, chips, swap = backward(
+    copies, blocks, edge, own, one, chips, swap, near = backward(
         groups, block_rows, block_cols, live_slots, vectors, damage, upper_blocks
     )
     every = lax.all_to_all(copies, "vec", 0, 0).reshape(groups * vecs, width)
@@ -278,10 +310,16 @@
     )(edge, far, one, chips, swap)
     mate = lax.ppermute(mate, "rows", mates)
 
-    product, partials = forward(
-        owners, block_rows, block_cols, live_slots, blocks, far, back, swap, mate, own, diag_blocks,
-        every, damage, upper_blocks,
-    )
+    (raw,) = forward(
+        block_rows, block_cols, live_slots, blocks, far, back, swap, mate, own, diag_blocks, near,
+        upper_blocks,
+    )
+    product, partials = call(
+        finish_kernel, "finish", [VM] * 3,
+        [((vecs, width), f32), ((owners, vecs // 2, 2 * groups * vecs), f32)],
+        [pltpu.VMEM((vecs, width), f32), pltpu.SemaphoreType.DMA(())],
+        SMALL_VMEM, 0, 8 * vecs * width, True,
+    )(raw, damage, every)
     partials = lax.all_to_all(partials, "rows", 0, 0)
     (projected,) = call(
         functools.partial(sum_kernel, 1.0 / (width * owners)), "sum", [VM],

time: 57 us -> 58.5 us (1.026)
  blocking collectives: 18.7 us -> 20.8 us
    all_to_all x1, blocking collectives: 18.7 us -> 20.8 us  [on_device(): partials = lax.all_to_all(partials, 'rows', 0, 0)]
    pallas_call x1 -> x2, Pallas kernels: 4.31 us -> 4.5 us  [the longest x1 3.73 us: forward(): call(forward_kernel, 'forward', [SM] * 3 + [VM] * 8 + [FAR], [((here, vec...]
  transfers between devices with their start and end apart: 5 -> 5, of which waited for: 2 -> 2; matrix products, arithmetic and copies ran while one was open for 0% -> 0% of each run, Pallas kernels for 0% -> 6%
where the time goes in v5:
time: 58.5 us; the launch traced here: 58.1 us
  starting transfers between devices  22.3 us (38%)
  blocking collectives  20.8 us (36%)
  Pallas kernels  8.11 us (14%)
  waiting for transfers between devices  5.41 us (9%)
  between operations  1.45 us (2%)
    all_to_all x1, blocking collectives, on_device(): partials = lax.all_to_all(partials, 'rows', 0, 0)  20.8 us
    all_to_all x1, starting transfers between devices, on_device(): every = lax.all_to_all(copies, 'vec', 0, 0).reshape(groups * vecs, width)  10.9 us
    ppermute x1, starting transfers between devices, on_device(): swap = lax.ppermute(swap, 'rows', across)  5.03 us
    ppermute x1, waiting for transfers between devices, on_device(): far = lax.ppermute(edge, 'rows', down)  4.17 us
    pallas_call x1, Pallas kernels, forward(): call(forward_kernel, 'forward', [SM] * 3 + [VM] * 8 + [FAR], [((here, vec...  3.73 us
    ppermute x1, starting transfers between devices, on_device(): chips = lax.ppermute(chips, 'rows', up)  3.2 us
    pallas_call x1, Pallas kernels, backward(): call(backward_kernel, 'backward', [FAR] * 6, [((groups, vecs, here * size...  2.86 us
    ppermute x1, starting transfers between devices, on_device(): mate = lax.ppermute(mate, 'rows', mates)  1.92 us
  transfers between devices with their start and end apart: 5, of which 2 were waited for; matrix products, arithmetic and copies ran while one was open for 0% of the time, Pallas kernels for 6%

profile of v5, /device:TPU:1, one launch (start us, length us, event | category | flops | bytes accessed | tf_op | source)
XLA Modules:
  0.0 58.1 jit_solution(14127076260965155291)
XLA Ops:
  0.6 0.0 copy-start.2
  0.6 0.0 copy-start.3
  0.7 0.0 copy-start
  1.4 2.9 %backward.1 = (bf16[8,8,2048]{2,1,0:T(8,128)(2,1)}, bf16[16,8,128]{2,1,0:T(8,128)(2,1)S(1)}, bf16[6,8,128]{2,1,0:T(8,128)(2,1)S(1)}, f32[16,8,128]{2,1,0:T(8,128...) custom-call(s32[128]{0:T(128)} %rows.1, s32[128]{0:T(128)} %cols.1, ...), custom_call_target="tpu_custom_call" | custom-call | flops 33554432 | bytes 4194304 | tf_op jit(solution)/shard_map/backward/pallas_call | solution.py:242
  4.2 0.0 copy-start.1
  4.2 10.9 %all-to-all-start = ((bf16[8,8,2048]{2,1,0:T(8,128)(2,1)}), bf16[8,8,2048]{2,1,0:T(8,128)(2,1)S(1)}, u32[]{:S(2)}, u32[]{:S(2)}) async-start(bf16[8,8,2048]{2,1,0:T(8,128)(2,1)} %get-tuple-element.23), calls=%async_computation | async-start | bytes 524288 | tf_op jit(solution)/shard_map/all_to_all | solution.py:296
  15.1 5.0 %collective-permute-start.2 = (f32[14,8,128]{2,1,0:T(8,128)S(1)}, f32[14,8,128]{2,1,0:T(8,128)S(1)}, u32[]{:S(2)}, u32[]{:S(2)}) collective-permute-start(f32[14,8,128]{2,1,0:T(8,128)S(1)} %get-tuple-element.18), channel_id=1, source_target_pairs={{8,32},{24,48},{40,64},{56,80},{72,96},{88,112},{104,128},{120,144... | collective-permute-start | bytes 172040 | tf_op jit(solution)/shard_map/ppermute | solution.py:306
  20.2 3.2 %collective-permute-start.1 = (f32[2,6,8,128]{3,2,1,0:T(8,128)S(1)}, f32[2,6,8,128]{3,2,1,0:T(8,128)S(1)}, u32[]{:S(2)}, u32[]{:S(2)}) collective-permute-start(f32[2,6,8,128]{3,2,1,0:T(8,128)S(1)} %get-tuple-element.17), channel_id=1, source_target_pairs={{0,16},{8,24},{16,32},{24,40},{32,48},{40,56},{48,64},{56,72},{64,... | collective-permute-start | bytes 147464 | tf_op jit(solution)/shard_map/ppermute | solution.py:305
  23.4 1.3 %collective-permute-start = (bf16[6,8,128]{2,1,0:T(8,128)(2,1)S(1)}, bf16[6,8,128]{2,1,0:T(8,128)(2,1)S(1)}, u32[]{:S(2)}, u32[]{:S(2)}) collective-permute-start(bf16[6,8,128]{2,1,0:T(8,128)(2,1)S(1)} %get-tuple-element.15.rim), channel_id=1, source_target_pairs={{16,0},{24,8},{32,16},{40,24},{48,32},{56,40},{64,48},{72,56},{80,... | collective-permute-start | bytes 36872 | tf_op jit(solution)/shard_map/ppermute | solution.py:304
  24.7 4.2 %collective-permute-done.far = bf16[6,8,128]{2,1,0:T(8,128)(2,1)S(1)} collective-permute-done((bf16[6,8,128]{2,1,0:T(8,128)(2,1)S(1)}, bf16[6,8,128]{2,1,0:T(8,128)(2,1)S(1)}, u32[]{:S(2)}, u32[]{:S(2)}) %collective-permute-start) | collective-permute-done | bytes 12320 | tf_op jit(solution)/shard_map/ppermute | solution.py:304
  28.8 0.0 collective-permute-done.1.chips
  28.8 0.0 collective-permute-done.2.swap
  28.9 1.9 %collective-permute-start.3 = (f32[3,6,8,128]{3,2,1,0:T(8,128)S(1)}, f32[3,6,8,128]{3,2,1,0:T(8,128)S(1)}, u32[]{:S(2)}, u32[]{:S(2)}) collective-permute-start(f32[3,6,8,128]{3,2,1,0:T(8,128)S(1)} %get-tuple-element.20), channel_id=1, source_target_pairs={{0,8},{8,0},{16,24},{24,16},{32,40},{40,32},{48,56},{56,48},{64,72... | collective-permute-start | bytes 221192 | tf_op jit(solution)/shard_map/ppermute | solution.py:311
  30.8 1.2 %collective-permute-done.3.mate = f32[3,6,8,128]{3,2,1,0:T(8,128)S(1)} collective-permute-done((f32[3,6,8,128]{3,2,1,0:T(8,128)S(1)}, f32[3,6,8,128]{3,2,1,0:T(8,128)S(1)}, u32[]{:S(2)}, u32[]{:S(2)}) %collective-permute-start.3) | collective-permute-done | bytes 73760 | tf_op jit(solution)/shard_map/ppermute | solution.py:311
  32.0 0.0 copy-done.2
  32.0 0.0 copy-done.3
  32.0 0.0 copy-done
  32.0 3.7 %forward.1.raws = f32[16,8,128]{2,1,0:T(8,128)S(1)} custom-call(s32[128]{0:T(128)S(1)} %copy-done.2, s32[128]{0:T(128)S(1)} %copy-done.3, s32[1]{0:T(128)S(6)} %copy.9.live_far.live, bf16[16,8,128]{2,1,0:T(8,128)(2,1)S(1)} %get-tuple-element.14.blocks, bf16[6,8,128]{2,1,0:T(8,128)(2,1)S(1)} %collective-permute-done.far, ...), custom_call_target="tpu_custom_call" | custom-call | flops 33554432 | bytes 4194304 | tf_op jit(solution)/shard_map/forward/pallas_call | solution.py:272
  35.8 0.0 all-to-all-done
  35.8 0.0 copy-done.1
  35.8 0.8 %finish.1 = (f32[8,2048]{1,0:T(8,128)}, f32[64,4,128]{2,1,0:T(4,128)S(1)}) custom-call(f32[16,8,128]{2,1,0:T(8,128)S(1)} %forward.1.raws, f32[16,128]{1,0:T(8,128)S(1)} %bitcast.4, bf16[64,2048]{1,0:T(8,128)(2,1)S(1)} %bitcast.2), custom_call_target="tpu_custom_call" | custom-call | bytes 131072 | tf_op jit(solution)/shard_map/finish/pallas_call | solution.py:317
  36.6 20.8 %all_to_all.10.parts = f32[64,4,128]{2,1,0:T(4,128)S(1)} all-to-all(f32[64,4,128]{2,1,0:T(4,128)S(1)} %get-tuple-element.25), channel_id=1, replica_groups=mesh['rows'=64,'vec'=8] {'rows'}, dimensions={0} | all-to-all | bytes 262144 | tf_op jit(solution)/shard_map/all_to_all | solution.py:323
  57.3 0.7 %sum.1 = f32[8,64]{1,0:T(8,128)} custom-call(f32[64,4,128]{2,1,0:T(4,128)S(1)} %all_to_all.10.parts), custom_call_target="tpu_custom_call" | custom-call | bytes 131072 | tf_op jit(solution)/shard_map/sum/pallas_call | solution.py:324
  (1 shorter events, 0.0 us)
Async XLA Ops:
  0.6 31.4 %copy-start.2 = (s32[128]{0:T(128)S(1)}, s32[128]{0:T(128)}, u32[]{:S(2)}) copy-start(s32[128]{0:T(128)} %rows.1) | copy-start | bytes 1540
  0.6 31.4 %copy-start.3 = (s32[128]{0:T(128)S(1)}, s32[128]{0:T(128)}, u32[]{:S(2)}) copy-start(s32[128]{0:T(128)} %cols.1) | copy-start | bytes 1540
  0.7 31.4 %copy-start = (bf16[16,128,128]{2,1,0:T(8,128)(2,1)S(1)}, bf16[16,128,128]{2,1,0:T(8,128)(2,1)}, u32[]{:S(2)}) copy-start(bf16[16,128,128]{2,1,0:T(8,128)(2,1)} %diag.1) | copy-start | bytes 1572868
  4.2 31.6 %copy-start.1 = (f32[2048]{0:T(1024)S(1)}, f32[2048]{0:T(1024)}, u32[]{:S(2)}) copy-start(f32[2048]{0:T(1024)} %param.8) | copy-start | bytes 24580
  4.2 31.5 %all-to-all-start = ((bf16[8,8,2048]{2,1,0:T(8,128)(2,1)}), bf16[8,8,2048]{2,1,0:T(8,128)(2,1)S(1)}, u32[]{:S(2)}, u32[]{:S(2)}) async-start(bf16[8,8,2048]{2,1,0:T(8,128)(2,1)} %get-tuple-element.23), calls=%async_computation | async-start | bytes 524288 | tf_op jit(solution)/shard_map/all_to_all | solution.py:296
  15.1 13.7 %collective-permute-start.2 = (f32[14,8,128]{2,1,0:T(8,128)S(1)}, f32[14,8,128]{2,1,0:T(8,128)S(1)}, u32[]{:S(2)}, u32[]{:S(2)}) collective-permute-start(f32[14,8,128]{2,1,0:T(8,128)S(1)} %get-tuple-element.18), channel_id=1, source_target_pairs={{8,32},{24,48},{40,64},{56,80},{72,96},{88,112},{104,128},{120,144... | collective-permute-start | bytes 172040 | tf_op jit(solution)/shard_map/ppermute | solution.py:306
  20.2 8.7 %collective-permute-start.1 = (f32[2,6,8,128]{3,2,1,0:T(8,128)S(1)}, f32[2,6,8,128]{3,2,1,0:T(8,128)S(1)}, u32[]{:S(2)}, u32[]{:S(2)}) collective-permute-start(f32[2,6,8,128]{3,2,1,0:T(8,128)S(1)} %get-tuple-element.17), channel_id=1, source_target_pairs={{0,16},{8,24},{16,32},{24,40},{32,48},{40,56},{48,64},{56,72},{64,... | collective-permute-start | bytes 147464 | tf_op jit(solution)/shard_map/ppermute | solution.py:305
  23.4 5.5 %collective-permute-start = (bf16[6,8,128]{2,1,0:T(8,128)(2,1)S(1)}, bf16[6,8,128]{2,1,0:T(8,128)(2,1)S(1)}, u32[]{:S(2)}, u32[]{:S(2)}) collective-permute-start(bf16[6,8,128]{2,1,0:T(8,128)(2,1)S(1)} %get-tuple-element.15.rim), channel_id=1, source_target_pairs={{16,0},{24,8},{32,16},{40,24},{48,32},{56,40},{64,48},{72,56},{80,... | collective-permute-start | bytes 36872 | tf_op jit(solution)/shard_map/ppermute | solution.py:304
  28.9 3.2 %collective-permute-start.3 = (f32[3,6,8,128]{3,2,1,0:T(8,128)S(1)}, f32[3,6,8,128]{3,2,1,0:T(8,128)S(1)}, u32[]{:S(2)}, u32[]{:S(2)}) collective-permute-start(f32[3,6,8,128]{3,2,1,0:T(8,128)S(1)} %get-tuple-element.20), channel_id=1, source_target_pairs={{0,8},{8,0},{16,24},{24,16},{32,40},{40,32},{48,56},{56,48},{64,72... | collective-permute-start | bytes 221192 | tf_op jit(solution)/shard_map/ppermute | solution.py:311

commit v6 on v4

--- a/solution.py
+++ b/solution.py
@@ -9,7 +9,8 @@
 
 REACH = 4
 RIM = 6
-PIECES = (16, 32, 32, 48)
+PIECES = (32, 32, 32, 32)
+LATE_PIECES = (64, 64)
 SMALL_VMEM = 8 << 20
 BLOCKS_STAY = 16 << 20
 
@@ -31,7 +32,7 @@
         kernel,
         name=name,
         in_specs=in_specs,
-        out_specs=[VM] * len(outs),
+        out_specs=[FAR if i == 0 else VM for i in range(len(outs))] if scratch else [VM] * len(outs),
         out_shape=[jax.ShapeDtypeStruct(shape, dtype) for shape, dtype in outs],
         scratch_shapes=scratch,
         compiler_params=pltpu.CompilerParams(vmem_limit_bytes=vmem),
@@ -49,9 +50,9 @@
     bottom[at] = jnp.concatenate([z, x], 0).astype(jnp.bfloat16)
 
 
-def streamed(upper_far, upper, sems):
+def streamed(upper_far, upper, sems, pieces):
     copies, first = [], 0
-    for i, count in enumerate(PIECES):
+    for i, count in enumerate(pieces):
         cut = pl.ds(first, count)
         copies.append(pltpu.make_async_copy(upper_far.at[cut], upper.at[cut], sems.at[i]))
         first += count
@@ -76,8 +77,9 @@
 
 
 def backward_kernel(
-    rows_far, cols_far, live_far, vectors_far, damage_far, upper_far, everyones, blocks, rim, own,
-    one, chips, swap, rows, cols, live, vectors, damage, upper, total, top, bottom, sems, few_sems
+    rows_far, cols_far, live_far, vectors_far, damage_far, upper_far, everyones_far, blocks, rim,
+    own, one, chips, swap, rows, cols, live, vectors, damage, flat, upper, total, top, bottom, sems,
+    few_sems, out_sems
 ):
     here = own.shape[0]
     size = upper.shape[1]
@@ -88,7 +90,7 @@
              (live_far, live))
         )
     ]
-    copies = streamed(upper_far, upper, sems)
+    copies = streamed(upper_far, upper, sems, PIECES)
     for copy in few + copies:
         copy.start()
     mine = lax.axis_index("rows")
@@ -102,10 +104,15 @@
         blocks[b] = scaled
         if b < RIM:
             rim[b] = scaled
-        for i in range(everyones.shape[0]):
-            everyones[i, :, cut] = scaled
+        flat[:, cut] = scaled
         put_halves(top, bottom, b, scaled.astype(jnp.float32))
     put_halves(top, bottom, here, jnp.zeros(total.shape[1:], jnp.float32))
+    gifts = [
+        pltpu.make_async_copy(flat, everyones_far.at[i], out_sems.at[i])
+        for i in range(everyones_far.shape[0])
+    ]
+    for gift in gifts:
+        gift.start()
 
     def product(x, s):
         pair = upper[pl.ds(s, 2)].reshape(2 * size, size)
@@ -128,6 +135,8 @@
     swap[...] = jnp.where(
         second_core == 1, total[3 * here : 3 * here + RIM], blocks[:RIM].astype(jnp.float32)
     )
+    for gift in gifts:
+        gift.wait()
 
 
 def relay_kernel(rim, far, one, chips, swap, out, back):
@@ -140,12 +149,12 @@
 
 def forward_kernel(
     rows, cols, live, blocks, far, back, swap, mate, own, diag, every, damage, upper_far,
-    product_out, copies_out, upper, total, top, bottom, sems
+    product_far, copies_out, product_near, upper, total, top, bottom, sems, out_sem
 ):
     here = own.shape[0]
     size = diag.shape[1]
     vecs = blocks.shape[1]
-    copies = streamed(upper_far, upper, sems)
+    copies = streamed(upper_far, upper, sems, LATE_PIECES)
     for copy in copies:
         copy.start()
     mine = lax.axis_index("rows")
@@ -168,7 +177,7 @@
         return lax.dot_general(x, pair, TRANSPOSED, preferred_element_type=jnp.float32)
 
     first = 0
-    for copy, count in zip(copies, PIECES):
+    for copy, count in zip(copies, LATE_PIECES):
         copy.wait()
         each_pair(
             first, count, live[0], lambda s: cols[s] - mine * here, lambda s: rows[s] - mine * here,
@@ -176,21 +185,24 @@
         )
         first += count
     soft = softness(damage[...])
+    for b in range(here):
+        product_near[:, b * size : (b + 1) * size] = total[b] * soft[b : b + 1, :]
+    leave = pltpu.make_async_copy(product_near, product_far, out_sem)
+    leave.start()
     gram = jnp.zeros((2 * vecs, every.shape[0]), jnp.float32)
     for b in range(here):
         raw = total[b]
-        cut = slice(b * size, (b + 1) * size)
-        product_out[:, cut] = raw * soft[b : b + 1, :]
         high = raw.astype(jnp.bfloat16)
         low = (raw - high.astype(jnp.float32)).astype(jnp.bfloat16)
         gram += lax.dot_general(
-            jnp.concatenate([high, low], 0), every[:, cut], TRANSPOSED,
+            jnp.concatenate([high, low], 0), every[:, b * size : (b + 1) * size], TRANSPOSED,
             preferred_element_type=jnp.float32,
         )
     gram = gram[:vecs] + gram[vecs:]
     half = vecs // 2
     packed = jnp.concatenate([gram[:half], gram[half:]], axis=1)
     copies_out[...] = jnp.broadcast_to(packed[None], copies_out.shape)
+    leave.wait()
 
 
 def sum_kernel(scale, parts, out):
@@ -219,12 +231,14 @@
             pltpu.SMEM(live.shape, live.dtype),
             pltpu.VMEM(vectors.shape, f32),
             pltpu.VMEM(damage.shape, f32),
+            pltpu.VMEM((vecs, here * size), bf16),
             pltpu.VMEM(upper.shape, bf16),
             pltpu.VMEM((REACH * here + 1, vecs, size), f32),
             pltpu.VMEM((here + 1, 2 * vecs, size), bf16),
             pltpu.VMEM((here + 1, 2 * vecs, size), bf16),
             pltpu.SemaphoreType.DMA((len(PIECES),)),
             pltpu.SemaphoreType.DMA((5,)),
+            pltpu.SemaphoreType.DMA((groups,)),
         ],
         BLOCKS_STAY, 2 * slots * vecs * size * size, 2 * slots * size * size,
     )(in_hbm(rows), in_hbm(cols), live, in_hbm(vectors), in_hbm(damage), in_hbm(upper))
@@ -240,11 +254,13 @@
         forward_kernel, "forward", [SM] * 3 + [VM] * 9 + [FAR],
         [((vecs, here * size), f32), ((owners, vecs // 2, 2 * every.shape[0]), f32)],
         [
+            pltpu.VMEM((vecs, here * size), f32),
             pltpu.VMEM(upper.shape, bf16),
             pltpu.VMEM((here + 1, vecs, size), f32),
             pltpu.VMEM((REACH * here + 1, 2 * vecs, size), bf16),
             pltpu.VMEM((REACH * here + 1, 2 * vecs, size), bf16),
-            pltpu.SemaphoreType.DMA((len(PIECES),)),
+            pltpu.SemaphoreType.DMA((len(LATE_PIECES),)),
+            pltpu.SemaphoreType.DMA(()),
         ],
         BLOCKS_STAY, 2 * slots * vecs * size * size, 2 * slots * size * size,
     )(rows, cols, live, blocks, far, back, swap, mate, own, diag, every, damage, in_hbm(upper))

time: 57 us -> 56.4 us (0.989)
  no operation moved by 1% of the time
where the time goes in v6:
time: 56.4 us; the launch traced here: 56.1 us
  starting transfers between devices  22.6 us (40%)
  blocking collectives  18.7 us (33%)
  Pallas kernels  7.84 us (14%)
  waiting for transfers between devices  5.42 us (10%)
  between operations  1.45 us (3%)
    all_to_all x1, blocking collectives, on_device(): partials = lax.all_to_all(partials, 'rows', 0, 0)  18.7 us
    all_to_all x1, starting transfers between devices, on_device(): every = lax.all_to_all(copies, 'vec', 0, 0).reshape(groups * vecs, width)  10.9 us
    ppermute x1, starting transfers between devices, on_device(): swap = lax.ppermute(swap, 'rows', across)  5.4 us
    pallas_call x1, Pallas kernels, forward(): call(forward_kernel, 'forward', [SM] * 3 + [VM] * 9 + [FAR], [((vecs, her...  4.24 us
    ppermute x1, waiting for transfers between devices, on_device(): far = lax.ppermute(edge, 'rows', down)  4.18 us
    ppermute x1, starting transfers between devices, on_device(): chips = lax.ppermute(chips, 'rows', up)  3.14 us
    pallas_call x1, Pallas kernels, backward(): call(backward_kernel, 'backward', [FAR] * 6, [((groups, vecs, here * size...  2.85 us
    ppermute x1, starting transfers between devices, on_device(): mate = lax.ppermute(mate, 'rows', mates)  1.92 us
  transfers between devices with their start and end apart: 5, of which 2 were waited for; matrix products, arithmetic and copies ran while one was open for 0% of the time, Pallas kernels for 0%

profile of v6, /device:TPU:1, one launch (start us, length us, event | category | flops | bytes accessed | tf_op | source)
XLA Modules:
  0.0 56.1 jit_solution(16740103395984686650)
XLA Ops:
  0.6 0.0 copy-start.3
  0.6 0.0 copy-start.2
  0.7 0.0 copy-start.1
  0.7 0.0 copy-start
  1.4 2.9 %backward.1 = (bf16[8,8,2048]{2,1,0:T(8,128)(2,1)}, bf16[16,8,128]{2,1,0:T(8,128)(2,1)S(1)}, bf16[6,8,128]{2,1,0:T(8,128)(2,1)S(1)}, f32[16,8,128]{2,1,0:T(8,128...) custom-call(s32[128]{0:T(128)} %rows.1, s32[128]{0:T(128)} %cols.1, ...), custom_call_target="tpu_custom_call" | custom-call | flops 33554432 | bytes 4194304 | tf_op jit(solution)/shard_map/backward/pallas_call | solution.py:222
  4.2 10.9 %all-to-all-start = ((bf16[8,8,2048]{2,1,0:T(8,128)(2,1)}), bf16[8,8,2048]{2,1,0:T(8,128)(2,1)S(1)}, u32[]{:S(2)}, u32[]{:S(2)}) async-start(bf16[8,8,2048]{2,1,0:T(8,128)(2,1)} %get-tuple-element.21), calls=%async_computation | async-start | bytes 524288 | tf_op jit(solution)/shard_map/all_to_all | solution.py:280
  15.1 3.1 %collective-permute-start.1 = (f32[2,6,8,128]{3,2,1,0:T(8,128)S(1)}, f32[2,6,8,128]{3,2,1,0:T(8,128)S(1)}, u32[]{:S(2)}, u32[]{:S(2)}) collective-permute-start(f32[2,6,8,128]{3,2,1,0:T(8,128)S(1)} %get-tuple-element.16), channel_id=1, source_target_pairs={{0,16},{8,24},{16,32},{24,40},{32,48},{40,56},{48,64},{56,72},{64,... | collective-permute-start | bytes 147464 | tf_op jit(solution)/shard_map/ppermute | solution.py:289
  18.3 5.4 %collective-permute-start.2 = (f32[6,8,128]{2,1,0:T(8,128)S(1)}, f32[6,8,128]{2,1,0:T(8,128)S(1)}, u32[]{:S(2)}, u32[]{:S(2)}) collective-permute-start(f32[6,8,128]{2,1,0:T(8,128)S(1)} %get-tuple-element.17), channel_id=1, source_target_pairs={{8,32},{24,48},{40,64},{56,80},{72,96},{88,112},{104,128},{120,144... | collective-permute-start | bytes 73736 | tf_op jit(solution)/shard_map/ppermute | solution.py:290
  23.7 1.3 %collective-permute-start = (bf16[6,8,128]{2,1,0:T(8,128)(2,1)S(1)}, bf16[6,8,128]{2,1,0:T(8,128)(2,1)S(1)}, u32[]{:S(2)}, u32[]{:S(2)}) collective-permute-start(bf16[6,8,128]{2,1,0:T(8,128)(2,1)S(1)} %get-tuple-element.14.rim), channel_id=1, source_target_pairs={{16,0},{24,8},{32,16},{40,24},{48,32},{56,40},{64,48},{72,56},{80,... | collective-permute-start | bytes 36872 | tf_op jit(solution)/shard_map/ppermute | solution.py:288
  25.0 4.2 %collective-permute-done.far = bf16[6,8,128]{2,1,0:T(8,128)(2,1)S(1)} collective-permute-done((bf16[6,8,128]{2,1,0:T(8,128)(2,1)S(1)}, bf16[6,8,128]{2,1,0:T(8,128)(2,1)S(1)}, u32[]{:S(2)}, u32[]{:S(2)}) %collective-permute-start) | collective-permute-done | bytes 12320 | tf_op jit(solution)/shard_map/ppermute | solution.py:288
  29.1 0.0 collective-permute-done.2.swap
  29.1 0.0 collective-permute-done.1.chips
  29.2 1.9 %collective-permute-start.3 = (f32[3,6,8,128]{3,2,1,0:T(8,128)S(1)}, f32[3,6,8,128]{3,2,1,0:T(8,128)S(1)}, u32[]{:S(2)}, u32[]{:S(2)}) collective-permute-start(f32[3,6,8,128]{3,2,1,0:T(8,128)S(1)} %get-tuple-element.19), channel_id=1, source_target_pairs={{0,8},{8,0},{16,24},{24,16},{32,40},{40,32},{48,56},{56,48},{64,72... | collective-permute-start | bytes 221192 | tf_op jit(solution)/shard_map/ppermute | solution.py:295
  31.1 1.2 %collective-permute-done.3.mate = f32[3,6,8,128]{3,2,1,0:T(8,128)S(1)} collective-permute-done((f32[3,6,8,128]{3,2,1,0:T(8,128)S(1)}, f32[3,6,8,128]{3,2,1,0:T(8,128)S(1)}, u32[]{:S(2)}, u32[]{:S(2)}) %collective-permute-start.3) | collective-permute-done | bytes 73760 | tf_op jit(solution)/shard_map/ppermute | solution.py:295
  32.3 0.0 all-to-all-done
  32.3 0.0 copy-done.3
  32.3 0.0 copy-done.2
  32.3 0.0 copy-done.1
  32.4 0.0 copy-done
  32.4 4.2 %forward.1 = (f32[8,2048]{1,0:T(8,128)}, f32[64,4,128]{2,1,0:T(4,128)S(1)}) custom-call(s32[128]{0:T(128)S(1)} %copy-done.2, s32[128]{0:T(128)S(1)} %copy-done.3, s32[1]{0:T(128)S(6)} %copy.9.live_far.live, bf16[16,8,128]{2,1,0:T(8,128)(2,1)S(1)} %get-tuple-element.13.blocks, bf16[6,8,128]{2,1,0:T(8,128)(2,1)S(1)} %collective-permute-done.far, ...), custom_call_target="tpu_custom_call" | custom-call | flops 33554432 | bytes 4194304 | tf_op jit(solution)/shard_map/forward/pallas_call | solution.py:253
  36.6 18.7 %all_to_all.10.parts = f32[64,4,128]{2,1,0:T(4,128)S(1)} all-to-all(f32[64,4,128]{2,1,0:T(4,128)S(1)} %get-tuple-element.23), channel_id=1, replica_groups=mesh['rows'=64,'vec'=8] {'rows'}, dimensions={0} | all-to-all | bytes 262144 | tf_op jit(solution)/shard_map/all_to_all | solution.py:301
  55.3 0.7 %sum.1 = f32[8,64]{1,0:T(8,128)} custom-call(f32[64,4,128]{2,1,0:T(4,128)S(1)} %all_to_all.10.parts), custom_call_target="tpu_custom_call" | custom-call | bytes 131072 | tf_op jit(solution)/shard_map/sum/pallas_call | solution.py:302
  (1 shorter events, 0.0 us)
Async XLA Ops:
  0.6 31.7 %copy-start.3 = (s32[128]{0:T(128)S(1)}, s32[128]{0:T(128)}, u32[]{:S(2)}) copy-start(s32[128]{0:T(128)} %cols.1) | copy-start | bytes 1540
  0.6 31.7 %copy-start.2 = (s32[128]{0:T(128)S(1)}, s32[128]{0:T(128)}, u32[]{:S(2)}) copy-start(s32[128]{0:T(128)} %rows.1) | copy-start | bytes 1540
  0.7 31.7 %copy-start.1 = (f32[2048]{0:T(1024)S(1)}, f32[2048]{0:T(1024)}, u32[]{:S(2)}) copy-start(f32[2048]{0:T(1024)} %param.8) | copy-start | bytes 24580
  0.7 31.7 %copy-start = (bf16[16,128,128]{2,1,0:T(8,128)(2,1)S(1)}, bf16[16,128,128]{2,1,0:T(8,128)(2,1)}, u32[]{:S(2)}) copy-start(bf16[16,128,128]{2,1,0:T(8,128)(2,1)} %diag.1) | copy-start | bytes 1572868
  4.2 28.1 %all-to-all-start = ((bf16[8,8,2048]{2,1,0:T(8,128)(2,1)}), bf16[8,8,2048]{2,1,0:T(8,128)(2,1)S(1)}, u32[]{:S(2)}, u32[]{:S(2)}) async-start(bf16[8,8,2048]{2,1,0:T(8,128)(2,1)} %get-tuple-element.21), calls=%async_computation | async-start | bytes 524288 | tf_op jit(solution)/shard_map/all_to_all | solution.py:280
  15.1 14.0 %collective-permute-start.1 = (f32[2,6,8,128]{3,2,1,0:T(8,128)S(1)}, f32[2,6,8,128]{3,2,1,0:T(8,128)S(1)}, u32[]{:S(2)}, u32[]{:S(2)}) collective-permute-start(f32[2,6,8,128]{3,2,1,0:T(8,128)S(1)} %get-tuple-element.16), channel_id=1, source_target_pairs={{0,16},{8,24},{16,32},{24,40},{32,48},{40,56},{48,64},{56,72},{64,... | collective-permute-start | bytes 147464 | tf_op jit(solution)/shard_map/ppermute | solution.py:289
  18.3 10.9 %collective-permute-start.2 = (f32[6,8,128]{2,1,0:T(8,128)S(1)}, f32[6,8,128]{2,1,0:T(8,128)S(1)}, u32[]{:S(2)}, u32[]{:S(2)}) collective-permute-start(f32[6,8,128]{2,1,0:T(8,128)S(1)} %get-tuple-element.17), channel_id=1, source_target_pairs={{8,32},{24,48},{40,64},{56,80},{72,96},{88,112},{104,128},{120,144... | collective-permute-start | bytes 73736 | tf_op jit(solution)/shard_map/ppermute | solution.py:290
  23.7 5.5 %collective-permute-start = (bf16[6,8,128]{2,1,0:T(8,128)(2,1)S(1)}, bf16[6,8,128]{2,1,0:T(8,128)(2,1)S(1)}, u32[]{:S(2)}, u32[]{:S(2)}) collective-permute-start(bf16[6,8,128]{2,1,0:T(8,128)(2,1)S(1)} %get-tuple-element.14.rim), channel_id=1, source_target_pairs={{16,0},{24,8},{32,16},{40,24},{48,32},{56,40},{64,48},{72,56},{80,... | collective-permute-start | bytes 36872 | tf_op jit(solution)/shard_map/ppermute | solution.py:288
  29.2 3.2 %collective-permute-start.3 = (f32[3,6,8,128]{3,2,1,0:T(8,128)S(1)}, f32[3,6,8,128]{3,2,1,0:T(8,128)S(1)}, u32[]{:S(2)}, u32[]{:S(2)}) collective-permute-start(f32[3,6,8,128]{3,2,1,0:T(8,128)S(1)} %get-tuple-element.19), channel_id=1, source_target_pairs={{0,8},{8,0},{16,24},{24,16},{32,40},{40,32},{48,56},{56,48},{64,72... | collective-permute-start | bytes 221192 | tf_op jit(solution)/shard_map/ppermute | solution.py:295

commit v7 on v6

--- a/solution.py
+++ b/solution.py
@@ -139,6 +139,13 @@
         gift.wait()
 
 
+def diagonal_kernel(blocks, diag, own, out):
+    for b in range(own.shape[0]):
+        out[b] = own[b] + lax.dot_general(
+            blocks[b], diag[b], TRANSPOSED, preferred_element_type=jnp.float32
+        )
+
+
 def relay_kernel(rim, far, one, chips, swap, out, back):
     first_core = lax.rem(lax.axis_index("rows"), 2) == 0
     out[0] = rim[...].astype(jnp.float32)
@@ -148,12 +155,11 @@
 
 
 def forward_kernel(
-    rows, cols, live, blocks, far, back, swap, mate, own, diag, every, damage, upper_far,
+    rows, cols, live, blocks, far, back, swap, mate, own, every, damage, upper_far,
     product_far, copies_out, product_near, upper, total, top, bottom, sems, out_sem
 ):
     here = own.shape[0]
-    size = diag.shape[1]
-    vecs = blocks.shape[1]
+    vecs, size = blocks.shape[1:]
     copies = streamed(upper_far, upper, sems, LATE_PIECES)
     for copy in copies:
         copy.start()
@@ -166,10 +172,7 @@
         put_halves(top, bottom, 2 * here + b, far[b].astype(jnp.float32))
         put_halves(top, bottom, 3 * here + b, jnp.where(second_core, swap[b], mate[1, b]))
     put_halves(top, bottom, REACH * here, jnp.zeros((vecs, size), jnp.float32))
-    for b in range(here):
-        total[b] = own[b] + lax.dot_general(
-            blocks[b], diag[b], TRANSPOSED, preferred_element_type=jnp.float32
-        )
+    total[:here] = own[...]
     total[:RIM] += back[...] + mate[2]
 
     def product(x, s):
@@ -245,13 +248,13 @@
 
 
 def forward(
-    owners, rows, cols, live, blocks, far, back, swap, mate, own, diag, every, damage, upper
+    owners, rows, cols, live, blocks, far, back, swap, mate, own, every, damage, upper
 ):
     f32, bf16 = jnp.float32, jnp.bfloat16
     here, vecs, size = blocks.shape
     slots = upper.shape[0]
     return call(
-        forward_kernel, "forward", [SM] * 3 + [VM] * 9 + [FAR],
+        forward_kernel, "forward", [SM] * 3 + [VM] * 8 + [FAR],
         [((vecs, here * size), f32), ((owners, vecs // 2, 2 * every.shape[0]), f32)],
         [
             pltpu.VMEM((vecs, here * size), f32),
@@ -263,7 +266,7 @@
             pltpu.SemaphoreType.DMA(()),
         ],
         BLOCKS_STAY, 2 * slots * vecs * size * size, 2 * slots * size * size,
-    )(rows, cols, live, blocks, far, back, swap, mate, own, diag, every, damage, in_hbm(upper))
+    )(rows, cols, live, blocks, far, back, swap, mate, own, every, damage, in_hbm(upper))
 
 
 def on_device(vectors, damage, diag_blocks, upper_blocks, block_rows, block_cols, live_slots):
@@ -288,6 +291,10 @@
     far = lax.ppermute(edge, "rows", down)
     chips = lax.ppermute(chips, "rows", up)
     swap = lax.ppermute(swap, "rows", across)
+    (own,) = call(
+        diagonal_kernel, "diagonal", [VM] * 3, [(own.shape, f32)], [], SMALL_VMEM,
+        2 * diag_blocks.size * vecs, 2 * diag_blocks.size,
+    )(blocks, diag_blocks, own)
     mate, back = call(
         relay_kernel, "relay", [VM] * 5, [((3,) + rim, f32), (rim, f32)], [], SMALL_VMEM,
         0, 8 * size,
@@ -295,8 +302,8 @@
     mate = lax.ppermute(mate, "rows", mates)
 
     product, partials = forward(
-        owners, block_rows, block_cols, live_slots, blocks, far, back, swap, mate, own, diag_blocks,
-        every, damage, upper_blocks,
+        owners, block_rows, block_cols, live_slots, blocks, far, back, swap, mate, own, every,
+        damage, upper_blocks,
     )
     partials = lax.all_to_all(partials, "rows", 0, 0)
     (projected,) = call(

time: 56.4 us -> 56.4 us (level)
    pallas_call x1 -> x2, Pallas kernels: 4.24 us -> 4.72 us  [the longest x1 4.35 us: forward(): call(forward_kernel, 'forward', [SM] * 3 + [VM] * 8 + [FAR], [((vecs, her...]
  transfers between devices with their start and end apart: 5 -> 5, of which waited for: 2 -> 2; matrix products, arithmetic and copies ran while one was open for 0% -> 0% of each run, Pallas kernels for 0% -> 1%
where the time goes in v7:
time: 56.4 us; the launch traced here: 56.1 us
  starting transfers between devices  22.6 us (40%)
  blocking collectives  18.7 us (33%)
  Pallas kernels  8.32 us (15%)
  waiting for transfers between devices  5.02 us (9%)
  between operations  1.45 us (3%)
    all_to_all x1, blocking collectives, on_device(): partials = lax.all_to_all(partials, 'rows', 0, 0)  18.7 us
    all_to_all x1, starting transfers between devices, on_device(): every = lax.all_to_all(copies, 'vec', 0, 0).reshape(groups * vecs, width)  10.9 us
    ppermute x1, starting transfers between devices, on_device(): swap = lax.ppermute(swap, 'rows', across)  5.37 us
    pallas_call x1, Pallas kernels, forward(): call(forward_kernel, 'forward', [SM] * 3 + [VM] * 8 + [FAR], [((vecs, her...  4.35 us
    ppermute x1, waiting for transfers between devices, on_device(): far = lax.ppermute(edge, 'rows', down)  4.16 us
    ppermute x1, starting transfers between devices, on_device(): chips = lax.ppermute(chips, 'rows', up)  3.15 us
    pallas_call x1, Pallas kernels, backward(): call(backward_kernel, 'backward', [FAR] * 6, [((groups, vecs, here * size...  2.85 us
    ppermute x1, starting transfers between devices, on_device(): mate = lax.ppermute(mate, 'rows', mates)  1.92 us
  transfers between devices with their start and end apart: 5, of which 2 were waited for; matrix products, arithmetic and copies ran while one was open for 0% of the time, Pallas kernels for 1%

profile of v7, /device:TPU:1, one launch (start us, length us, event | category | flops | bytes accessed | tf_op | source)
XLA Modules:
  0.0 56.1 jit_solution(16188355950320080285)
XLA Ops:
  0.6 0.0 copy-start.3
  0.6 0.0 copy-start.2
  0.7 0.0 copy-start.1
  0.7 0.0 copy-start
  1.4 2.9 %backward.1 = (bf16[8,8,2048]{2,1,0:T(8,128)(2,1)}, bf16[16,8,128]{2,1,0:T(8,128)(2,1)S(1)}, bf16[6,8,128]{2,1,0:T(8,128)(2,1)S(1)}, f32[16,8,128]{2,1,0:T(8,128...) custom-call(s32[128]{0:T(128)} %rows.1, s32[128]{0:T(128)} %cols.1, ...), custom_call_target="tpu_custom_call" | custom-call | flops 33554432 | bytes 4194304 | tf_op jit(solution)/shard_map/backward/pallas_call | solution.py:225
  4.2 10.9 %all-to-all-start = ((bf16[8,8,2048]{2,1,0:T(8,128)(2,1)}), bf16[8,8,2048]{2,1,0:T(8,128)(2,1)S(1)}, u32[]{:S(2)}, u32[]{:S(2)}) async-start(bf16[8,8,2048]{2,1,0:T(8,128)(2,1)} %get-tuple-element.21), calls=%async_computation | async-start | bytes 524288 | tf_op jit(solution)/shard_map/all_to_all | solution.py:283
  15.1 3.1 %collective-permute-start.1 = (f32[2,6,8,128]{3,2,1,0:T(8,128)S(1)}, f32[2,6,8,128]{3,2,1,0:T(8,128)S(1)}, u32[]{:S(2)}, u32[]{:S(2)}) collective-permute-start(f32[2,6,8,128]{3,2,1,0:T(8,128)S(1)} %get-tuple-element.16), channel_id=1, source_target_pairs={{0,16},{8,24},{16,32},{24,40},{32,48},{40,56},{48,64},{56,72},{64,... | collective-permute-start | bytes 147464 | tf_op jit(solution)/shard_map/ppermute | solution.py:292
  18.3 5.4 %collective-permute-start.2 = (f32[6,8,128]{2,1,0:T(8,128)S(1)}, f32[6,8,128]{2,1,0:T(8,128)S(1)}, u32[]{:S(2)}, u32[]{:S(2)}) collective-permute-start(f32[6,8,128]{2,1,0:T(8,128)S(1)} %get-tuple-element.17), channel_id=1, source_target_pairs={{8,32},{24,48},{40,64},{56,80},{72,96},{88,112},{104,128},{120,144... | collective-permute-start | bytes 73736 | tf_op jit(solution)/shard_map/ppermute | solution.py:293
  23.6 1.3 %collective-permute-start = (bf16[6,8,128]{2,1,0:T(8,128)(2,1)S(1)}, bf16[6,8,128]{2,1,0:T(8,128)(2,1)S(1)}, u32[]{:S(2)}, u32[]{:S(2)}) collective-permute-start(bf16[6,8,128]{2,1,0:T(8,128)(2,1)S(1)} %get-tuple-element.14.rim), channel_id=1, source_target_pairs={{16,0},{24,8},{32,16},{40,24},{48,32},{56,40},{64,48},{72,56},{80,... | collective-permute-start | bytes 36872 | tf_op jit(solution)/shard_map/ppermute | solution.py:291
  24.9 4.2 %collective-permute-done.far = bf16[6,8,128]{2,1,0:T(8,128)(2,1)S(1)} collective-permute-done((bf16[6,8,128]{2,1,0:T(8,128)(2,1)S(1)}, bf16[6,8,128]{2,1,0:T(8,128)(2,1)S(1)}, u32[]{:S(2)}, u32[]{:S(2)}) %collective-permute-start) | collective-permute-done | bytes 12320 | tf_op jit(solution)/shard_map/ppermute | solution.py:291
  29.1 0.0 collective-permute-done.2.swap
  29.1 0.0 collective-permute-done.1.chips
  29.1 1.9 %collective-permute-start.3 = (f32[3,6,8,128]{3,2,1,0:T(8,128)S(1)}, f32[3,6,8,128]{3,2,1,0:T(8,128)S(1)}, u32[]{:S(2)}, u32[]{:S(2)}) collective-permute-start(f32[3,6,8,128]{3,2,1,0:T(8,128)S(1)} %get-tuple-element.19), channel_id=1, source_target_pairs={{0,8},{8,0},{16,24},{24,16},{32,40},{40,32},{48,56},{56,48},{64,72... | collective-permute-start | bytes 221192 | tf_op jit(solution)/shard_map/ppermute | solution.py:302
  31.1 0.0 copy-done
  31.1 0.4 diagonal.1.own
  31.4 0.9 %collective-permute-done.3.mate = f32[3,6,8,128]{3,2,1,0:T(8,128)S(1)} collective-permute-done((f32[3,6,8,128]{3,2,1,0:T(8,128)S(1)}, f32[3,6,8,128]{3,2,1,0:T(8,128)S(1)}, u32[]{:S(2)}, u32[]{:S(2)}) %collective-permute-start.3) | collective-permute-done | bytes 73760 | tf_op jit(solution)/shard_map/ppermute | solution.py:302
  32.3 0.0 all-to-all-done
  32.3 0.0 copy-done.3
  32.3 0.0 copy-done.2
  32.3 0.0 copy-done.1
  32.3 4.3 %forward.1 = (f32[8,2048]{1,0:T(8,128)}, f32[64,4,128]{2,1,0:T(4,128)S(1)}) custom-call(s32[128]{0:T(128)S(1)} %copy-done.2, s32[128]{0:T(128)S(1)} %copy-done.3, s32[1]{0:T(128)S(6)} %copy.9.live_far.live, bf16[16,8,128]{2,1,0:T(8,128)(2,1)S(1)} %get-tuple-element.13.blocks, bf16[6,8,128]{2,1,0:T(8,128)(2,1)S(1)} %collective-permute-done.far, ...), custom_call_target="tpu_custom_call" | custom-call | flops 33554432 | bytes 4194304 | tf_op jit(solution)/shard_map/forward/pallas_call | solution.py:256
  36.7 18.7 %all_to_all.10.parts = f32[64,4,128]{2,1,0:T(4,128)S(1)} all-to-all(f32[64,4,128]{2,1,0:T(4,128)S(1)} %get-tuple-element.23), channel_id=1, replica_groups=mesh['rows'=64,'vec'=8] {'rows'}, dimensions={0} | all-to-all | bytes 262144 | tf_op jit(solution)/shard_map/all_to_all | solution.py:308
  55.4 0.7 %sum.1 = f32[8,64]{1,0:T(8,128)} custom-call(f32[64,4,128]{2,1,0:T(4,128)S(1)} %all_to_all.10.parts), custom_call_target="tpu_custom_call" | custom-call | bytes 131072 | tf_op jit(solution)/shard_map/sum/pallas_call | solution.py:309
  (1 shorter events, 0.0 us)
Async XLA Ops:
  0.6 31.7 %copy-start.3 = (s32[128]{0:T(128)S(1)}, s32[128]{0:T(128)}, u32[]{:S(2)}) copy-start(s32[128]{0:T(128)} %cols.1) | copy-start | bytes 1540
  0.6 31.7 %copy-start.2 = (s32[128]{0:T(128)S(1)}, s32[128]{0:T(128)}, u32[]{:S(2)}) copy-start(s32[128]{0:T(128)} %rows.1) | copy-start | bytes 1540
  0.7 31.7 %copy-start.1 = (f32[2048]{0:T(1024)S(1)}, f32[2048]{0:T(1024)}, u32[]{:S(2)}) copy-start(f32[2048]{0:T(1024)} %param.8) | copy-start | bytes 24580
  0.7 30.4 %copy-start = (bf16[16,128,128]{2,1,0:T(8,128)(2,1)S(1)}, bf16[16,128,128]{2,1,0:T(8,128)(2,1)}, u32[]{:S(2)}) copy-start(bf16[16,128,128]{2,1,0:T(8,128)(2,1)} %diag.1) | copy-start | bytes 1572868
  4.2 28.1 %all-to-all-start = ((bf16[8,8,2048]{2,1,0:T(8,128)(2,1)}), bf16[8,8,2048]{2,1,0:T(8,128)(2,1)S(1)}, u32[]{:S(2)}, u32[]{:S(2)}) async-start(bf16[8,8,2048]{2,1,0:T(8,128)(2,1)} %get-tuple-element.21), calls=%async_computation | async-start | bytes 524288 | tf_op jit(solution)/shard_map/all_to_all | solution.py:283
  15.1 14.0 %collective-permute-start.1 = (f32[2,6,8,128]{3,2,1,0:T(8,128)S(1)}, f32[2,6,8,128]{3,2,1,0:T(8,128)S(1)}, u32[]{:S(2)}, u32[]{:S(2)}) collective-permute-start(f32[2,6,8,128]{3,2,1,0:T(8,128)S(1)} %get-tuple-element.16), channel_id=1, source_target_pairs={{0,16},{8,24},{16,32},{24,40},{32,48},{40,56},{48,64},{56,72},{64,... | collective-permute-start | bytes 147464 | tf_op jit(solution)/shard_map/ppermute | solution.py:292
  18.3 10.8 %collective-permute-start.2 = (f32[6,8,128]{2,1,0:T(8,128)S(1)}, f32[6,8,128]{2,1,0:T(8,128)S(1)}, u32[]{:S(2)}, u32[]{:S(2)}) collective-permute-start(f32[6,8,128]{2,1,0:T(8,128)S(1)} %get-tuple-element.17), channel_id=1, source_target_pairs={{8,32},{24,48},{40,64},{56,80},{72,96},{88,112},{104,128},{120,144... | collective-permute-start | bytes 73736 | tf_op jit(solution)/shard_map/ppermute | solution.py:293
  23.6 5.5 %collective-permute-start = (bf16[6,8,128]{2,1,0:T(8,128)(2,1)S(1)}, bf16[6,8,128]{2,1,0:T(8,128)(2,1)S(1)}, u32[]{:S(2)}, u32[]{:S(2)}) collective-permute-start(bf16[6,8,128]{2,1,0:T(8,128)(2,1)S(1)} %get-tuple-element.14.rim), channel_id=1, source_target_pairs={{16,0},{24,8},{32,16},{40,24},{48,32},{56,40},{64,48},{72,56},{80,... | collective-permute-start | bytes 36872 | tf_op jit(solution)/shard_map/ppermute | solution.py:291
  29.1 3.2 %collective-permute-start.3 = (f32[3,6,8,128]{3,2,1,0:T(8,128)S(1)}, f32[3,6,8,128]{3,2,1,0:T(8,128)S(1)}, u32[]{:S(2)}, u32[]{:S(2)}) collective-permute-start(f32[3,6,8,128]{3,2,1,0:T(8,128)S(1)} %get-tuple-element.19), channel_id=1, source_target_pairs={{0,8},{8,0},{16,24},{24,16},{32,40},{40,32},{48,56},{56,48},{64,72... | collective-permute-start | bytes 221192 | tf_op jit(solution)/shard_map/ppermute | solution.py:302

commit v8 on v6

--- a/solution.py
+++ b/solution.py
@@ -201,12 +201,12 @@
     gram = gram[:vecs] + gram[vecs:]
     half = vecs // 2
     packed = jnp.concatenate([gram[:half], gram[half:]], axis=1)
-    copies_out[...] = jnp.broadcast_to(packed[None], copies_out.shape)
+    copies_out[...] = jnp.broadcast_to(packed.astype(copies_out.dtype)[None], copies_out.shape)
     leave.wait()
 
 
 def sum_kernel(scale, parts, out):
-    packed = jnp.sum(parts[...], axis=0) * scale
+    packed = jnp.sum(parts[...].astype(jnp.float32), axis=0) * scale
     columns = out.shape[1]
     half = packed.shape[0]
     out[:half] = packed[:, :columns]
@@ -252,7 +252,7 @@
     slots = upper.shape[0]
     return call(
         forward_kernel, "forward", [SM] * 3 + [VM] * 9 + [FAR],
-        [((vecs, here * size), f32), ((owners, vecs // 2, 2 * every.shape[0]), f32)],
+        [((vecs, here * size), f32), ((owners, vecs // 2, 2 * every.shape[0]), bf16)],
         [
             pltpu.VMEM((vecs, here * size), f32),
             pltpu.VMEM(upper.shape, bf16),
@@ -301,7 +301,7 @@
     partials = lax.all_to_all(partials, "rows", 0, 0)
     (projected,) = call(
         functools.partial(sum_kernel, 1.0 / (width * owners)), "sum", [VM],
-        [((vecs, groups * vecs), f32)], [], SMALL_VMEM, 0, partials.size * 4,
+        [((vecs, groups * vecs), f32)], [], SMALL_VMEM, 0, partials.size * 2,
     )(partials)
     return (product, projected)
 

time: 56.4 us -> 55.8 us (0.989)
  no operation moved by 1% of the time
where the time goes in v8:
time: 55.8 us; the launch traced here: 55.4 us
  starting transfers between devices  22.6 us (41%)
  blocking collectives  18.2 us (33%)
  Pallas kernels  7.79 us (14%)
  waiting for transfers between devices  5.44 us (10%)
  between operations  1.45 us (3%)
    all_to_all x1, blocking collectives, on_device(): partials = lax.all_to_all(partials, 'rows', 0, 0)  18.2 us
    all_to_all x1, starting transfers between devices, on_device(): every = lax.all_to_all(copies, 'vec', 0, 0).reshape(groups * vecs, width)  10.9 us
    ppermute x1, starting transfers between devices, on_device(): swap = lax.ppermute(swap, 'rows', across)  5.29 us
    ppermute x1, waiting for transfers between devices, on_device(): far = lax.ppermute(edge, 'rows', down)  4.2 us
    pallas_call x1, Pallas kernels, forward(): call(forward_kernel, 'forward', [SM] * 3 + [VM] * 9 + [FAR], [((vecs, her...  4.2 us
    ppermute x1, starting transfers between devices, on_device(): chips = lax.ppermute(chips, 'rows', up)  3.21 us
    pallas_call x1, Pallas kernels, backward(): call(backward_kernel, 'backward', [FAR] * 6, [((groups, vecs, here * size...  2.84 us
    ppermute x1, starting transfers between devices, on_device(): mate = lax.ppermute(mate, 'rows', mates)  1.92 us
  transfers between devices with their start and end apart: 5, of which 2 were waited for; matrix products, arithmetic and copies ran while one was open for 0% of the time, Pallas kernels for 0%

profile of v8, /device:TPU:1, one launch (start us, length us, event | category | flops | bytes accessed | tf_op | source)
XLA Modules:
  0.0 55.4 jit_solution(3041762398143735159)
XLA Ops:
  0.6 0.0 copy-start.3
  0.6 0.0 copy-start.2
  0.7 0.0 copy-start.1
  0.7 0.0 copy-start
  1.4 2.8 %backward.1 = (bf16[8,8,2048]{2,1,0:T(8,128)(2,1)}, bf16[16,8,128]{2,1,0:T(8,128)(2,1)S(1)}, bf16[6,8,128]{2,1,0:T(8,128)(2,1)S(1)}, f32[16,8,128]{2,1,0:T(8,128...) custom-call(s32[128]{0:T(128)} %rows.1, s32[128]{0:T(128)} %cols.1, ...), custom_call_target="tpu_custom_call" | custom-call | flops 33554432 | bytes 4194304 | tf_op jit(solution)/shard_map/backward/pallas_call | solution.py:222
  4.2 10.9 %all-to-all-start = ((bf16[8,8,2048]{2,1,0:T(8,128)(2,1)}), bf16[8,8,2048]{2,1,0:T(8,128)(2,1)S(1)}, u32[]{:S(2)}, u32[]{:S(2)}) async-start(bf16[8,8,2048]{2,1,0:T(8,128)(2,1)} %get-tuple-element.21), calls=%async_computation | async-start | bytes 524288 | tf_op jit(solution)/shard_map/all_to_all | solution.py:280
  15.1 3.2 %collective-permute-start.1 = (f32[2,6,8,128]{3,2,1,0:T(8,128)S(1)}, f32[2,6,8,128]{3,2,1,0:T(8,128)S(1)}, u32[]{:S(2)}, u32[]{:S(2)}) collective-permute-start(f32[2,6,8,128]{3,2,1,0:T(8,128)S(1)} %get-tuple-element.16), channel_id=1, source_target_pairs={{0,16},{8,24},{16,32},{24,40},{32,48},{40,56},{48,64},{56,72},{64,... | collective-permute-start | bytes 147464 | tf_op jit(solution)/shard_map/ppermute | solution.py:289
  18.3 5.3 %collective-permute-start.2 = (f32[6,8,128]{2,1,0:T(8,128)S(1)}, f32[6,8,128]{2,1,0:T(8,128)S(1)}, u32[]{:S(2)}, u32[]{:S(2)}) collective-permute-start(f32[6,8,128]{2,1,0:T(8,128)S(1)} %get-tuple-element.17), channel_id=1, source_target_pairs={{8,32},{24,48},{40,64},{56,80},{72,96},{88,112},{104,128},{120,144... | collective-permute-start | bytes 73736 | tf_op jit(solution)/shard_map/ppermute | solution.py:290
  23.6 1.3 %collective-permute-start = (bf16[6,8,128]{2,1,0:T(8,128)(2,1)S(1)}, bf16[6,8,128]{2,1,0:T(8,128)(2,1)S(1)}, u32[]{:S(2)}, u32[]{:S(2)}) collective-permute-start(bf16[6,8,128]{2,1,0:T(8,128)(2,1)S(1)} %get-tuple-element.14.rim), channel_id=1, source_target_pairs={{16,0},{24,8},{32,16},{40,24},{48,32},{56,40},{64,48},{72,56},{80,... | collective-permute-start | bytes 36872 | tf_op jit(solution)/shard_map/ppermute | solution.py:288
  24.9 4.2 %collective-permute-done.far = bf16[6,8,128]{2,1,0:T(8,128)(2,1)S(1)} collective-permute-done((bf16[6,8,128]{2,1,0:T(8,128)(2,1)S(1)}, bf16[6,8,128]{2,1,0:T(8,128)(2,1)S(1)}, u32[]{:S(2)}, u32[]{:S(2)}) %collective-permute-start) | collective-permute-done | bytes 12320 | tf_op jit(solution)/shard_map/ppermute | solution.py:288
  29.1 0.0 collective-permute-done.2.swap
  29.1 0.0 collective-permute-done.1.chips
  29.1 1.9 %collective-permute-start.3 = (f32[3,6,8,128]{3,2,1,0:T(8,128)S(1)}, f32[3,6,8,128]{3,2,1,0:T(8,128)S(1)}, u32[]{:S(2)}, u32[]{:S(2)}) collective-permute-start(f32[3,6,8,128]{3,2,1,0:T(8,128)S(1)} %get-tuple-element.19), channel_id=1, source_target_pairs={{0,8},{8,0},{16,24},{24,16},{32,40},{40,32},{48,56},{56,48},{64,72... | collective-permute-start | bytes 221192 | tf_op jit(solution)/shard_map/ppermute | solution.py:295
  31.1 1.2 %collective-permute-done.3.mate = f32[3,6,8,128]{3,2,1,0:T(8,128)S(1)} collective-permute-done((f32[3,6,8,128]{3,2,1,0:T(8,128)S(1)}, f32[3,6,8,128]{3,2,1,0:T(8,128)S(1)}, u32[]{:S(2)}, u32[]{:S(2)}) %collective-permute-start.3) | collective-permute-done | bytes 73760 | tf_op jit(solution)/shard_map/ppermute | solution.py:295
  32.3 0.0 all-to-all-done
  32.3 0.0 copy-done.3
  32.3 0.0 copy-done.2
  32.3 0.0 copy-done.1
  32.3 0.0 copy-done
  32.3 4.2 %forward.1 = (f32[8,2048]{1,0:T(8,128)}, bf16[64,4,128]{2,1,0:T(4,128)(2,1)S(1)}) custom-call(s32[128]{0:T(128)S(1)} %copy-done.2, s32[128]{0:T(128)S(1)} %copy-done.3, s32[1]{0:T(128)S(6)} %copy.9.live_far.live, bf16[16,8,128]{2,1,0:T(8,128)(2,1)S(1)} %get-tuple-element.13.blocks, bf16[6,8,128]{2,1,0:T(8,128)(2,1)S(1)} %collective-permute-done.far, ...), custom_call_target="tpu_custom_call" | custom-call | flops 33554432 | bytes 4194304 | tf_op jit(solution)/shard_map/forward/pallas_call | solution.py:253
  36.5 18.2 %all_to_all.10.parts = bf16[64,4,128]{2,1,0:T(4,128)(2,1)S(1)} all-to-all(bf16[64,4,128]{2,1,0:T(4,128)(2,1)S(1)} %get-tuple-element.23), channel_id=1, replica_groups=mesh['rows'=64,'vec'=8] {'rows'}, dimensions={0} | all-to-all | bytes 131072 | tf_op jit(solution)/shard_map/all_to_all | solution.py:301
  54.7 0.7 %sum.1 = f32[8,64]{1,0:T(8,128)} custom-call(bf16[64,4,128]{2,1,0:T(4,128)(2,1)S(1)} %all_to_all.10.parts), custom_call_target="tpu_custom_call" | custom-call | bytes 65536 | tf_op jit(solution)/shard_map/sum/pallas_call | solution.py:302
  (1 shorter events, 0.0 us)
Async XLA Ops:
  0.6 31.7 %copy-start.3 = (s32[128]{0:T(128)S(1)}, s32[128]{0:T(128)}, u32[]{:S(2)}) copy-start(s32[128]{0:T(128)} %cols.1) | copy-start | bytes 1540
  0.6 31.7 %copy-start.2 = (s32[128]{0:T(128)S(1)}, s32[128]{0:T(128)}, u32[]{:S(2)}) copy-start(s32[128]{0:T(128)} %rows.1) | copy-start | bytes 1540
  0.7 31.7 %copy-start.1 = (f32[2048]{0:T(1024)S(1)}, f32[2048]{0:T(1024)}, u32[]{:S(2)}) copy-start(f32[2048]{0:T(1024)} %param.8) | copy-start | bytes 24580
  0.7 31.7 %copy-start = (bf16[16,128,128]{2,1,0:T(8,128)(2,1)S(1)}, bf16[16,128,128]{2,1,0:T(8,128)(2,1)}, u32[]{:S(2)}) copy-start(bf16[16,128,128]{2,1,0:T(8,128)(2,1)} %diag.1) | copy-start | bytes 1572868
  4.2 28.1 %all-to-all-start = ((bf16[8,8,2048]{2,1,0:T(8,128)(2,1)}), bf16[8,8,2048]{2,1,0:T(8,128)(2,1)S(1)}, u32[]{:S(2)}, u32[]{:S(2)}) async-start(bf16[8,8,2048]{2,1,0:T(8,128)(2,1)} %get-tuple-element.21), calls=%async_computation | async-start | bytes 524288 | tf_op jit(solution)/shard_map/all_to_all | solution.py:280
  15.1 14.0 %collective-permute-start.1 = (f32[2,6,8,128]{3,2,1,0:T(8,128)S(1)}, f32[2,6,8,128]{3,2,1,0:T(8,128)S(1)}, u32[]{:S(2)}, u32[]{:S(2)}) collective-permute-start(f32[2,6,8,128]{3,2,1,0:T(8,128)S(1)} %get-tuple-element.16), channel_id=1, source_target_pairs={{0,16},{8,24},{16,32},{24,40},{32,48},{40,56},{48,64},{56,72},{64,... | collective-permute-start | bytes 147464 | tf_op jit(solution)/shard_map/ppermute | solution.py:289
  18.3 10.8 %collective-permute-start.2 = (f32[6,8,128]{2,1,0:T(8,128)S(1)}, f32[6,8,128]{2,1,0:T(8,128)S(1)}, u32[]{:S(2)}, u32[]{:S(2)}) collective-permute-start(f32[6,8,128]{2,1,0:T(8,128)S(1)} %get-tuple-element.17), channel_id=1, source_target_pairs={{8,32},{24,48},{40,64},{56,80},{72,96},{88,112},{104,128},{120,144... | collective-permute-start | bytes 73736 | tf_op jit(solution)/shard_map/ppermute | solution.py:290
  23.6 5.5 %collective-permute-start = (bf16[6,8,128]{2,1,0:T(8,128)(2,1)S(1)}, bf16[6,8,128]{2,1,0:T(8,128)(2,1)S(1)}, u32[]{:S(2)}, u32[]{:S(2)}) collective-permute-start(bf16[6,8,128]{2,1,0:T(8,128)(2,1)S(1)} %get-tuple-element.14.rim), channel_id=1, source_target_pairs={{16,0},{24,8},{32,16},{40,24},{48,32},{56,40},{64,48},{72,56},{80,... | collective-permute-start | bytes 36872 | tf_op jit(solution)/shard_map/ppermute | solution.py:288
  29.1 3.2 %collective-permute-start.3 = (f32[3,6,8,128]{3,2,1,0:T(8,128)S(1)}, f32[3,6,8,128]{3,2,1,0:T(8,128)S(1)}, u32[]{:S(2)}, u32[]{:S(2)}) collective-permute-start(f32[3,6,8,128]{3,2,1,0:T(8,128)S(1)} %get-tuple-element.19), channel_id=1, source_target_pairs={{0,8},{8,0},{16,24},{24,16},{32,40},{40,32},{48,56},{56,48},{64,72... | collective-permute-start | bytes 221192 | tf_op jit(solution)/shard_map/ppermute | solution.py:295

commit v9 on v6

--- a/solution.py
+++ b/solution.py
@@ -103,10 +103,11 @@
         scaled = (vectors[:, cut] * soft[b : b + 1, :]).astype(jnp.bfloat16)
         blocks[b] = scaled
         if b < RIM:
-            rim[b] = scaled
+            rim[b] = scaled.astype(jnp.float32)
         flat[:, cut] = scaled
         put_halves(top, bottom, b, scaled.astype(jnp.float32))
     put_halves(top, bottom, here, jnp.zeros(total.shape[1:], jnp.float32))
+    rim[RIM:] = jnp.zeros((rim.shape[0] - RIM,) + rim.shape[1:], jnp.float32)
     gifts = [
         pltpu.make_async_copy(flat, everyones_far.at[i], out_sems.at[i])
         for i in range(everyones_far.shape[0])
@@ -141,8 +142,8 @@
 
 def relay_kernel(rim, far, one, chips, swap, out, back):
     first_core = lax.rem(lax.axis_index("rows"), 2) == 0
-    out[0] = rim[...].astype(jnp.float32)
-    out[1] = far[...].astype(jnp.float32)
+    out[0] = rim[:RIM]
+    out[1] = far[:RIM]
     out[2] = chips[1] + jnp.where(first_core, one[...], 0.0)
     back[...] = chips[0] + jnp.where(first_core, swap[...], 0.0)
 
@@ -222,7 +223,7 @@
     return call(
         backward_kernel, "backward", [FAR] * 6,
         [
-            ((groups, vecs, here * size), bf16), ((here, vecs, size), bf16), (rim, bf16),
+            ((groups, vecs, here * size), bf16), ((here, vecs, size), bf16), ((RIM + 1, vecs, size), f32),
             ((here, vecs, size), f32), (rim, f32), ((2,) + rim, f32), (rim, f32),
         ],
         [

time: 56.4 us -> 59.1 us (1.048)
  blocking collectives: 18.7 us -> 23.1 us
  waiting for transfers between devices: 5.42 us -> 2.74 us
  starting transfers between devices: 22.6 us -> 23.7 us
    all_to_all x1, blocking collectives: 18.7 us -> 23.1 us  [on_device(): partials = lax.all_to_all(partials, 'rows', 0, 0)]
    ppermute x1, waiting for transfers between devices: 4.18 us -> 0.01 us  [on_device(): far = lax.ppermute(edge, 'rows', down)]
    ppermute x1, waiting for transfers between devices: 0.01 us -> 1.5 us  [on_device(): swap = lax.ppermute(swap, 'rows', across)]
    ppermute x1, starting transfers between devices: 5.4 us -> 6.42 us  [on_device(): swap = lax.ppermute(swap, 'rows', across)]
where the time goes in v9:
time: 59.1 us; the launch traced here: 58.8 us
  starting transfers between devices  23.7 us (40%)
  blocking collectives  23.1 us (39%)
  Pallas kernels  7.71 us (13%)
  waiting for transfers between devices  2.74 us (5%)
  between operations  1.45 us (2%)
    all_to_all x1, blocking collectives, on_device(): partials = lax.all_to_all(partials, 'rows', 0, 0)  23.1 us
    all_to_all x1, starting transfers between devices, on_device(): every = lax.all_to_all(copies, 'vec', 0, 0).reshape(groups * vecs, width)  10.9 us
    ppermute x1, starting transfers between devices, on_device(): swap = lax.ppermute(swap, 'rows', across)  6.42 us
    pallas_call x1, Pallas kernels, forward(): call(forward_kernel, 'forward', [SM] * 3 + [VM] * 9 + [FAR], [((vecs, her...  4.17 us
    ppermute x1, starting transfers between devices, on_device(): chips = lax.ppermute(chips, 'rows', up)  3.23 us
    pallas_call x1, Pallas kernels, backward(): call(backward_kernel, 'backward', [FAR] * 6, [((groups, vecs, here * size...  2.79 us
    ppermute x1, starting transfers between devices, on_device(): mate = lax.ppermute(mate, 'rows', mates)  1.92 us
    ppermute x1, waiting for transfers between devices, on_device(): swap = lax.ppermute(swap, 'rows', across)  1.5 us
  transfers between devices with their start and end apart: 5, of which 2 were waited for; matrix products, arithmetic and copies ran while one was open for 0% of the time, Pallas kernels for 0%

profile of v9, /device:TPU:1, one launch (start us, length us, event | category | flops | bytes accessed | tf_op | source)
XLA Modules:
  0.0 58.8 jit_solution(18199534306368321786)
XLA Ops:
  0.6 0.0 copy-start.3
  0.6 0.0 copy-start.2
  0.7 0.0 copy-start.1
  0.7 0.0 copy-start
  1.4 2.8 %backward.1 = (bf16[8,8,2048]{2,1,0:T(8,128)(2,1)}, bf16[16,8,128]{2,1,0:T(8,128)(2,1)S(1)}, f32[7,8,128]{2,1,0:T(8,128)S(1)}, f32[16,8,128]{2,1,0:T(8,128)S(1)}...) custom-call(s32[128]{0:T(128)} %rows.1, s32[128]{0:T(128)} %cols.1, ...), custom_call_target="tpu_custom_call" | custom-call | flops 33554432 | bytes 4194304 | tf_op jit(solution)/shard_map/backward/pallas_call | solution.py:223
  4.2 10.9 %all-to-all-start = ((bf16[8,8,2048]{2,1,0:T(8,128)(2,1)}), bf16[8,8,2048]{2,1,0:T(8,128)(2,1)S(1)}, u32[]{:S(2)}, u32[]{:S(2)}) async-start(bf16[8,8,2048]{2,1,0:T(8,128)(2,1)} %get-tuple-element.21), calls=%async_computation | async-start | bytes 524288 | tf_op jit(solution)/shard_map/all_to_all | solution.py:281
  15.1 3.2 %collective-permute-start.1 = (f32[2,6,8,128]{3,2,1,0:T(8,128)S(1)}, f32[2,6,8,128]{3,2,1,0:T(8,128)S(1)}, u32[]{:S(2)}, u32[]{:S(2)}) collective-permute-start(f32[2,6,8,128]{3,2,1,0:T(8,128)S(1)} %get-tuple-element.16), channel_id=1, source_target_pairs={{0,16},{8,24},{16,32},{24,40},{32,48},{40,56},{48,64},{56,72},{64,... | collective-permute-start | bytes 147464 | tf_op jit(solution)/shard_map/ppermute | solution.py:290
  18.3 1.3 %collective-permute-start = (f32[7,8,128]{2,1,0:T(8,128)S(1)}, f32[7,8,128]{2,1,0:T(8,128)S(1)}, u32[]{:S(2)}, u32[]{:S(2)}) collective-permute-start(f32[7,8,128]{2,1,0:T(8,128)S(1)} %get-tuple-element.14.rim), channel_id=1, source_target_pairs={{16,0},{24,8},{32,16},{40,24},{48,32},{56,40},{64,48},{72,56},{80,... | collective-permute-start | bytes 86024 | tf_op jit(solution)/shard_map/ppermute | solution.py:289
  19.6 6.4 %collective-permute-start.2 = (f32[6,8,128]{2,1,0:T(8,128)S(1)}, f32[6,8,128]{2,1,0:T(8,128)S(1)}, u32[]{:S(2)}, u32[]{:S(2)}) collective-permute-start(f32[6,8,128]{2,1,0:T(8,128)S(1)} %get-tuple-element.17), channel_id=1, source_target_pairs={{8,32},{24,48},{40,64},{56,80},{72,96},{88,112},{104,128},{120,144... | collective-permute-start | bytes 73736 | tf_op jit(solution)/shard_map/ppermute | solution.py:291
  26.0 1.5 %collective-permute-done.2.swap = f32[6,8,128]{2,1,0:T(8,128)S(1)} collective-permute-done((f32[6,8,128]{2,1,0:T(8,128)S(1)}, f32[6,8,128]{2,1,0:T(8,128)S(1)}, u32[]{:S(2)}, u32[]{:S(2)}) %collective-permute-start.2) | collective-permute-done | bytes 24608 | tf_op jit(solution)/shard_map/ppermute | solution.py:291
  27.5 0.0 collective-permute-done.far
  27.5 0.0 collective-permute-done.1.chips
  27.5 1.9 %collective-permute-start.3 = (f32[3,6,8,128]{3,2,1,0:T(8,128)S(1)}, f32[3,6,8,128]{3,2,1,0:T(8,128)S(1)}, u32[]{:S(2)}, u32[]{:S(2)}) collective-permute-start(f32[3,6,8,128]{3,2,1,0:T(8,128)S(1)} %get-tuple-element.19), channel_id=1, source_target_pairs={{0,8},{8,0},{16,24},{24,16},{32,40},{40,32},{48,56},{56,48},{64,72... | collective-permute-start | bytes 221192 | tf_op jit(solution)/shard_map/ppermute | solution.py:296
  29.5 1.2 %collective-permute-done.3.mate = f32[3,6,8,128]{3,2,1,0:T(8,128)S(1)} collective-permute-done((f32[3,6,8,128]{3,2,1,0:T(8,128)S(1)}, f32[3,6,8,128]{3,2,1,0:T(8,128)S(1)}, u32[]{:S(2)}, u32[]{:S(2)}) %collective-permute-start.3) | collective-permute-done | bytes 73760 | tf_op jit(solution)/shard_map/ppermute | solution.py:296
  30.7 0.0 all-to-all-done
  30.7 0.0 copy-done.3
  30.7 0.0 copy-done.2
  30.7 0.0 copy-done.1
  30.7 0.0 copy-done
  30.7 4.2 %forward.1 = (f32[8,2048]{1,0:T(8,128)}, f32[64,4,128]{2,1,0:T(4,128)S(1)}) custom-call(s32[128]{0:T(128)S(1)} %copy-done.2, s32[128]{0:T(128)S(1)} %copy-done.3, s32[1]{0:T(128)S(6)} %copy.9.live_far.live, bf16[16,8,128]{2,1,0:T(8,128)(2,1)S(1)} %get-tuple-element.13.blocks, f32[7,8,128]{2,1,0:T(8,128)S(1)} %collective-permute-done.far, ...), custom_call_target="tpu_custom_call" | custom-call | flops 33554432 | bytes 4194304 | tf_op jit(solution)/shard_map/forward/pallas_call | solution.py:254
  34.9 23.1 %all_to_all.10.parts = f32[64,4,128]{2,1,0:T(4,128)S(1)} all-to-all(f32[64,4,128]{2,1,0:T(4,128)S(1)} %get-tuple-element.23), channel_id=1, replica_groups=mesh['rows'=64,'vec'=8] {'rows'}, dimensions={0} | all-to-all | bytes 262144 | tf_op jit(solution)/shard_map/all_to_all | solution.py:302
  58.0 0.7 %sum.1 = f32[8,64]{1,0:T(8,128)} custom-call(f32[64,4,128]{2,1,0:T(4,128)S(1)} %all_to_all.10.parts), custom_call_target="tpu_custom_call" | custom-call | bytes 131072 | tf_op jit(solution)/shard_map/sum/pallas_call | solution.py:303
  (1 shorter events, 0.0 us)
Async XLA Ops:
  0.6 30.1 %copy-start.3 = (s32[128]{0:T(128)S(1)}, s32[128]{0:T(128)}, u32[]{:S(2)}) copy-start(s32[128]{0:T(128)} %cols.1) | copy-start | bytes 1540
  0.6 30.1 %copy-start.2 = (s32[128]{0:T(128)S(1)}, s32[128]{0:T(128)}, u32[]{:S(2)}) copy-start(s32[128]{0:T(128)} %rows.1) | copy-start | bytes 1540
  0.7 30.1 %copy-start.1 = (f32[2048]{0:T(1024)S(1)}, f32[2048]{0:T(1024)}, u32[]{:S(2)}) copy-start(f32[2048]{0:T(1024)} %param.8) | copy-start | bytes 24580
  0.7 30.1 %copy-start = (bf16[16,128,128]{2,1,0:T(8,128)(2,1)S(1)}, bf16[16,128,128]{2,1,0:T(8,128)(2,1)}, u32[]{:S(2)}) copy-start(bf16[16,128,128]{2,1,0:T(8,128)(2,1)} %diag.1) | copy-start | bytes 1572868
  4.2 26.5 %all-to-all-start = ((bf16[8,8,2048]{2,1,0:T(8,128)(2,1)}), bf16[8,8,2048]{2,1,0:T(8,128)(2,1)S(1)}, u32[]{:S(2)}, u32[]{:S(2)}) async-start(bf16[8,8,2048]{2,1,0:T(8,128)(2,1)} %get-tuple-element.21), calls=%async_computation | async-start | bytes 524288 | tf_op jit(solution)/shard_map/all_to_all | solution.py:281
  15.1 12.5 %collective-permute-start.1 = (f32[2,6,8,128]{3,2,1,0:T(8,128)S(1)}, f32[2,6,8,128]{3,2,1,0:T(8,128)S(1)}, u32[]{:S(2)}, u32[]{:S(2)}) collective-permute-start(f32[2,6,8,128]{3,2,1,0:T(8,128)S(1)} %get-tuple-element.16), channel_id=1, source_target_pairs={{0,16},{8,24},{16,32},{24,40},{32,48},{40,56},{48,64},{56,72},{64,... | collective-permute-start | bytes 147464 | tf_op jit(solution)/shard_map/ppermute | solution.py:290
  18.3 9.2 %collective-permute-start = (f32[7,8,128]{2,1,0:T(8,128)S(1)}, f32[7,8,128]{2,1,0:T(8,128)S(1)}, u32[]{:S(2)}, u32[]{:S(2)}) collective-permute-start(f32[7,8,128]{2,1,0:T(8,128)S(1)} %get-tuple-element.14.rim), channel_id=1, source_target_pairs={{16,0},{24,8},{32,16},{40,24},{48,32},{56,40},{64,48},{72,56},{80,... | collective-permute-start | bytes 86024 | tf_op jit(solution)/shard_map/ppermute | solution.py:289
  19.6 7.9 %collective-permute-start.2 = (f32[6,8,128]{2,1,0:T(8,128)S(1)}, f32[6,8,128]{2,1,0:T(8,128)S(1)}, u32[]{:S(2)}, u32[]{:S(2)}) collective-permute-start(f32[6,8,128]{2,1,0:T(8,128)S(1)} %get-tuple-element.17), channel_id=1, source_target_pairs={{8,32},{24,48},{40,64},{56,80},{72,96},{88,112},{104,128},{120,144... | collective-permute-start | bytes 73736 | tf_op jit(solution)/shard_map/ppermute | solution.py:291
  27.5 3.2 %collective-permute-start.3 = (f32[3,6,8,128]{3,2,1,0:T(8,128)S(1)}, f32[3,6,8,128]{3,2,1,0:T(8,128)S(1)}, u32[]{:S(2)}, u32[]{:S(2)}) collective-permute-start(f32[3,6,8,128]{3,2,1,0:T(8,128)S(1)} %get-tuple-element.19), channel_id=1, source_target_pairs={{0,8},{8,0},{16,24},{24,16},{32,40},{40,32},{48,56},{56,48},{64,72... | collective-permute-start | bytes 221192 | tf_op jit(solution)/shard_map/ppermute | solution.py:296
